TPU v7x, 1024 devices: a whole 4x4x32 slice. The times are simulated.
1024 devices in a mesh: role: 2 (over y_hi), dp: 64 (over z, y_lo), tp: 8 (over x, core).
Axes of the slice: x: 4, y: 4 (y_hi: 2, y_lo: 2; y = y_hi * 2 + y_lo), z: 32, core: 2. Of those that a mesh axis runs over, the one named last changes fastest.
Arguments:
- hidden: bfloat16 [2, 8192, 8192], P('role', 'dp'), may hold values from -16 to 16
- out_grad: bfloat16 [8192, 1024], P('dp', 'tp'), may hold values from -6 to 6
- master: float32 [8192, 1024], P('dp', 'tp'), may hold values from -0.0625 to 0.0625
- moment1: float32 [8192, 1024], P('dp', 'tp'), may hold values from -18 to 18
- moment2: float32 [8192, 1024], P('dp', 'tp'), may hold values from 50 to 500
- queries: bfloat16 [8, 1024, 8192], P(None, 'dp', 'tp'), may hold values from -160 to 160
- new_keys: bfloat16 [8, 1024, 1024], P(None, 'dp', 'tp'), may hold values from -6 to 6
- k_cache: bfloat16 [1024, 256, 1024], P('dp', None, 'tp'), may hold values from -6 to 6
- v_cache: bfloat16 [1024, 256, 1024], P('dp', None, 'tp'), may hold values from -6 to 6
- cache_len: int32 [1024], P('dp'), may hold values from 2 to 256, as said below
Outputs:
- row_result: bfloat16 [2, 8192, 8192], P('role', 'dp', 'tp')
Inputs may be any that keep to these rules, and one draw needn't show every extreme that they name: `cache_len`: some row holds exactly 256 cached positions.
All inputs are finite; a program needn't handle non-finite values.
Results may differ from a plain program's by a relative error of at most 0.008.
Values may be sent and summed in bfloat16 or wider, within the bound.
No kernel may reach another device: no remote copies, remote signals or barrier semaphores. Data moves between devices by JAX's collectives and lax.ppermute only.
A program may use at most 32 MiB of HBM per device.

v0:
```python
import jax
import jax.numpy as jnp
from jax import lax
from jax.sharding import PartitionSpec as P

D = 8192
KVH = 8
QH = 64
HD = 128
STEPS = 8


beta_one = 0.9
beta_two = 0.95
adam_eps = 1e-08
bias_one = 1.0 - 0.9**10
bias_two = 1.0 - 0.95**10
neg_fill = -1e30


def from_behind(value, axis, by):
    peers = lax.axis_size(axis)
    pairs = [(i, i + by) for i in range(peers) if 0 <= i + by < peers]
    return lax.ppermute(value, axis, pairs)


def adam_fresh(master, moment1, moment2, gradient):
    step_size = 2.0 * D ** (-0.5)
    first = beta_one * moment1 + (1.0 - beta_one) * gradient
    second = beta_two * moment2 + (1.0 - beta_two) * gradient * gradient
    change = first / bias_one / (jnp.sqrt(second / bias_two) + adam_eps)
    return (master - step_size * change).astype(jnp.bfloat16)


def stream_out(fresh):
    return from_behind(fresh, "role", 1)


def local(
    hidden, out_grad, master, moment1, moment2, queries, new_keys, k_cache, v_cache, cache_len
):
    group_index = lax.axis_index("role")
    is_learner = group_index == 0
    own_rows = hidden[0]
    width_here = out_grad.shape[1]
    heads_here = width_here // HD
    share = QH // KVH
    replica_rows = cache_len.shape[0]
    cache_size = k_cache.shape[1]
    picked = own_rows
    gradient = lax.psum_scatter(
        lax.dot_general(
            picked, out_grad, (((0,), (0,)), ((), ())), preferred_element_type=jnp.float32
        ),
        "dp",
        scatter_dimension=0,
        tiled=True,
    )
    fresh = adam_fresh(master, moment1, moment2, gradient)
    old_weight = master.astype(jnp.bfloat16)
    partial_value = lax.dot_general(
        out_grad,
        lax.all_gather(old_weight, "dp", axis=0, tiled=True),
        (((1,), (1,)), ((), ())),
        preferred_element_type=jnp.float32,
    )
    learner_rows = lax.psum_scatter(
        partial_value.astype(jnp.bfloat16), "tp", scatter_dimension=1, tiled=True
    )
    arrived = stream_out(fresh)
    picked = own_rows
    values = jnp.dot(
        picked,
        lax.all_gather(arrived, "dp", axis=0, tiled=True),
        preferred_element_type=jnp.float32,
    )
    values = values.astype(jnp.bfloat16).reshape(STEPS, replica_rows, heads_here, HD)
    query_all = queries.reshape(STEPS, replica_rows, heads_here, share, HD)
    newkey_all = new_keys.reshape(STEPS, replica_rows, heads_here, HD)
    cache_keys = k_cache.reshape(replica_rows, cache_size, heads_here, HD)
    cache_vals = v_cache.reshape(replica_rows, cache_size, heads_here, HD)
    scale = HD ** (-0.5)
    cache_score = (
        jnp.einsum("srkgd,rpkd->srkgp", query_all, cache_keys, preferred_element_type=jnp.float32)
        * scale
    )
    valid = jnp.arange(cache_size)[None, :] < cache_len[:, None]
    cache_score = jnp.where(valid[None, :, None, None, :], cache_score, neg_fill)
    fresh_score = (
        jnp.einsum("srkgd,trkd->srkgt", query_all, newkey_all, preferred_element_type=jnp.float32)
        * scale
    )
    causal = jnp.arange(STEPS)[:, None] >= jnp.arange(STEPS)[None, :]
    fresh_score = jnp.where(causal[:, None, None, None, :], fresh_score, neg_fill)
    top = jnp.maximum(jnp.max(cache_score, axis=-1), jnp.max(fresh_score, axis=-1))
    cache_exp = jnp.exp(cache_score - top[..., None])
    fresh_exp = jnp.exp(fresh_score - top[..., None])
    total = jnp.sum(cache_exp, axis=-1) + jnp.sum(fresh_exp, axis=-1)
    cache_wts = (cache_exp / total[..., None]).astype(jnp.bfloat16)
    fresh_wts = (fresh_exp / total[..., None]).astype(jnp.bfloat16)
    output = jnp.einsum(
        "srkgp,rpkd->srkgd", cache_wts, cache_vals, preferred_element_type=jnp.float32
    )
    output = output + jnp.einsum(
        "srkgt,trkd->srkgd", fresh_wts, values, preferred_element_type=jnp.float32
    )
    decoded = output.astype(jnp.bfloat16).reshape(STEPS * replica_rows, heads_here * share * HD)
    result = jnp.where(is_learner, learner_rows, decoded)
    return result[None]


def solution(mesh):
    return jax.shard_map(
        local,
        mesh=mesh,
        in_specs=(
            P("role", "dp", None),
            P("dp", "tp"),
            P("dp", "tp"),
            P("dp", "tp"),
            P("dp", "tp"),
            P(None, "dp", "tp"),
            P(None, "dp", "tp"),
            P("dp", None, "tp"),
            P("dp", None, "tp"),
            P("dp"),
        ),
        out_specs=P("role", "dp", "tp"),
        check_vma=False,
    )
```

profile of v0, /device:TPU:7, one launch (start us, length us, event | category | flops | bytes accessed | tf_op | source)
XLA Modules:
  0.0 871.1 jit_solution(4909036245802367786)
XLA Ops:
  6.5 0.0 copy-start
  6.5 0.0 reduce-scatter.5.cloned.1.call-start
  6.5 1.6 copy-done
  8.1 3.5 fusion.2
  11.6 0.0 reduce-scatter.5.cloned.1.call-update
  11.6 0.0 all-gather.3.cloned.1.call-start
  11.7 236.4 %reduce-scatter.5.cloned.1.call-done = f32[128,128]{1,0:T(8,128)} async-done(((f32[8192,128]{1,0:T(8,128)}), f32[128,128]{1,0:T(8,128)}) %reduce-scatter.5.cloned.1.call-update) | async-done | bytes 65552 | tf_op jit(solution)/shard_map/reduce_scatter | solution.py:51
  248.1 0.0 copy-done.5
  248.1 1.5 fusion.32
  249.6 0.0 all-gather.3.cloned.1.call-update
  249.6 0.0 all-gather.5.cloned.1.call-start
  249.7 4.0 collective-permute-start
  253.7 1.0 collective-permute-done
  254.7 0.6 copy-done.9
  255.3 0.0 all-gather.5.cloned.1.call-update
  255.3 0.0 reduce-scatter.3.cloned.1.call-start
  255.4 252.2 %all-gather.3.cloned.1.call-done = bf16[8192,128]{1,0:T(8,128)(2,1)} async-done(((bf16[128,128]{1,0:T(8,128)(2,1)}), bf16[8192,128]{1,0:T(8,128)(2,1)}) %all-gather.3.cloned.1.call-update) | async-done | bytes 2097168 | tf_op jit(solution)/shard_map/all_gather | solution.py:63
  507.5 3.6 convolution_convert_fusion
  511.2 0.0 reduce-scatter.3.cloned.1.call-update
  511.2 0.9 copy-done.3
  512.2 0.1 iota_compare_fusion
  512.3 1.3 fusion.36
  513.6 2.0 fusion.35
  515.6 0.2 fusion.19
  515.8 0.4 fusion.16
  516.2 0.0 copy-done.1
  516.2 2.5 convolution_bitcast_fusion
  518.7 246.4 %all-gather.5.cloned.1.call-done = bf16[8192,128]{1,0:T(8,128)(2,1)} async-done(((bf16[128,128]{1,0:T(8,128)(2,1)}), bf16[8192,128]{1,0:T(8,128)(2,1)}) %all-gather.5.cloned.1.call-update) | async-done | bytes 2097168 | tf_op jit(solution)/shard_map/all_gather | solution.py:74
  765.1 2.3 fusion.11
  767.5 0.3 fusion.10
  767.9 95.0 %reduce-scatter.3.cloned.1.call-done = bf16[128,1024]{1,0:T(8,128)(2,1)} async-done(((bf16[128,8192]{1,0:T(8,128)(2,1)}), bf16[128,1024]{1,0:T(8,128)(2,1)}) %reduce-scatter.3.cloned.1.call-update) | async-done | bytes 262160 | tf_op jit(solution)/shard_map/reduce_scatter | solution.py:67
  862.9 1.7 fusion.20
  (23 shorter events, 0.1 us)
Async XLA Ops:
  6.5 1.6 copy-start
  6.5 241.6 %reduce-scatter.5.cloned.1.call-start = ((), (), s32[]{:S(2)}) async-start(), calls=%async_computation.4 | async-start | bytes 4259840 | tf_op jit(solution)/shard_map/reduce_scatter | solution.py:51
  11.6 236.5 %copy-start.5 = (f32[128,128]{1,0:T(8,128)S(1)}, f32[128,128]{1,0:T(8,128)}, u32[]{:S(2)}) copy-start(f32[128,128]{1,0:T(8,128)} %param.12) | copy-start | bytes 196612
  11.6 236.5 %copy-start.6 = (f32[128,128]{1,0:T(8,128)S(1)}, f32[128,128]{1,0:T(8,128)}, u32[]{:S(2)}) copy-start(f32[128,128]{1,0:T(8,128)} %param.14) | copy-start | bytes 196612
  11.6 236.5 %copy-start.7 = (f32[128,128]{1,0:T(8,128)S(1)}, f32[128,128]{1,0:T(8,128)}, u32[]{:S(2)}) copy-start(f32[128,128]{1,0:T(8,128)} %param.13) | copy-start | bytes 196612
  11.6 495.9 %copy-start.4 = (bf16[128,128]{1,0:T(8,128)(2,1)S(1)}, bf16[128,128]{1,0:T(8,128)(2,1)}, u32[]{:S(2)}) copy-start(bf16[128,128]{1,0:T(8,128)(2,1)} %param.11) | copy-start | bytes 98308
  11.6 495.9 %all-gather.3.cloned.1.call-start = ((), (), s32[]{:S(2)}) async-start(), calls=%async_computation.2 | async-start | bytes 2129920 | tf_op jit(solution)/shard_map/all_gather | solution.py:63
  249.6 515.4 %all-gather.5.cloned.1.call-start = ((), (), s32[]{:S(2)}) async-start(), calls=%async_computation.5 | async-start | bytes 2129920 | tf_op jit(solution)/shard_map/all_gather | solution.py:74
  249.7 5.0 collective-permute-start
  254.7 0.6 copy-start.9
  255.3 607.6 %reduce-scatter.3.cloned.1.call-start = ((), (), s32[]{:S(2)}) async-start(), calls=%async_computation.3 | async-start | bytes 2359296 | tf_op jit(solution)/shard_map/reduce_scatter | solution.py:67
  511.2 0.9 copy-start.3
  511.2 1.0 copy-start.10
  511.2 1.1 copy-start.8
  513.6 2.7 copy-start.1
  518.7 248.7 %copy-start.2 = (f32[8,16,1,8,8]{3,4,0,1,2:T(8,128)S(1)}, f32[8,16,1,8,8]{3,4,0,1,2:T(8,128)}, u32[]{:S(2)}) copy-start(f32[8,16,1,8,8]{3,4,0,1,2:T(8,128)} %copy-done.1) | copy-start | bytes 98308
  765.1 2.4 copy-start.11
Sparse Core Ops, SparseCore 0:
  11.7 236.3 reduce-scatter.4
  250.8 256.7 all-gather.2
  510.2 254.8 all-gather.4
  768.4 94.4 reduce-scatter.2
where the time goes:
time: 872 us; the launch traced here: 871 us
  waiting for transfers between devices  831 us (95%)
  matrix products  15.5 us (2%)
  between operations  13.3 us (2%)
    all_gather x1, waiting for transfers between devices, local(): lax.all_gather(old_weight, 'dp', axis=0, tiled=True)  252 us
    all_gather x1, waiting for transfers between devices, local(): lax.all_gather(arrived, 'dp', axis=0, tiled=True)  246 us
    reduce_scatter x1, waiting for transfers between devices, local(): lax.psum_scatter(lax.dot_general(picked, out_grad, (((0,), (0,)), ((), ()...  236 us
    reduce_scatter x1, waiting for transfers between devices, local(): lax.psum_scatter(partial_value.astype(jnp.bfloat16), 'tp', scatter_dimens...  95 us
  transfers between devices with their start and end apart: 5, of which 5 were waited for; matrix products, arithmetic and copies ran while one was open for 1% of the time, Pallas kernels for 0%

commit v1 on v0

v1 whole, which is shorter than its diff:
```python
import jax
import jax.numpy as jnp
from jax import lax
from jax.sharding import Mesh, PartitionSpec as P

D = 8192
KVH = 8
QH = 64
HD = 128
STEPS = 8


beta_one = 0.9
beta_two = 0.95
adam_eps = 1e-08
bias_one = 1.0 - 0.9**10
bias_two = 1.0 - 0.95**10
neg_fill = -1e30

DP = ("zh", "zl", "yl")
TP = ("x", "core")
NEAR = ("zl", "yl")


def adam_fresh(master, moment1, moment2, gradient):
    step_size = 2.0 * D ** (-0.5)
    first = beta_one * moment1 + (1.0 - beta_one) * gradient
    second = beta_two * moment2 + (1.0 - beta_two) * gradient * gradient
    change = first / bias_one / (jnp.sqrt(second / bias_two) + adam_eps)
    return (master - step_size * change).astype(jnp.bfloat16)


def exchange(value, axis):
    return lax.all_to_all(value, axis, 0, 0, tiled=True)


def gather(value, axis):
    peers = lax.axis_size(axis)
    return exchange(jnp.broadcast_to(value[None], (peers, *value.shape)), axis)


def swap_core(value):
    return lax.ppermute(value, "core", [(0, 1), (1, 0)])


def dot32(a, b, dims):
    return lax.dot_general(a, b, (dims, ((), ())), preferred_element_type=jnp.float32)


def local(
    hidden, out_grad, master, moment1, moment2, queries, new_keys, k_cache, v_cache, cache_len
):
    is_learner = lax.axis_index("role") == 0
    x_at = lax.axis_index("x")
    core_at = lax.axis_index("core")
    far, near = lax.axis_size("zh"), lax.axis_size("zl") * lax.axis_size("yl")
    tokens, block = hidden.shape[1], master.shape[0]
    half = tokens // 2
    width_here = out_grad.shape[1]
    heads_here = width_here // HD
    share = QH // KVH
    replica_rows = cache_len.shape[0]
    cache_size = k_cache.shape[1]

    mine = lax.dynamic_slice(hidden[0], (core_at * half, x_at * near * block), (half, near * block))
    mine = mine.reshape(half, near, block).transpose(1, 0, 2)
    mine = exchange(mine, NEAR)
    mine = gather(mine.reshape(near * half, block), "x")
    other = swap_core(mine)

    grads = gather(out_grad, "zl")
    grads = jnp.stack(yl_pair(grads), axis=1)
    grads = grads.reshape(near, tokens, width_here)
    at_mine = lax.dynamic_slice(grads, (0, core_at * half, 0), (near, half, width_here))
    at_other = lax.dynamic_slice(grads, (0, (1 - core_at) * half, 0), (near, half, width_here))
    at_mine = at_mine.reshape(near * half, width_here)
    at_other = at_other.reshape(near * half, width_here)

    partial = jnp.stack(
        [
            dot32(mine[f], at_mine, ((0,), (0,))) + dot32(other[f], at_other, ((0,), (0,)))
            for f in range(far)
        ]
    ).astype(jnp.bfloat16)
    gradient = jnp.sum(exchange(partial, "zh").astype(jnp.float32), axis=0)
    fresh = adam_fresh(master, moment1, moment2, gradient)

    old_weight = gather(master.astype(jnp.bfloat16), "zh")
    back = jnp.stack(
        [
            jnp.stack(
                [
                    dot32(rows, old_weight[f], ((1,), (1,))).astype(jnp.bfloat16)
                    for f in range(far)
                ]
            )
            for rows in (at_mine, at_other)
        ]
    )
    kept, sent = back[0], back[1]
    back = (kept.astype(jnp.float32) + swap_core(sent).astype(jnp.float32)).astype(jnp.bfloat16)
    back = jnp.sum(exchange(back, "x").astype(jnp.float32), axis=0).astype(jnp.bfloat16)
    back = exchange(back.reshape(near, half, block), NEAR)
    back = back.reshape(2, near // 2, half, block)
    stays = lax.dynamic_index_in_dim(back, core_at, 0, keepdims=False)
    leaves = lax.dynamic_index_in_dim(back, 1 - core_at, 0, keepdims=False)
    comes = swap_core(leaves)
    low = jnp.where(core_at == 0, stays, comes)
    high = jnp.where(core_at == 0, comes, stays)
    learner_rows = jnp.concatenate([low, high], axis=1).transpose(1, 0, 2)
    learner_rows = learner_rows.reshape(tokens, near // 2 * block)

    arrived = lax.ppermute(fresh, "role", [(0, 1)])
    weight = gather(arrived, "zh")
    new_mine = sum(dot32(mine[f], weight[f], ((1,), (0,))) for f in range(far))
    new_other = sum(dot32(other[f], weight[f], ((1,), (0,))) for f in range(far))
    new_mine = new_mine.astype(jnp.bfloat16).reshape(near, half, width_here)
    new_other = new_other.astype(jnp.bfloat16).reshape(near, half, width_here)
    low = jnp.where(core_at == 0, new_mine, new_other)
    high = jnp.where(core_at == 0, new_other, new_mine)
    values = exchange(jnp.concatenate([low, high], axis=1), NEAR)
    values = jnp.sum(values.astype(jnp.float32), axis=0)

    values = values.astype(jnp.bfloat16).reshape(STEPS, replica_rows, heads_here, HD)
    query_all = queries.reshape(STEPS, replica_rows, heads_here, share, HD)
    newkey_all = new_keys.reshape(STEPS, replica_rows, heads_here, HD)
    cache_keys = k_cache.reshape(replica_rows, cache_size, heads_here, HD)
    cache_vals = v_cache.reshape(replica_rows, cache_size, heads_here, HD)
    scale = HD ** (-0.5)
    cache_score = (
        jnp.einsum("srkgd,rpkd->srkgp", query_all, cache_keys, preferred_element_type=jnp.float32)
        * scale
    )
    valid = jnp.arange(cache_size)[None, :] < cache_len[:, None]
    cache_score = jnp.where(valid[None, :, None, None, :], cache_score, neg_fill)
    fresh_score = (
        jnp.einsum("srkgd,trkd->srkgt", query_all, newkey_all, preferred_element_type=jnp.float32)
        * scale
    )
    causal = jnp.arange(STEPS)[:, None] >= jnp.arange(STEPS)[None, :]
    fresh_score = jnp.where(causal[:, None, None, None, :], fresh_score, neg_fill)
    top = jnp.maximum(jnp.max(cache_score, axis=-1), jnp.max(fresh_score, axis=-1))
    cache_exp = jnp.exp(cache_score - top[..., None])
    fresh_exp = jnp.exp(fresh_score - top[..., None])
    total = jnp.sum(cache_exp, axis=-1) + jnp.sum(fresh_exp, axis=-1)
    cache_wts = (cache_exp / total[..., None]).astype(jnp.bfloat16)
    fresh_wts = (fresh_exp / total[..., None]).astype(jnp.bfloat16)
    output = jnp.einsum(
        "srkgp,rpkd->srkgd", cache_wts, cache_vals, preferred_element_type=jnp.float32
    )
    output = output + jnp.einsum(
        "srkgt,trkd->srkgd", fresh_wts, values, preferred_element_type=jnp.float32
    )
    decoded = output.astype(jnp.bfloat16).reshape(STEPS * replica_rows, heads_here * share * HD)
    result = jnp.where(is_learner, learner_rows, decoded)
    return result[None]


def yl_pair(value):
    met = lax.ppermute(value, "yl", [(0, 1), (1, 0)])
    first = lax.axis_index("yl") == 0
    return jnp.where(first, value, met), jnp.where(first, met, value)


def solution(mesh):
    roles, dp, tp = (mesh.shape[name] for name in ("role", "dp", "tp"))
    x_size = tp // 2
    fine = Mesh(
        mesh.devices.reshape(roles, x_size, dp // (2 * x_size), 2, x_size, 2),
        ("role", *DP, *TP),
    )
    return jax.shard_map(
        local,
        mesh=fine,
        in_specs=(
            P("role", DP, None),
            P(DP, TP),
            P(DP, TP),
            P(DP, TP),
            P(DP, TP),
            P(None, DP, TP),
            P(None, DP, TP),
            P(DP, None, TP),
            P(DP, None, TP),
            P(DP),
        ),
        out_specs=P("role", DP, TP),
        check_vma=False,
    )
```

time: 872 us -> 278 us (0.32)
  the two profiles are of different devices: /device:TPU:7 before, /device:TPU:32 now
where the time goes in v1:
time: 278 us; the launch traced here: 277 us
  blocking collectives  104 us (37%)
  waiting for transfers between devices  90.6 us (33%)
  starting transfers between devices  51.4 us (18%)
  matrix products  14.2 us (5%)
  other arithmetic  8.71 us (3%)
  local copies, waits for them, and re-layouts  7.46 us (3%)
    all_to_all x3, blocking collectives, exchange(): return lax.all_to_all(value, axis, 0, 0, tiled=True)  104 us
    all_to_all x6, waiting for transfers between devices, exchange(): return lax.all_to_all(value, axis, 0, 0, tiled=True)  80.7 us
    all_to_all x6, starting transfers between devices, exchange(): return lax.all_to_all(value, axis, 0, 0, tiled=True)  38.4 us
    dot_general x24, matrix products, dot32(): lax.dot_general(a, b, (dims, ((), ())), preferred_element_type=jnp.float32)  7.63 us
    ppermute x1, waiting for transfers between devices, yl_pair(): met = lax.ppermute(value, 'yl', [(0, 1), (1, 0)])  5.88 us
    ppermute x3, starting transfers between devices, swap_core(): return lax.ppermute(value, 'core', [(0, 1), (1, 0)])  5.87 us
  transfers between devices with their start and end apart: 11, of which 11 were waited for; matrix products, arithmetic and copies ran while one was open for 7% of the time, Pallas kernels for 0%

profile of v1, /device:TPU:32, one launch (start us, length us, event | category | flops | bytes accessed | tf_op | source)
XLA Modules:
  0.0 276.8 jit_solution(7125392524747993207)
XLA Ops:
  0.0 1.6 broadcast_in_dim.30
  1.6 16.0 %all-to-all-start = ((bf16[8,128,128]{2,1,0:T(8,128)(2,1)}), bf16[8,128,128]{2,1,0:T(8,128)(2,1)S(1)}, u32[]{:S(2)}, u32[]{:S(2)}) async-start(bf16[8,128,128]{2,1,0:T(8,128)(2,1)} %broadcast_in_dim.30), calls=%async_computation | async-start | bytes 524288 | tf_op jit(solution)/shard_map/all_to_all | solution.py:34
  17.8 12.7 %all-to-all-done = bf16[8,128,128]{2,1,0:T(8,128)(2,1)S(1)} async-done(((bf16[8,128,128]{2,1,0:T(8,128)(2,1)}), bf16[8,128,128]{2,1,0:T(8,128)(2,1)S(1)}, u32[]{:S(2)}, u32[]{:S(2)}) %all-to-all-start) | async-done | bytes 262176 | tf_op jit(solution)/shard_map/all_to_all | solution.py:34
  30.6 22.5 %all_to_all.45 = bf16[16,64,128]{2,1,0:T(8,128)(2,1)S(1)} all-to-all(bf16[16,64,128]{2,1,0:T(8,128)(2,1)S(1)} %copy.50), channel_id=1, replica_groups=mesh['role'=2,'zh'=4,'zl'=8,'yl'=2,'x'=4,'core'=2] {'zl','yl'}, dimensions={0} | all-to-all | bytes 524288 | tf_op jit(solution)/shard_map/all_to_all | solution.py:34
  54.2 4.3 %all-to-all-start.5 = ((bf16[4,1024,128]{2,1,0:T(8,128)(2,1)}), bf16[4,1024,128]{2,1,0:T(8,128)(2,1)S(1)}, u32[]{:S(2)}, u32[]{:S(2)}) async-start(bf16[4,1024,128]{2,1,0:T(8,128)(2,1)} %broadcast_in_dim.41), calls=%async_computation.5 | async-start | bytes 2097152 | tf_op jit(solution)/shard_map/all_to_all | solution.py:34
  58.5 2.5 collective-permute-start
  61.0 5.9 %collective-permute-done = bf16[8,128,128]{2,1,0:T(8,128)(2,1)} collective-permute-done((bf16[8,128,128]{2,1,0:T(8,128)(2,1)S(1)}, bf16[8,128,128]{2,1,0:T(8,128)(2,1)}, u32[]{:S(2)}, u32[]{:S(2)}) %collective-permute-start) | collective-permute-done | bytes 262176 | tf_op jit(solution)/shard_map/ppermute | solution.py:160
  68.7 1.8 all-to-all-done.5
  70.5 1.9 collective-permute-start.3
  76.1 51.9 %all_to_all.46 = bf16[4,128,128]{2,1,0:T(8,128)(2,1)S(1)} all-to-all(bf16[4,128,128]{2,1,0:T(8,128)(2,1)S(1)} %pad_maximum_fusion.3), channel_id=1, replica_groups=mesh['role'=2,'zh'=4,'zl'=8,'yl'=2,'x'=4,'core'=2] {'zh'}, dimensions={0} | all-to-all | bytes 262144 | tf_op jit(solution)/shard_map/all_to_all | solution.py:34
  128.2 29.5 %all_to_all.47 = bf16[4,128,128]{2,1,0:T(8,128)(2,1)S(1)} all-to-all(bf16[4,128,128]{2,1,0:T(8,128)(2,1)S(1)} %broadcast_in_dim.31), channel_id=1, replica_groups=mesh['role'=2,'zh'=4,'zl'=8,'yl'=2,'x'=4,'core'=2] {'zh'}, dimensions={0} | all-to-all | bytes 262144 | tf_op jit(solution)/shard_map/all_to_all | solution.py:34
  158.7 1.9 collective-permute-start.1
  161.6 1.7 collective-permute-done.1
  163.3 1.2 add_convert_fusion
  164.5 4.3 %all-to-all-start.2 = ((bf16[4,1024,128]{2,1,0:T(8,128)(2,1)}), bf16[4,1024,128]{2,1,0:T(8,128)(2,1)}, u32[]{:S(2)}, u32[]{:S(2)}) async-start(bf16[4,1024,128]{2,1,0:T(8,128)(2,1)} %add_convert_fusion), calls=%async_computation.2 | async-start | bytes 2097152 | tf_op jit(solution)/shard_map/all_to_all | solution.py:34
  168.8 4.6 %collective-permute-start.4 = (bf16[128,128]{1,0:T(8,128)(2,1)S(1)}, bf16[128,128]{1,0:T(8,128)(2,1)S(1)}, u32[]{:S(2)}, u32[]{:S(2)}) collective-permute-start(bf16[128,128]{1,0:T(8,128)(2,1)S(1)} %get-tuple-element.14), channel_id=1, source_target_pairs={{0,512},{1,513},{2,514},{3,515},{4,516},{5,517},{6,518},{7,519},{8... | collective-permute-start | bytes 98312 | tf_op jit(solution)/shard_map/ppermute | solution.py:113
  173.4 1.6 collective-permute-done.4
  175.0 9.5 %all-to-all-done.2 = bf16[4,1024,128]{2,1,0:T(8,128)(2,1)} async-done(((bf16[4,1024,128]{2,1,0:T(8,128)(2,1)}), bf16[4,1024,128]{2,1,0:T(8,128)(2,1)}, u32[]{:S(2)}, u32[]{:S(2)}) %all-to-all-start.2) | async-done | bytes 1048608 | tf_op jit(solution)/shard_map/all_to_all | solution.py:34
  185.2 3.9 %all-to-all-start.7 = ((bf16[4,128,128]{2,1,0:T(8,128)(2,1)}), bf16[4,128,128]{2,1,0:T(8,128)(2,1)S(1)}, u32[]{:S(2)}, u32[]{:S(2)}) async-start(bf16[4,128,128]{2,1,0:T(8,128)(2,1)} %broadcast_in_dim.68), calls=%async_computation.7 | async-start | bytes 262144 | tf_op jit(solution)/shard_map/all_to_all | solution.py:34
  189.1 2.1 reduce_sum.51
  191.3 28.6 %all-to-all-done.7 = bf16[4,128,128]{2,1,0:T(8,128)(2,1)S(1)} async-done(((bf16[4,128,128]{2,1,0:T(8,128)(2,1)}), bf16[4,128,128]{2,1,0:T(8,128)(2,1)S(1)}, u32[]{:S(2)}, u32[]{:S(2)}) %all-to-all-start.7) | async-done | bytes 131104 | tf_op jit(solution)/shard_map/all_to_all | solution.py:34
  219.8 3.7 %all-to-all-start.3 = ((bf16[16,64,128]{2,1,0:T(8,128)(2,1)}), bf16[16,64,128]{2,1,0:T(8,128)(2,1)S(1)}, u32[]{:S(2)}, u32[]{:S(2)}) async-start(bf16[16,64,128]{2,1,0:T(8,128)(2,1)} %bitcast.18), calls=%async_computation.3 | async-start | bytes 524288 | tf_op jit(solution)/shard_map/all_to_all | solution.py:34
  223.7 1.3 fusion.38
  225.0 1.2 fusion.40
  228.1 12.0 %all-to-all-done.3 = bf16[16,64,128]{2,1,0:T(8,128)(2,1)S(1)} async-done(((bf16[16,64,128]{2,1,0:T(8,128)(2,1)}), bf16[16,64,128]{2,1,0:T(8,128)(2,1)S(1)}, u32[]{:S(2)}, u32[]{:S(2)}) %all-to-all-start.3) | async-done | bytes 262176 | tf_op jit(solution)/shard_map/all_to_all | solution.py:34
  240.2 6.2 %all-to-all-start.8 = ((bf16[16,128,128]{2,1,0:T(8,128)(2,1)}), bf16[16,128,128]{2,1,0:T(8,128)(2,1)S(1)}, u32[]{:S(2)}, u32[]{:S(2)}) async-start(bf16[16,128,128]{2,1,0:T(8,128)(2,1)} %pad_maximum_fusion.2), calls=%async_computation.8 | async-start | bytes 1048576 | tf_op jit(solution)/shard_map/all_to_all | solution.py:34
  246.5 2.0 fusion.57
  248.6 1.9 fusion.56
  251.8 2.0 collective-permute-start.2
  253.9 1.3 convolution_bitcast_fusion
  257.3 16.1 %all-to-all-done.8 = bf16[16,128,128]{2,1,0:T(8,128)(2,1)S(1)} async-done(((bf16[16,128,128]{2,1,0:T(8,128)(2,1)}), bf16[16,128,128]{2,1,0:T(8,128)(2,1)S(1)}, u32[]{:S(2)}, u32[]{:S(2)}) %all-to-all-start.8) | async-done | bytes 524320 | tf_op jit(solution)/shard_map/all_to_all | solution.py:34
  274.1 1.4 fusion.10
  (81 shorter events, 17.2 us)
Async XLA Ops:
  0.0 17.7 %copy-start = (bf16[1,128,8192]{2,1,0:T(8,128)(2,1)S(1)}, bf16[1,128,8192]{2,1,0:T(8,128)(2,1)}, u32[]{:S(2)}) copy-start(bf16[1,128,8192]{2,1,0:T(8,128)(2,1)} %param.10) | copy-start | bytes 6291460
  1.6 28.9 %all-to-all-start = ((bf16[8,128,128]{2,1,0:T(8,128)(2,1)}), bf16[8,128,128]{2,1,0:T(8,128)(2,1)S(1)}, u32[]{:S(2)}, u32[]{:S(2)}) async-start(bf16[8,128,128]{2,1,0:T(8,128)(2,1)} %broadcast_in_dim.30), calls=%async_computation | async-start | bytes 524288 | tf_op jit(solution)/shard_map/all_to_all | solution.py:34
  54.2 16.3 %all-to-all-start.5 = ((bf16[4,1024,128]{2,1,0:T(8,128)(2,1)}), bf16[4,1024,128]{2,1,0:T(8,128)(2,1)S(1)}, u32[]{:S(2)}, u32[]{:S(2)}) async-start(bf16[4,1024,128]{2,1,0:T(8,128)(2,1)} %broadcast_in_dim.41), calls=%async_computation.5 | async-start | bytes 2097152 | tf_op jit(solution)/shard_map/all_to_all | solution.py:34
  58.5 8.4 %collective-permute-start = (bf16[8,128,128]{2,1,0:T(8,128)(2,1)S(1)}, bf16[8,128,128]{2,1,0:T(8,128)(2,1)}, u32[]{:S(2)}, u32[]{:S(2)}) collective-permute-start(bf16[8,128,128]{2,1,0:T(8,128)(2,1)S(1)} %all-to-all-done), channel_id=1, source_target_pairs={{0,8},{8,0},{1,9},{9,1},{2,10},{10,2},{3,11},{11,3},{4,12},{12,4},... | collective-permute-start | bytes 786440 | tf_op jit(solution)/shard_map/ppermute | solution.py:160
  70.5 4.5 %collective-permute-start.3 = (bf16[4,1024,128]{2,1,0:T(8,128)(2,1)S(1)}, bf16[4,1024,128]{2,1,0:T(8,128)(2,1)S(1)}, u32[]{:S(2)}, u32[]{:S(2)}) collective-permute-start(bf16[4,1024,128]{2,1,0:T(8,128)(2,1)S(1)} %all-to-all-done.5), channel_id=1, source_target_pairs={{0,1},{1,0},{2,3},{3,2},{4,5},{5,4},{6,7},{7,6},{8,9},{9,8},{10,11... | collective-permute-start | bytes 3145736 | tf_op jit(solution)/shard_map/ppermute | solution.py:43
  74.0 54.0 %copy-start.8 = (f32[128,128]{1,0:T(8,128)S(1)}, f32[128,128]{1,0:T(8,128)}, u32[]{:S(2)}) copy-start(f32[128,128]{1,0:T(8,128)} %param.12) | copy-start | bytes 196612
  74.0 54.0 %copy-start.9 = (f32[128,128]{1,0:T(8,128)S(1)}, f32[128,128]{1,0:T(8,128)}, u32[]{:S(2)}) copy-start(f32[128,128]{1,0:T(8,128)} %param.14) | copy-start | bytes 196612
  74.1 54.0 %copy-start.10 = (f32[128,128]{1,0:T(8,128)S(1)}, f32[128,128]{1,0:T(8,128)}, u32[]{:S(2)}) copy-start(f32[128,128]{1,0:T(8,128)} %param.13) | copy-start | bytes 196612
  75.0 82.8 %copy-start.1 = (bf16[4,1024,128]{2,1,0:T(8,128)(2,1)}, bf16[4,1024,128]{2,1,0:T(8,128)(2,1)S(1)}, u32[]{:S(2)}) copy-start(bf16[4,1024,128]{2,1,0:T(8,128)(2,1)S(1)} %collective-permute-done.3) | copy-start | bytes 3145732
  158.7 4.6 %collective-permute-start.1 = (bf16[4,1024,128]{2,1,0:T(8,128)(2,1)S(1)}, bf16[4,1024,128]{2,1,0:T(8,128)(2,1)S(1)}, u32[]{:S(2)}, u32[]{:S(2)}) collective-permute-start(bf16[4,1024,128]{2,1,0:T(8,128)(2,1)S(1)} %pad_maximum_fusion), channel_id=1, source_target_pairs={{0,1},{1,0},{2,3},{3,2},{4,5},{5,4},{6,7},{7,6},{8,9},{9,8},{10,11... | collective-permute-start | bytes 3145736 | tf_op jit(solution)/shard_map/ppermute | solution.py:43
  164.5 20.0 %all-to-all-start.2 = ((bf16[4,1024,128]{2,1,0:T(8,128)(2,1)}), bf16[4,1024,128]{2,1,0:T(8,128)(2,1)}, u32[]{:S(2)}, u32[]{:S(2)}) async-start(bf16[4,1024,128]{2,1,0:T(8,128)(2,1)} %add_convert_fusion), calls=%async_computation.2 | async-start | bytes 2097152 | tf_op jit(solution)/shard_map/all_to_all | solution.py:34
  168.8 6.2 %collective-permute-start.4 = (bf16[128,128]{1,0:T(8,128)(2,1)S(1)}, bf16[128,128]{1,0:T(8,128)(2,1)S(1)}, u32[]{:S(2)}, u32[]{:S(2)}) collective-permute-start(bf16[128,128]{1,0:T(8,128)(2,1)S(1)} %get-tuple-element.14), channel_id=1, source_target_pairs={{0,512},{1,513},{2,514},{3,515},{4,516},{5,517},{6,518},{7,519},{8... | collective-permute-start | bytes 98312 | tf_op jit(solution)/shard_map/ppermute | solution.py:113
  185.2 34.7 %all-to-all-start.7 = ((bf16[4,128,128]{2,1,0:T(8,128)(2,1)}), bf16[4,128,128]{2,1,0:T(8,128)(2,1)S(1)}, u32[]{:S(2)}, u32[]{:S(2)}) async-start(bf16[4,128,128]{2,1,0:T(8,128)(2,1)} %broadcast_in_dim.68), calls=%async_computation.7 | async-start | bytes 262144 | tf_op jit(solution)/shard_map/all_to_all | solution.py:34
  219.8 20.3 %all-to-all-start.3 = ((bf16[16,64,128]{2,1,0:T(8,128)(2,1)}), bf16[16,64,128]{2,1,0:T(8,128)(2,1)S(1)}, u32[]{:S(2)}, u32[]{:S(2)}) async-start(bf16[16,64,128]{2,1,0:T(8,128)(2,1)} %bitcast.18), calls=%async_computation.3 | async-start | bytes 524288 | tf_op jit(solution)/shard_map/all_to_all | solution.py:34
  223.5 2.6 copy-start.2
  227.1 19.3 %copy-start.11 = (s32[16]{0:T(128)S(1)}, s32[16]{0:T(128)}, u32[]{:S(2)}) copy-start(s32[16]{0:T(128)} %param.19) | copy-start | bytes 196
  227.3 19.0 %copy-start.7 = (bf16[8,16,1024]{2,1,0:T(8,128)(2,1)S(1)}, bf16[8,16,1024]{2,1,0:T(8,128)(2,1)}, u32[]{:S(2)}) copy-start(bf16[8,16,1024]{2,1,0:T(8,128)(2,1)} %param.15) | copy-start | bytes 786436
  240.2 6.2 %copy-start.3 = (bf16[16,64,128]{2,1,0:T(8,128)(2,1)}, bf16[16,64,128]{2,1,0:T(8,128)(2,1)S(1)}, u32[]{:S(2)}) copy-start(bf16[16,64,128]{2,1,0:T(8,128)(2,1)S(1)} %all-to-all-done.3) | copy-start | bytes 786436
  240.2 33.3 %all-to-all-start.8 = ((bf16[16,128,128]{2,1,0:T(8,128)(2,1)}), bf16[16,128,128]{2,1,0:T(8,128)(2,1)S(1)}, u32[]{:S(2)}, u32[]{:S(2)}) async-start(bf16[16,128,128]{2,1,0:T(8,128)(2,1)} %pad_maximum_fusion.2), calls=%async_computation.8 | async-start | bytes 1048576 | tf_op jit(solution)/shard_map/all_to_all | solution.py:34
  248.5 2.6 copy-start.4
  248.5 5.3 %copy-start.12 = (bf16[16,256,128]{2,1,0:T(8,128)(2,1)S(1)}, bf16[16,256,128]{2,1,0:T(8,128)(2,1)}, u32[]{:S(2)}) copy-start(bf16[16,256,128]{2,1,0:T(8,128)(2,1)} %param.18) | copy-start | bytes 3145732
  251.8 3.7 %copy-start.5 = (bf16[16,64,128]{2,1,0:T(8,128)(2,1)S(1)}, bf16[16,64,128]{2,1,0:T(8,128)(2,1)}, u32[]{:S(2)}) copy-start(bf16[16,64,128]{2,1,0:T(8,128)(2,1)} %copy-done.3) | copy-start | bytes 786436
  251.8 3.7 %collective-permute-start.2 = (bf16[8,64,128]{2,1,0:T(8,128)(2,1)}, bf16[8,64,128]{2,1,0:T(8,128)(2,1)}, u32[]{:S(2)}, u32[]{:S(2)}) collective-permute-start(bf16[8,64,128]{2,1,0:T(8,128)(2,1)} %dynamic-slice_bitcast_fusion.1), channel_id=1, source_target_pairs={{0,1},{1,0},{2,3},{3,2},{4,5},{5,4},{6,7},{7,6},{8,9},{9,8},{10,11... | collective-permute-start | bytes 393224 | tf_op jit(solution)/shard_map/ppermute | solution.py:43
  257.3 18.5 %copy-start.6 = (bf16[128,8,128]{0,2,1:T(8,128)(2,1)S(1)}, bf16[128,8,128]{0,2,1:T(8,128)(2,1)}, u32[]{:S(2)}) copy-start(bf16[128,8,128]{0,2,1:T(8,128)(2,1)} %copy.46) | copy-start | bytes 786436

commit v2 on v1

--- a/solution.py
+++ b/solution.py
@@ -39,8 +39,42 @@
     return exchange(jnp.broadcast_to(value[None], (peers, *value.shape)), axis)
 
 
-def swap_core(value):
-    return lax.ppermute(value, "core", [(0, 1), (1, 0)])
+def swap(value, axis, by=1):
+    peers = lax.axis_size(axis)
+    return lax.ppermute(value, axis, [(i, i ^ by) for i in range(peers)])
+
+
+def ordered(value, met, first):
+    return jnp.where(first, value, met), jnp.where(first, met, value)
+
+
+def doubled(value, axis):
+    by, at = lax.axis_size(axis) // 2, 0
+    while by:
+        first = lax.axis_index(axis) & by == 0
+        value = jnp.stack(ordered(value, swap(value, axis, by), first), axis=at)
+        by, at = by // 2, at + 1
+    return value, at
+
+
+def far_shift(value, by, to_role):
+    far = lax.axis_size("zh")
+    pairs = [(i, to_role * far + (i + by) % far) for i in range(far)]
+    return lax.ppermute(value, ("role", "zh"), pairs)
+
+
+def far_order(far):
+    return sorted(range(far), key=lambda k: -min(k, far - k))
+
+
+def by_source(received):
+    far = len(received)
+    back = [received[-m % far] for m in range(far)]
+    return lax.dynamic_slice_in_dim(jnp.stack(back + back), -lax.axis_index("zh") % far, far, 0)
+
+
+def at_index(value, index):
+    return lax.dynamic_index_in_dim(value, index, 0, keepdims=False)
 
 
 def dot32(a, b, dims):
@@ -51,9 +85,10 @@
     hidden, out_grad, master, moment1, moment2, queries, new_keys, k_cache, v_cache, cache_len
 ):
     is_learner = lax.axis_index("role") == 0
-    x_at = lax.axis_index("x")
-    core_at = lax.axis_index("core")
-    far, near = lax.axis_size("zh"), lax.axis_size("zl") * lax.axis_size("yl")
+    x_at, core_at = lax.axis_index("x"), lax.axis_index("core")
+    zh_at, yl_at = lax.axis_index("zh"), lax.axis_index("yl")
+    far, line = lax.axis_size("zh"), lax.axis_size("zl")
+    near = line * 2
     tokens, block = hidden.shape[1], master.shape[0]
     half = tokens // 2
     width_here = out_grad.shape[1]
@@ -66,60 +101,57 @@
     mine = mine.reshape(half, near, block).transpose(1, 0, 2)
     mine = exchange(mine, NEAR)
     mine = gather(mine.reshape(near * half, block), "x")
-    other = swap_core(mine)
-
-    grads = gather(out_grad, "zl")
-    grads = jnp.stack(yl_pair(grads), axis=1)
+    other = swap(mine, "core")
+
+    grads, at = doubled(out_grad, "zl")
+    grads = jnp.stack(ordered(grads, swap(grads, "yl"), yl_at == 0), axis=at)
     grads = grads.reshape(near, tokens, width_here)
-    at_mine = lax.dynamic_slice(grads, (0, core_at * half, 0), (near, half, width_here))
-    at_other = lax.dynamic_slice(grads, (0, (1 - core_at) * half, 0), (near, half, width_here))
-    at_mine = at_mine.reshape(near * half, width_here)
-    at_other = at_other.reshape(near * half, width_here)
+    rows_at = [lax.dynamic_slice(grads, (0, at * half, 0), (near, half, width_here)) for at in (core_at, 1 - core_at)]
+    at_mine, at_other = (rows.reshape(near * half, width_here) for rows in rows_at)
+
+    old_weight = master.astype(jnp.bfloat16)
+    old_parts = {k: far_shift(old_weight, k, 0) for k in far_order(far)[:-1]}
+    old_parts[0] = old_weight
+    old_weight = by_source([old_parts[k] for k in range(far)])
+    kept, sent = (
+        jnp.stack([dot32(rows, old_weight[f], ((1,), (1,))).astype(jnp.bfloat16) for f in range(far)])
+        for rows in (at_mine, at_other)
+    )
+    sent_back = (kept.astype(jnp.float32) + swap(sent, "core").astype(jnp.float32)).astype(jnp.bfloat16)
 
     partial = jnp.stack(
         [
             dot32(mine[f], at_mine, ((0,), (0,))) + dot32(other[f], at_other, ((0,), (0,)))
             for f in range(far)
         ]
-    ).astype(jnp.bfloat16)
-    gradient = jnp.sum(exchange(partial, "zh").astype(jnp.float32), axis=0)
+    )
+    gradient = at_index(partial, zh_at)
+    narrow, sent_back = lax.optimization_barrier((partial.astype(jnp.bfloat16), sent_back))
+    for k in far_order(far)[:-1]:
+        gradient += far_shift(at_index(narrow, (zh_at + k) % far), k, 0).astype(jnp.float32)
     fresh = adam_fresh(master, moment1, moment2, gradient)
 
-    old_weight = gather(master.astype(jnp.bfloat16), "zh")
-    back = jnp.stack(
-        [
-            jnp.stack(
-                [
-                    dot32(rows, old_weight[f], ((1,), (1,))).astype(jnp.bfloat16)
-                    for f in range(far)
-                ]
-            )
-            for rows in (at_mine, at_other)
-        ]
-    )
-    kept, sent = back[0], back[1]
-    back = (kept.astype(jnp.float32) + swap_core(sent).astype(jnp.float32)).astype(jnp.bfloat16)
-    back = jnp.sum(exchange(back, "x").astype(jnp.float32), axis=0).astype(jnp.bfloat16)
-    back = exchange(back.reshape(near, half, block), NEAR)
-    back = back.reshape(2, near // 2, half, block)
-    stays = lax.dynamic_index_in_dim(back, core_at, 0, keepdims=False)
-    leaves = lax.dynamic_index_in_dim(back, 1 - core_at, 0, keepdims=False)
-    comes = swap_core(leaves)
-    low = jnp.where(core_at == 0, stays, comes)
-    high = jnp.where(core_at == 0, comes, stays)
-    learner_rows = jnp.concatenate([low, high], axis=1).transpose(1, 0, 2)
-    learner_rows = learner_rows.reshape(tokens, near // 2 * block)
-
-    arrived = lax.ppermute(fresh, "role", [(0, 1)])
-    weight = gather(arrived, "zh")
-    new_mine = sum(dot32(mine[f], weight[f], ((1,), (0,))) for f in range(far))
-    new_other = sum(dot32(other[f], weight[f], ((1,), (0,))) for f in range(far))
-    new_mine = new_mine.astype(jnp.bfloat16).reshape(near, half, width_here)
-    new_other = new_other.astype(jnp.bfloat16).reshape(near, half, width_here)
-    low = jnp.where(core_at == 0, new_mine, new_other)
-    high = jnp.where(core_at == 0, new_other, new_mine)
-    values = exchange(jnp.concatenate([low, high], axis=1), NEAR)
-    values = jnp.sum(values.astype(jnp.float32), axis=0)
+    back = jnp.sum(exchange(sent_back, "x").astype(jnp.float32), axis=0).astype(jnp.bfloat16)
+    back = back.reshape(line, 2, half, block)
+    stays = lax.dynamic_index_in_dim(back, yl_at, 1, keepdims=False)
+    leaves = lax.dynamic_index_in_dim(back, 1 - yl_at, 1, keepdims=False)
+    back = jnp.stack(ordered(stays, swap(leaves, "yl"), yl_at == 0), axis=1)
+
+    parts = {k: far_shift(fresh, k, 1) for k in far_order(far)}
+    weight = by_source([parts[k] for k in range(far)])
+    terms = [sum(dot32(rows[f], weight[f], ((1,), (0,))) for f in range(far)) for rows in (mine, other)]
+    terms = jnp.stack([rows.reshape(line, 2, half, width_here) for rows in terms], axis=2)
+    stays = lax.dynamic_index_in_dim(terms, yl_at, 1, keepdims=False)
+    leaves = lax.dynamic_index_in_dim(terms, 1 - yl_at, 1, keepdims=False)
+    terms = stays + swap(leaves.astype(jnp.bfloat16), "yl").astype(jnp.float32)
+
+    moved = exchange(jnp.where(is_learner, back, terms.astype(jnp.bfloat16)), "zl")
+    values = jnp.sum(moved.astype(jnp.float32), axis=0)
+    values = jnp.concatenate(ordered(values[0], values[1], core_at == 0))
+    back = moved.reshape(2, near // 2, half, block)
+    stays, leaves = at_index(back, core_at), at_index(back, 1 - core_at)
+    learner_rows = jnp.concatenate(ordered(stays, swap(leaves, "core"), core_at == 0), axis=1)
+    learner_rows = learner_rows.transpose(1, 0, 2).reshape(tokens, near // 2 * block)
 
     values = values.astype(jnp.bfloat16).reshape(STEPS, replica_rows, heads_here, HD)
     query_all = queries.reshape(STEPS, replica_rows, heads_here, share, HD)
@@ -156,12 +188,6 @@
     return result[None]
 
 
-def yl_pair(value):
-    met = lax.ppermute(value, "yl", [(0, 1), (1, 0)])
-    first = lax.axis_index("yl") == 0
-    return jnp.where(first, value, met), jnp.where(first, met, value)
-
-
 def solution(mesh):
     roles, dp, tp = (mesh.shape[name] for name in ("role", "dp", "tp"))
     x_size = tp // 2

time: 278 us -> 236 us (0.85)
  the two profiles are of different devices: /device:TPU:32 before, /device:TPU:19 now
where the time goes in v2:
time: 236 us; the launch traced here: 234 us
  waiting for transfers between devices  112 us (47%)
  starting transfers between devices  85 us (36%)
  matrix products  22.3 us (9%)
  other arithmetic  10.7 us (5%)
  local copies, waits for them, and re-layouts  3.65 us (2%)
    ppermute x10, waiting for transfers between devices, far_shift(): return lax.ppermute(value, ('role', 'zh'), pairs)  76.1 us
    ppermute x9, starting transfers between devices, swap(): return lax.ppermute(value, axis, [(i, i ^ by) for i in range(peers)])  44.6 us
    all_to_all x4, starting transfers between devices, exchange(): return lax.all_to_all(value, axis, 0, 0, tiled=True)  31.1 us
    ppermute x9, waiting for transfers between devices, swap(): return lax.ppermute(value, axis, [(i, i ^ by) for i in range(peers)])  18 us
    all_to_all x4, waiting for transfers between devices, exchange(): return lax.all_to_all(value, axis, 0, 0, tiled=True)  17.5 us
    dot_general x24, matrix products, dot32(): lax.dot_general(a, b, (dims, ((), ())), preferred_element_type=jnp.float32)  16.5 us
    ppermute x10, starting transfers between devices, far_shift(): return lax.ppermute(value, ('role', 'zh'), pairs)  9.27 us
  transfers between devices with their start and end apart: 23, of which 9 were waited for; matrix products, arithmetic and copies ran while one was open for 13% of the time, Pallas kernels for 0%

profile of v2, /device:TPU:19, one launch (start us, length us, event | category | flops | bytes accessed | tf_op | source)
XLA Modules:
  0.0 234.3 jit_solution(16093145623548251257)
XLA Ops:
  3.0 8.8 %collective-permute-start = (bf16[128,128]{1,0:T(8,128)(2,1)}, bf16[128,128]{1,0:T(8,128)(2,1)S(1)}, u32[]{:S(2)}, u32[]{:S(2)}) collective-permute-start(bf16[128,128]{1,0:T(8,128)(2,1)} %param.11), channel_id=1, source_target_pairs={{0,64},{16,80},{32,96},{48,112},{64,0},{80,16},{96,32},{112,48},{1... | collective-permute-start | bytes 98312 | tf_op jit(solution)/shard_map/ppermute | solution.py:44
  12.7 6.4 %all-to-all-start = ((bf16[16,64,128]{2,1,0:T(8,128)(2,1)}), bf16[16,64,128]{2,1,0:T(8,128)(2,1)S(1)}, u32[]{:S(2)}, u32[]{:S(2)}) async-start(bf16[16,64,128]{2,1,0:T(8,128)(2,1)} %copy.60), calls=%async_computation | async-start | bytes 524288 | tf_op jit(solution)/shard_map/all_to_all | solution.py:34
  19.3 4.1 %collective-permute-start.1 = (bf16[2,128,128]{2,1,0:T(8,128)(2,1)S(1)}, bf16[2,128,128]{2,1,0:T(8,128)(2,1)S(1)}, u32[]{:S(2)}, u32[]{:S(2)}) collective-permute-start(bf16[2,128,128]{2,1,0:T(8,128)(2,1)S(1)} %pad_maximum_fusion.5), channel_id=1, source_target_pairs={{0,32},{16,48},{32,0},{48,16},{64,96},{80,112},{96,64},{112,80},{1... | collective-permute-start | bytes 196616 | tf_op jit(solution)/shard_map/ppermute | solution.py:44
  23.5 4.8 %collective-permute-done.1 = bf16[2,128,128]{2,1,0:T(8,128)(2,1)S(1)} collective-permute-done((bf16[2,128,128]{2,1,0:T(8,128)(2,1)S(1)}, bf16[2,128,128]{2,1,0:T(8,128)(2,1)S(1)}, u32[]{:S(2)}, u32[]{:S(2)}) %collective-permute-start.1) | collective-permute-done | bytes 65568 | tf_op jit(solution)/shard_map/ppermute | solution.py:44
  28.4 6.5 %collective-permute-start.2 = (bf16[2,2,128,128]{3,2,1,0:T(8,128)(2,1)S(1)}, bf16[2,2,128,128]{3,2,1,0:T(8,128)(2,1)S(1)}, u32[]{:S(2)}, u32[]{:S(2)}) collective-permute-start(bf16[2,2,128,128]{3,2,1,0:T(8,128)(2,1)S(1)} %pad_maximum_fusion.4), channel_id=1, source_target_pairs={{0,16},{16,0},{32,48},{48,32},{64,80},{80,64},{96,112},{112,96},{1... | collective-permute-start | bytes 393224 | tf_op jit(solution)/shard_map/ppermute | solution.py:44
  34.9 2.8 %collective-permute-done.2 = bf16[2,2,128,128]{3,2,1,0:T(8,128)(2,1)S(1)} collective-permute-done((bf16[2,2,128,128]{3,2,1,0:T(8,128)(2,1)S(1)}, bf16[2,2,128,128]{3,2,1,0:T(8,128)(2,1)S(1)}, u32[]{:S(2)}, u32[]{:S(2)}) %collective-permute-start.2) | collective-permute-done | bytes 131104 | tf_op jit(solution)/shard_map/ppermute | solution.py:44
  37.7 2.8 %collective-permute-start.3 = (bf16[2,2,2,128,128]{4,3,2,1,0:T(8,128)(2,1)S(1)}, bf16[2,2,2,128,128]{4,3,2,1,0:T(8,128)(2,1)S(1)}, u32[]{:S(2)}, u32[]{:S(2)}) collective-permute-start(bf16[2,2,2,128,128]{4,3,2,1,0:T(8,128)(2,1)S(1)} %pad_maximum_fusion.2), channel_id=1, source_target_pairs={{0,8},{8,0},{1,9},{9,1},{2,10},{10,2},{3,11},{11,3},{4,12},{12,4},... | collective-permute-start | bytes 786440 | tf_op jit(solution)/shard_map/ppermute | solution.py:44
  40.6 4.3 %collective-permute-done.3 = bf16[2,2,2,128,128]{4,3,2,1,0:T(8,128)(2,1)S(1)} collective-permute-done((bf16[2,2,2,128,128]{4,3,2,1,0:T(8,128)(2,1)S(1)}, bf16[2,2,2,128,128]{4,3,2,1,0:T(8,128)(2,1)S(1)}, u32[]{:S(2)}, u32[]{:S(2)}) %collective-permute-start.3) | collective-permute-done | bytes 262176 | tf_op jit(solution)/shard_map/ppermute | solution.py:44
  47.1 6.2 %collective-permute-start.8 = (bf16[4,1024,128]{2,1,0:T(8,128)(2,1)}, bf16[4,1024,128]{2,1,0:T(8,128)(2,1)}, u32[]{:S(2)}, u32[]{:S(2)}) collective-permute-start(bf16[4,1024,128]{2,1,0:T(8,128)(2,1)} %pad_maximum_fusion), channel_id=1, source_target_pairs={{0,1},{1,0},{2,3},{3,2},{4,5},{5,4},{6,7},{7,6},{8,9},{9,8},{10,11... | collective-permute-start | bytes 3145736 | tf_op jit(solution)/shard_map/ppermute | solution.py:44
  54.5 4.4 %all-to-all-start.1 = ((bf16[4,1024,128]{2,1,0:T(8,128)(2,1)}), bf16[4,1024,128]{2,1,0:T(8,128)(2,1)}, u32[]{:S(2)}, u32[]{:S(2)}) async-start(bf16[4,1024,128]{2,1,0:T(8,128)(2,1)} %broadcast_in_dim.29), calls=%async_computation.1 | async-start | bytes 2097152 | tf_op jit(solution)/shard_map/all_to_all | solution.py:34
  60.4 1.7 fusion.9
  62.1 10.8 %all-to-all-done.1 = bf16[4,1024,128]{2,1,0:T(8,128)(2,1)} async-done(((bf16[4,1024,128]{2,1,0:T(8,128)(2,1)}), bf16[4,1024,128]{2,1,0:T(8,128)(2,1)}, u32[]{:S(2)}, u32[]{:S(2)}) %all-to-all-start.1) | async-done | bytes 1048608 | tf_op jit(solution)/shard_map/all_to_all | solution.py:34
  72.9 2.9 %collective-permute-start.4 = (bf16[4,1024,128]{2,1,0:T(8,128)(2,1)}, bf16[4,1024,128]{2,1,0:T(8,128)(2,1)S(1)}, u32[]{:S(2)}, u32[]{:S(2)}) collective-permute-start(bf16[4,1024,128]{2,1,0:T(8,128)(2,1)} %all-to-all-done.1), channel_id=1, source_target_pairs={{0,1},{1,0},{2,3},{3,2},{4,5},{5,4},{6,7},{7,6},{8,9},{9,8},{10,11... | collective-permute-start | bytes 3145736 | tf_op jit(solution)/shard_map/ppermute | solution.py:44
  75.8 2.5 %add_convert_fusion = bf16[4,1024,128]{2,1,0:T(8,128)(2,1)} fusion(bf16[4,1024,128]{2,1,0:T(8,128)(2,1)} %collective-permute-done.8, bf16[1,1024,128]{2,1,0:T(8,128)(2,1)S(1)} %fusion.12, bf16[1,1024,128]{2,1,0:T(8,128)(2,1)S(1)} %fusion.11, bf16[1,1024,128]{2,1,0:T(8,128)(2,1)S(1)} %fusion.10, bf16[1,1024,128]{2,1,0:T(8,128)(2,1)} %fusion.9), kind=kLoop, calls=%fused_computation | loop fusion | flops 3670016 | bytes 3145728 | tf_op jit(solution)/shard_map/convert_element_type | solution.py:120
  86.8 1.3 collective-permute-start.13
  88.1 5.4 %all-to-all-start.2 = ((bf16[4,1024,128]{2,1,0:T(8,128)(2,1)}), bf16[4,1024,128]{2,1,0:T(8,128)(2,1)}, u32[]{:S(2)}, u32[]{:S(2)}) async-start(bf16[4,1024,128]{2,1,0:T(8,128)(2,1)} %add_convert_fusion), calls=%async_computation.2 | async-start | bytes 2097152 | tf_op jit(solution)/shard_map/all_to_all | solution.py:34
  94.8 1.3 collective-permute-start.15
  96.1 1.3 collective-permute-start.16
  97.4 55.5 %collective-permute-done.13 = bf16[128,128]{1,0:T(8,128)(2,1)S(1)} collective-permute-done((bf16[128,128]{1,0:T(8,128)(2,1)S(1)}, bf16[128,128]{1,0:T(8,128)(2,1)S(1)}, u32[]{:S(2)}, u32[]{:S(2)}) %collective-permute-start.13) | collective-permute-done | bytes 32800 | tf_op jit(solution)/shard_map/ppermute | solution.py:63
  152.9 15.4 %collective-permute-done.14 = bf16[128,128]{1,0:T(8,128)(2,1)S(1)} collective-permute-done((bf16[128,128]{1,0:T(8,128)(2,1)S(1)}, bf16[128,128]{1,0:T(8,128)(2,1)S(1)}, u32[]{:S(2)}, u32[]{:S(2)}) %collective-permute-start.14) | collective-permute-done | bytes 32800 | tf_op jit(solution)/shard_map/ppermute | solution.py:63
  168.3 5.1 %collective-permute-done.15 = bf16[128,128]{1,0:T(8,128)(2,1)S(1)} collective-permute-done((bf16[128,128]{1,0:T(8,128)(2,1)S(1)}, bf16[128,128]{1,0:T(8,128)(2,1)S(1)}, u32[]{:S(2)}, u32[]{:S(2)}) %collective-permute-start.15) | collective-permute-done | bytes 32800 | tf_op jit(solution)/shard_map/ppermute | solution.py:63
  180.1 1.5 reduce_sum.39
  181.6 3.8 %collective-permute-start.9 = (bf16[8,64,128]{2,1,0:T(8,128)(2,1)S(1)}, bf16[8,64,128]{2,1,0:T(8,128)(2,1)}, u32[]{:S(2)}, u32[]{:S(2)}) collective-permute-start(bf16[8,64,128]{2,1,0:T(8,128)(2,1)S(1)} %dynamic-slice_bitcast_fusion.2), channel_id=1, source_target_pairs={{0,8},{8,0},{1,9},{9,1},{2,10},{10,2},{3,11},{11,3},{4,12},{12,4},... | collective-permute-start | bytes 393224 | tf_op jit(solution)/shard_map/ppermute | solution.py:44
  186.1 1.9 collective-permute-start.17
  189.0 6.1 %collective-permute-done.17 = bf16[8,2,64,128]{3,2,1,0:T(8,128)(2,1)} collective-permute-done((bf16[8,2,64,128]{3,2,1,0:T(8,128)(2,1)}, bf16[8,2,64,128]{3,2,1,0:T(8,128)(2,1)}, u32[]{:S(2)}, u32[]{:S(2)}) %collective-permute-start.17) | collective-permute-done | bytes 262176 | tf_op jit(solution)/shard_map/ppermute | solution.py:44
  195.1 1.8 fusion.31
  196.8 14.9 %all-to-all-start.3 = ((bf16[8,2,64,128]{3,2,1,0:T(8,128)(2,1)}), bf16[8,2,64,128]{3,2,1,0:T(8,128)(2,1)S(1)}, u32[]{:S(2)}, u32[]{:S(2)}) async-start(bf16[8,2,64,128]{3,2,1,0:T(8,128)(2,1)} %fusion.31), calls=%async_computation.3 | async-start | bytes 524288 | tf_op jit(solution)/shard_map/all_to_all | solution.py:34
  213.2 1.9 fusion.78
  215.7 1.3 convolution_bitcast_fusion
  217.0 6.7 %all-to-all-done.3 = bf16[8,2,64,128]{3,2,1,0:T(8,128)(2,1)S(1)} async-done(((bf16[8,2,64,128]{3,2,1,0:T(8,128)(2,1)}), bf16[8,2,64,128]{3,2,1,0:T(8,128)(2,1)S(1)}, u32[]{:S(2)}, u32[]{:S(2)}) %all-to-all-start.3) | async-done | bytes 262176 | tf_op jit(solution)/shard_map/all_to_all | solution.py:34
  223.7 7.6 %collective-permute-start.18 = (bf16[8,64,128]{2,1,0:T(8,128)(2,1)S(1)}, bf16[8,64,128]{2,1,0:T(8,128)(2,1)S(1)}, u32[]{:S(2)}, u32[]{:S(2)}) collective-permute-start(bf16[8,64,128]{2,1,0:T(8,128)(2,1)S(1)} %dynamic-slice_bitcast_fusion.1), channel_id=1, source_target_pairs={{0,1},{1,0},{2,3},{3,2},{4,5},{5,4},{6,7},{7,6},{8,9},{9,8},{10,11... | collective-permute-start | bytes 393224 | tf_op jit(solution)/shard_map/ppermute | solution.py:44
  231.4 1.4 fusion.8
  (125 shorter events, 30.1 us)
Async XLA Ops:
  0.0 11.9 %copy-start = (bf16[1,128,8192]{2,1,0:T(8,128)(2,1)S(1)}, bf16[1,128,8192]{2,1,0:T(8,128)(2,1)}, u32[]{:S(2)}) copy-start(bf16[1,128,8192]{2,1,0:T(8,128)(2,1)} %param.10) | copy-start | bytes 6291460
  0.0 19.2 %copy-start.9 = (bf16[128,128]{1,0:T(8,128)(2,1)S(1)}, bf16[128,128]{1,0:T(8,128)(2,1)}, u32[]{:S(2)}) copy-start(bf16[128,128]{1,0:T(8,128)(2,1)} %param.11) | copy-start | bytes 98308
  1.0 22.4 %collective-permute-start.5 = (bf16[128,128]{1,0:T(8,128)(2,1)S(1)}, bf16[128,128]{1,0:T(8,128)(2,1)S(1)}, u32[]{:S(2)}, u32[]{:S(2)}) collective-permute-start(bf16[128,128]{1,0:T(8,128)(2,1)S(1)} %get-tuple-element.10), channel_id=1, source_target_pairs={{0,384},{128,0},{256,128},{384,256},{1,385},{129,1},{257,129},{385... | collective-permute-start | bytes 98312 | tf_op jit(solution)/shard_map/ppermute | solution.py:63
  1.7 21.8 %collective-permute-start.6 = (bf16[128,128]{1,0:T(8,128)(2,1)S(1)}, bf16[128,128]{1,0:T(8,128)(2,1)S(1)}, u32[]{:S(2)}, u32[]{:S(2)}) collective-permute-start(bf16[128,128]{1,0:T(8,128)(2,1)S(1)} %get-tuple-element.10), channel_id=1, source_target_pairs={{0,256},{128,384},{256,0},{384,128},{1,257},{129,385},{257,1},{385... | collective-permute-start | bytes 98312 | tf_op jit(solution)/shard_map/ppermute | solution.py:63
  2.3 21.1 %collective-permute-start.7 = (bf16[128,128]{1,0:T(8,128)(2,1)S(1)}, bf16[128,128]{1,0:T(8,128)(2,1)S(1)}, u32[]{:S(2)}, u32[]{:S(2)}) collective-permute-start(bf16[128,128]{1,0:T(8,128)(2,1)S(1)} %get-tuple-element.10), channel_id=1, source_target_pairs={{0,128},{128,256},{256,384},{384,0},{1,129},{129,257},{257,385},{3... | collective-permute-start | bytes 98312 | tf_op jit(solution)/shard_map/ppermute | solution.py:63
  3.0 16.2 %collective-permute-start = (bf16[128,128]{1,0:T(8,128)(2,1)}, bf16[128,128]{1,0:T(8,128)(2,1)S(1)}, u32[]{:S(2)}, u32[]{:S(2)}) collective-permute-start(bf16[128,128]{1,0:T(8,128)(2,1)} %param.11), channel_id=1, source_target_pairs={{0,64},{16,80},{32,96},{48,112},{64,0},{80,16},{96,32},{112,48},{1... | collective-permute-start | bytes 98312 | tf_op jit(solution)/shard_map/ppermute | solution.py:44
  12.7 40.6 %all-to-all-start = ((bf16[16,64,128]{2,1,0:T(8,128)(2,1)}), bf16[16,64,128]{2,1,0:T(8,128)(2,1)S(1)}, u32[]{:S(2)}, u32[]{:S(2)}) async-start(bf16[16,64,128]{2,1,0:T(8,128)(2,1)} %copy.60), calls=%async_computation | async-start | bytes 524288 | tf_op jit(solution)/shard_map/all_to_all | solution.py:34
  19.3 9.0 %collective-permute-start.1 = (bf16[2,128,128]{2,1,0:T(8,128)(2,1)S(1)}, bf16[2,128,128]{2,1,0:T(8,128)(2,1)S(1)}, u32[]{:S(2)}, u32[]{:S(2)}) collective-permute-start(bf16[2,128,128]{2,1,0:T(8,128)(2,1)S(1)} %pad_maximum_fusion.5), channel_id=1, source_target_pairs={{0,32},{16,48},{32,0},{48,16},{64,96},{80,112},{96,64},{112,80},{1... | collective-permute-start | bytes 196616 | tf_op jit(solution)/shard_map/ppermute | solution.py:44
  28.4 9.3 %collective-permute-start.2 = (bf16[2,2,128,128]{3,2,1,0:T(8,128)(2,1)S(1)}, bf16[2,2,128,128]{3,2,1,0:T(8,128)(2,1)S(1)}, u32[]{:S(2)}, u32[]{:S(2)}) collective-permute-start(bf16[2,2,128,128]{3,2,1,0:T(8,128)(2,1)S(1)} %pad_maximum_fusion.4), channel_id=1, source_target_pairs={{0,16},{16,0},{32,48},{48,32},{64,80},{80,64},{96,112},{112,96},{1... | collective-permute-start | bytes 393224 | tf_op jit(solution)/shard_map/ppermute | solution.py:44
  37.7 7.1 %collective-permute-start.3 = (bf16[2,2,2,128,128]{4,3,2,1,0:T(8,128)(2,1)S(1)}, bf16[2,2,2,128,128]{4,3,2,1,0:T(8,128)(2,1)S(1)}, u32[]{:S(2)}, u32[]{:S(2)}) collective-permute-start(bf16[2,2,2,128,128]{4,3,2,1,0:T(8,128)(2,1)S(1)} %pad_maximum_fusion.2), channel_id=1, source_target_pairs={{0,8},{8,0},{1,9},{9,1},{2,10},{10,2},{3,11},{11,3},{4,12},{12,4},... | collective-permute-start | bytes 786440 | tf_op jit(solution)/shard_map/ppermute | solution.py:44
  40.6 18.5 %copy-start.3 = (bf16[8,128,128]{2,1,0:T(8,128)(2,1)}, bf16[8,128,128]{2,1,0:T(8,128)(2,1)S(1)}, u32[]{:S(2)}) copy-start(bf16[8,128,128]{2,1,0:T(8,128)(2,1)S(1)} %constant_dynamic-update-slice_fusion) | copy-start | bytes 786436
  47.1 28.7 %collective-permute-start.8 = (bf16[4,1024,128]{2,1,0:T(8,128)(2,1)}, bf16[4,1024,128]{2,1,0:T(8,128)(2,1)}, u32[]{:S(2)}, u32[]{:S(2)}) collective-permute-start(bf16[4,1024,128]{2,1,0:T(8,128)(2,1)} %pad_maximum_fusion), channel_id=1, source_target_pairs={{0,1},{1,0},{2,3},{3,2},{4,5},{5,4},{6,7},{7,6},{8,9},{9,8},{10,11... | collective-permute-start | bytes 3145736 | tf_op jit(solution)/shard_map/ppermute | solution.py:44
  54.5 18.4 %all-to-all-start.1 = ((bf16[4,1024,128]{2,1,0:T(8,128)(2,1)}), bf16[4,1024,128]{2,1,0:T(8,128)(2,1)}, u32[]{:S(2)}, u32[]{:S(2)}) async-start(bf16[4,1024,128]{2,1,0:T(8,128)(2,1)} %broadcast_in_dim.29), calls=%async_computation.1 | async-start | bytes 2097152 | tf_op jit(solution)/shard_map/all_to_all | solution.py:34
  72.9 10.4 %collective-permute-start.4 = (bf16[4,1024,128]{2,1,0:T(8,128)(2,1)}, bf16[4,1024,128]{2,1,0:T(8,128)(2,1)S(1)}, u32[]{:S(2)}, u32[]{:S(2)}) collective-permute-start(bf16[4,1024,128]{2,1,0:T(8,128)(2,1)} %all-to-all-done.1), channel_id=1, source_target_pairs={{0,1},{1,0},{2,3},{3,2},{4,5},{5,4},{6,7},{7,6},{8,9},{9,8},{10,11... | collective-permute-start | bytes 3145736 | tf_op jit(solution)/shard_map/ppermute | solution.py:44
  82.0 4.7 %copy-start.5 = (f32[128,128]{1,0:T(8,128)S(1)}, f32[128,128]{1,0:T(8,128)}, u32[]{:S(2)}) copy-start(f32[128,128]{1,0:T(8,128)} %param.12) | copy-start | bytes 196612
  82.0 4.7 %copy-start.6 = (f32[128,128]{1,0:T(8,128)S(1)}, f32[128,128]{1,0:T(8,128)}, u32[]{:S(2)}) copy-start(f32[128,128]{1,0:T(8,128)} %param.14) | copy-start | bytes 196612
  84.5 89.1 %copy-start.2 = (bf16[4,1024,128]{2,1,0:T(8,128)(2,1)S(1)}, bf16[4,1024,128]{2,1,0:T(8,128)(2,1)}, u32[]{:S(2)}) copy-start(bf16[4,1024,128]{2,1,0:T(8,128)(2,1)} %copy-done.1) | copy-start | bytes 3145732
  84.5 2.2 collective-permute-start.10
  85.3 1.4 collective-permute-start.11
  86.0 0.7 collective-permute-start.12
  86.8 66.1 %collective-permute-start.13 = (bf16[128,128]{1,0:T(8,128)(2,1)S(1)}, bf16[128,128]{1,0:T(8,128)(2,1)S(1)}, u32[]{:S(2)}, u32[]{:S(2)}) collective-permute-start(bf16[128,128]{1,0:T(8,128)(2,1)S(1)} %fusion.56), channel_id=1, source_target_pairs={{0,512},{128,640},{256,768},{384,896},{1,513},{129,641},{257,769},... | collective-permute-start | bytes 98312 | tf_op jit(solution)/shard_map/ppermute | solution.py:63
  88.1 91.9 %all-to-all-start.2 = ((bf16[4,1024,128]{2,1,0:T(8,128)(2,1)}), bf16[4,1024,128]{2,1,0:T(8,128)(2,1)}, u32[]{:S(2)}, u32[]{:S(2)}) async-start(bf16[4,1024,128]{2,1,0:T(8,128)(2,1)} %add_convert_fusion), calls=%async_computation.2 | async-start | bytes 2097152 | tf_op jit(solution)/shard_map/all_to_all | solution.py:34
  93.5 74.8 %collective-permute-start.14 = (bf16[128,128]{1,0:T(8,128)(2,1)S(1)}, bf16[128,128]{1,0:T(8,128)(2,1)S(1)}, u32[]{:S(2)}, u32[]{:S(2)}) collective-permute-start(bf16[128,128]{1,0:T(8,128)(2,1)S(1)} %fusion.56), channel_id=1, source_target_pairs={{0,896},{128,512},{256,640},{384,768},{1,897},{129,513},{257,641},... | collective-permute-start | bytes 98312 | tf_op jit(solution)/shard_map/ppermute | solution.py:63
  94.8 78.7 %collective-permute-start.15 = (bf16[128,128]{1,0:T(8,128)(2,1)S(1)}, bf16[128,128]{1,0:T(8,128)(2,1)S(1)}, u32[]{:S(2)}, u32[]{:S(2)}) collective-permute-start(bf16[128,128]{1,0:T(8,128)(2,1)S(1)} %fusion.56), channel_id=1, source_target_pairs={{0,768},{128,896},{256,512},{384,640},{1,769},{129,897},{257,513},... | collective-permute-start | bytes 98312 | tf_op jit(solution)/shard_map/ppermute | solution.py:63
  96.1 77.4 %collective-permute-start.16 = (bf16[128,128]{1,0:T(8,128)(2,1)S(1)}, bf16[128,128]{1,0:T(8,128)(2,1)S(1)}, u32[]{:S(2)}, u32[]{:S(2)}) collective-permute-start(bf16[128,128]{1,0:T(8,128)(2,1)S(1)} %fusion.56), channel_id=1, source_target_pairs={{0,640},{128,768},{256,896},{384,512},{1,641},{129,769},{257,897},... | collective-permute-start | bytes 98312 | tf_op jit(solution)/shard_map/ppermute | solution.py:63
  181.6 6.5 %collective-permute-start.9 = (bf16[8,64,128]{2,1,0:T(8,128)(2,1)S(1)}, bf16[8,64,128]{2,1,0:T(8,128)(2,1)}, u32[]{:S(2)}, u32[]{:S(2)}) collective-permute-start(bf16[8,64,128]{2,1,0:T(8,128)(2,1)S(1)} %dynamic-slice_bitcast_fusion.2), channel_id=1, source_target_pairs={{0,8},{8,0},{1,9},{9,1},{2,10},{10,2},{3,11},{11,3},{4,12},{12,4},... | collective-permute-start | bytes 393224 | tf_op jit(solution)/shard_map/ppermute | solution.py:44
  185.3 26.5 %copy-start.10 = (s32[16]{0:T(128)S(1)}, s32[16]{0:T(128)}, u32[]{:S(2)}) copy-start(s32[16]{0:T(128)} %param.19) | copy-start | bytes 196
  186.1 9.0 %collective-permute-start.17 = (bf16[8,2,64,128]{3,2,1,0:T(8,128)(2,1)}, bf16[8,2,64,128]{3,2,1,0:T(8,128)(2,1)}, u32[]{:S(2)}, u32[]{:S(2)}) collective-permute-start(bf16[8,2,64,128]{3,2,1,0:T(8,128)(2,1)} %fusion.32), channel_id=1, source_target_pairs={{0,8},{8,0},{1,9},{9,1},{2,10},{10,2},{3,11},{11,3},{4,12},{12,4},... | collective-permute-start | bytes 786440 | tf_op jit(solution)/shard_map/ppermute | solution.py:44
  188.0 23.8 %copy-start.8 = (bf16[8,16,128]{2,1,0:T(8,128)(2,1)S(1)}, bf16[8,16,128]{2,1,0:T(8,128)(2,1)}, u32[]{:S(2)}) copy-start(bf16[8,16,128]{2,1,0:T(8,128)(2,1)} %param.16) | copy-start | bytes 98308
  189.0 22.7 %copy-start.4 = (bf16[8,16,1024]{2,1,0:T(8,128)(2,1)S(1)}, bf16[8,16,1024]{2,1,0:T(8,128)(2,1)}, u32[]{:S(2)}) copy-start(bf16[8,16,1024]{2,1,0:T(8,128)(2,1)} %param.15) | copy-start | bytes 786436
  196.8 26.9 %all-to-all-start.3 = ((bf16[8,2,64,128]{3,2,1,0:T(8,128)(2,1)}), bf16[8,2,64,128]{3,2,1,0:T(8,128)(2,1)S(1)}, u32[]{:S(2)}, u32[]{:S(2)}) async-start(bf16[8,2,64,128]{3,2,1,0:T(8,128)(2,1)} %fusion.31), calls=%async_computation.3 | async-start | bytes 524288 | tf_op jit(solution)/shard_map/all_to_all | solution.py:34
  223.7 9.4 %collective-permute-start.18 = (bf16[8,64,128]{2,1,0:T(8,128)(2,1)S(1)}, bf16[8,64,128]{2,1,0:T(8,128)(2,1)S(1)}, u32[]{:S(2)}, u32[]{:S(2)}) collective-permute-start(bf16[8,64,128]{2,1,0:T(8,128)(2,1)S(1)} %dynamic-slice_bitcast_fusion.1), channel_id=1, source_target_pairs={{0,1},{1,0},{2,3},{3,2},{4,5},{5,4},{6,7},{7,6},{8,9},{9,8},{10,11... | collective-permute-start | bytes 393224 | tf_op jit(solution)/shard_map/ppermute | solution.py:44
  (3 other events, 8.4 us)

commit v3 on v2

--- a/solution.py
+++ b/solution.py
@@ -2,6 +2,7 @@
 import jax.numpy as jnp
 from jax import lax
 from jax.sharding import Mesh, PartitionSpec as P
+
 
 D = 8192
 KVH = 8
@@ -48,18 +49,9 @@
     return jnp.where(first, value, met), jnp.where(first, met, value)
 
 
-def doubled(value, axis):
-    by, at = lax.axis_size(axis) // 2, 0
-    while by:
-        first = lax.axis_index(axis) & by == 0
-        value = jnp.stack(ordered(value, swap(value, axis, by), first), axis=at)
-        by, at = by // 2, at + 1
-    return value, at
-
-
-def far_shift(value, by, to_role):
+def far_shift(value, by, from_role, to_role):
     far = lax.axis_size("zh")
-    pairs = [(i, to_role * far + (i + by) % far) for i in range(far)]
+    pairs = [(from_role * far + i, to_role * far + (i + by) % far) for i in range(far)]
     return lax.ppermute(value, ("role", "zh"), pairs)
 
 
@@ -100,44 +92,51 @@
     mine = lax.dynamic_slice(hidden[0], (core_at * half, x_at * near * block), (half, near * block))
     mine = mine.reshape(half, near, block).transpose(1, 0, 2)
     mine = exchange(mine, NEAR)
+
+    by, grads, at = line // 2, out_grad, 0
+    while by:
+        first = lax.axis_index("zl") & by == 0
+        grads = jnp.stack(ordered(grads, swap(grads, "zl", by), first), axis=at)
+        if at == 0:
+            grads, mine = lax.optimization_barrier((grads, mine))
+        by, at = by // 2, at + 1
+    grads = jnp.stack(ordered(grads, swap(grads, "yl"), yl_at == 0), axis=at)
+    grads = grads.reshape(near, tokens, width_here)
+    at_mine, at_other = (
+        lax.dynamic_slice(grads, (0, at * half, 0), (near, half, width_here)).reshape(near * half, width_here)
+        for at in (core_at, 1 - core_at)
+    )
+
     mine = gather(mine.reshape(near * half, block), "x")
     other = swap(mine, "core")
 
-    grads, at = doubled(out_grad, "zl")
-    grads = jnp.stack(ordered(grads, swap(grads, "yl"), yl_at == 0), axis=at)
-    grads = grads.reshape(near, tokens, width_here)
-    rows_at = [lax.dynamic_slice(grads, (0, at * half, 0), (near, half, width_here)) for at in (core_at, 1 - core_at)]
-    at_mine, at_other = (rows.reshape(near * half, width_here) for rows in rows_at)
-
-    old_weight = master.astype(jnp.bfloat16)
-    old_parts = {k: far_shift(old_weight, k, 0) for k in far_order(far)[:-1]}
+    partial = jnp.stack(
+        [
+            dot32(mine[f], at_mine, ((0,), (0,))) + dot32(other[f], at_other, ((0,), (0,)))
+            for f in range(far)
+        ]
+    ).astype(jnp.bfloat16)
+    partial, old_weight = lax.optimization_barrier((partial, master.astype(jnp.bfloat16)))
+    gradient = [far_shift(at_index(partial, (zh_at + k) % far), k, 0, 1) for k in far_order(far)]
+
+    old_parts = {k: far_shift(old_weight, k, 0, 0) for k in far_order(far)[:-1]}
     old_parts[0] = old_weight
     old_weight = by_source([old_parts[k] for k in range(far)])
     kept, sent = (
         jnp.stack([dot32(rows, old_weight[f], ((1,), (1,))).astype(jnp.bfloat16) for f in range(far)])
         for rows in (at_mine, at_other)
     )
-    sent_back = (kept.astype(jnp.float32) + swap(sent, "core").astype(jnp.float32)).astype(jnp.bfloat16)
-
-    partial = jnp.stack(
-        [
-            dot32(mine[f], at_mine, ((0,), (0,))) + dot32(other[f], at_other, ((0,), (0,)))
-            for f in range(far)
-        ]
-    )
-    gradient = at_index(partial, zh_at)
-    narrow, sent_back = lax.optimization_barrier((partial.astype(jnp.bfloat16), sent_back))
-    for k in far_order(far)[:-1]:
-        gradient += far_shift(at_index(narrow, (zh_at + k) % far), k, 0).astype(jnp.float32)
-    fresh = adam_fresh(master, moment1, moment2, gradient)
-
-    back = jnp.sum(exchange(sent_back, "x").astype(jnp.float32), axis=0).astype(jnp.bfloat16)
+    back = (kept.astype(jnp.float32) + swap(sent, "core").astype(jnp.float32)).astype(jnp.bfloat16)
+    gradient, back = lax.optimization_barrier((gradient, back))
+    back = jnp.sum(exchange(back, "x").astype(jnp.float32), axis=0).astype(jnp.bfloat16)
     back = back.reshape(line, 2, half, block)
     stays = lax.dynamic_index_in_dim(back, yl_at, 1, keepdims=False)
     leaves = lax.dynamic_index_in_dim(back, 1 - yl_at, 1, keepdims=False)
     back = jnp.stack(ordered(stays, swap(leaves, "yl"), yl_at == 0), axis=1)
 
-    parts = {k: far_shift(fresh, k, 1) for k in far_order(far)}
+    fresh = adam_fresh(master, moment1, moment2, sum(g.astype(jnp.float32) for g in gradient))
+    parts = {k: far_shift(fresh, k, 1, 1) for k in far_order(far)[:-1]}
+    parts[0] = fresh
     weight = by_source([parts[k] for k in range(far)])
     terms = [sum(dot32(rows[f], weight[f], ((1,), (0,))) for f in range(far)) for rows in (mine, other)]
     terms = jnp.stack([rows.reshape(line, 2, half, width_here) for rows in terms], axis=2)

time: 236 us -> 234 us (level)
  the two profiles are of different devices: /device:TPU:19 before, /device:TPU:25 now
where the time goes in v3:
time: 234 us; the launch traced here: 233 us
  starting transfers between devices  104 us (44%)
  waiting for transfers between devices  86.1 us (37%)
  matrix products  16.7 us (7%)
  other arithmetic  16.3 us (7%)
  local copies, waits for them, and re-layouts  8.13 us (3%)
    ppermute x10, waiting for transfers between devices, far_shift(): return lax.ppermute(value, ('role', 'zh'), pairs)  45 us
    ppermute x10, starting transfers between devices, far_shift(): return lax.ppermute(value, ('role', 'zh'), pairs)  37.7 us
    ppermute x9, starting transfers between devices, swap(): return lax.ppermute(value, axis, [(i, i ^ by) for i in range(peers)])  35.7 us
    all_to_all x4, starting transfers between devices, exchange(): return lax.all_to_all(value, axis, 0, 0, tiled=True)  31 us
    ppermute x9, waiting for transfers between devices, swap(): return lax.ppermute(value, axis, [(i, i ^ by) for i in range(peers)])  25 us
    all_to_all x4, waiting for transfers between devices, exchange(): return lax.all_to_all(value, axis, 0, 0, tiled=True)  16.2 us
    dot_general x24, matrix products, dot32(): lax.dot_general(a, b, (dims, ((), ())), preferred_element_type=jnp.float32)  10.6 us
  transfers between devices with their start and end apart: 23, of which 10 were waited for; matrix products, arithmetic and copies ran while one was open for 13% of the time, Pallas kernels for 0%

profile of v3, /device:TPU:25, one launch (start us, length us, event | category | flops | bytes accessed | tf_op | source)
XLA Modules:
  0.0 232.6 jit_solution(10926967225876524091)
XLA Ops:
  0.0 1.6 copy-done
  2.4 13.4 %all-to-all-start = ((bf16[16,64,128]{2,1,0:T(8,128)(2,1)}), bf16[16,64,128]{2,1,0:T(8,128)(2,1)S(1)}, u32[]{:S(2)}, u32[]{:S(2)}) async-start(bf16[16,64,128]{2,1,0:T(8,128)(2,1)} %copy.60), calls=%async_computation | async-start | bytes 524288 | tf_op jit(solution)/shard_map/all_to_all | solution.py:35
  15.9 7.0 %collective-permute-start = (bf16[128,128]{1,0:T(8,128)(2,1)S(1)}, bf16[128,128]{1,0:T(8,128)(2,1)S(1)}, u32[]{:S(2)}, u32[]{:S(2)}) collective-permute-start(bf16[128,128]{1,0:T(8,128)(2,1)S(1)} %copy-done.11), channel_id=1, source_target_pairs={{0,64},{16,80},{32,96},{48,112},{64,0},{80,16},{96,32},{112,48},{1... | collective-permute-start | bytes 98312 | tf_op jit(solution)/shard_map/ppermute | solution.py:45
  22.9 10.7 %collective-permute-done = bf16[128,128]{1,0:T(8,128)(2,1)S(1)} collective-permute-done((bf16[128,128]{1,0:T(8,128)(2,1)S(1)}, bf16[128,128]{1,0:T(8,128)(2,1)S(1)}, u32[]{:S(2)}, u32[]{:S(2)}) %collective-permute-start) | collective-permute-done | bytes 32800 | tf_op jit(solution)/shard_map/ppermute | solution.py:45
  33.7 1.9 collective-permute-start.1
  35.6 4.0 %collective-permute-done.1 = bf16[2,128,128]{2,1,0:T(8,128)(2,1)S(1)} collective-permute-done((bf16[2,128,128]{2,1,0:T(8,128)(2,1)S(1)}, bf16[2,128,128]{2,1,0:T(8,128)(2,1)S(1)}, u32[]{:S(2)}, u32[]{:S(2)}) %collective-permute-start.1) | collective-permute-done | bytes 65568 | tf_op jit(solution)/shard_map/ppermute | solution.py:45
  39.6 3.5 %collective-permute-start.2 = (bf16[2,2,128,128]{3,2,1,0:T(8,128)(2,1)S(1)}, bf16[2,2,128,128]{3,2,1,0:T(8,128)(2,1)}, u32[]{:S(2)}, u32[]{:S(2)}) collective-permute-start(bf16[2,2,128,128]{3,2,1,0:T(8,128)(2,1)S(1)} %pad_maximum_fusion.3), channel_id=1, source_target_pairs={{0,16},{16,0},{32,48},{48,32},{64,80},{80,64},{96,112},{112,96},{1... | collective-permute-start | bytes 393224 | tf_op jit(solution)/shard_map/ppermute | solution.py:45
  44.3 4.0 %all-to-all-start.1 = ((bf16[4,1024,128]{2,1,0:T(8,128)(2,1)}), bf16[4,1024,128]{2,1,0:T(8,128)(2,1)S(1)}, u32[]{:S(2)}, u32[]{:S(2)}) async-start(bf16[4,1024,128]{2,1,0:T(8,128)(2,1)} %broadcast_in_dim.29), calls=%async_computation.1 | async-start | bytes 2097152 | tf_op jit(solution)/shard_map/all_to_all | solution.py:35
  49.9 1.9 collective-permute-start.3
  51.9 1.4 convert_element_type.90
  53.3 4.2 %collective-permute-done.3 = bf16[2,2,2,128,128]{4,3,2,1,0:T(8,128)(2,1)} collective-permute-done((bf16[2,2,2,128,128]{4,3,2,1,0:T(8,128)(2,1)}, bf16[2,2,2,128,128]{4,3,2,1,0:T(8,128)(2,1)}, u32[]{:S(2)}, u32[]{:S(2)}) %collective-permute-start.3) | collective-permute-done | bytes 262176 | tf_op jit(solution)/shard_map/ppermute | solution.py:45
  59.9 6.3 %collective-permute-start.4 = (bf16[4,1024,128]{2,1,0:T(8,128)(2,1)S(1)}, bf16[4,1024,128]{2,1,0:T(8,128)(2,1)S(1)}, u32[]{:S(2)}, u32[]{:S(2)}) collective-permute-start(bf16[4,1024,128]{2,1,0:T(8,128)(2,1)S(1)} %all-to-all-done.1), channel_id=1, source_target_pairs={{0,1},{1,0},{2,3},{3,2},{4,5},{5,4},{6,7},{7,6},{8,9},{9,8},{10,11... | collective-permute-start | bytes 3145736 | tf_op jit(solution)/shard_map/ppermute | solution.py:45
  73.9 2.2 collective-permute-start.12
  76.2 1.3 collective-permute-start.5
  85.5 2.5 %add_convert_fusion = bf16[4,1024,128]{2,1,0:T(8,128)(2,1)} fusion(bf16[4,1024,128]{2,1,0:T(8,128)(2,1)} %collective-permute-done.12, bf16[1,1024,128]{2,1,0:T(8,128)(2,1)S(1)} %fusion.12, bf16[1,1024,128]{2,1,0:T(8,128)(2,1)S(1)} %fusion.11, bf16[1,1024,128]{2,1,0:T(8,128)(2,1)S(1)} %fusion.10, bf16[1,1024,128]{2,1,0:T(8,128)(2,1)S(1)} %fusion.9), kind=kLoop, calls=%fused_computation | loop fusion | flops 3670016 | bytes 3145728 | tf_op jit(solution)/shard_map/convert_element_type | solution.py:129
  88.0 42.1 %collective-permute-done.5 = bf16[128,128]{1,0:T(8,128)(2,1)S(1)} collective-permute-done((bf16[128,128]{1,0:T(8,128)(2,1)S(1)}, bf16[128,128]{1,0:T(8,128)(2,1)S(1)}, u32[]{:S(2)}, u32[]{:S(2)}) %collective-permute-start.5) | collective-permute-done | bytes 32800 | tf_op jit(solution)/shard_map/ppermute | solution.py:55
  130.1 2.9 %collective-permute-done.7 = bf16[128,128]{1,0:T(8,128)(2,1)S(1)} collective-permute-done((bf16[128,128]{1,0:T(8,128)(2,1)S(1)}, bf16[128,128]{1,0:T(8,128)(2,1)S(1)}, u32[]{:S(2)}, u32[]{:S(2)}) %collective-permute-start.7) | collective-permute-done | bytes 32800 | tf_op jit(solution)/shard_map/ppermute | solution.py:55
  133.0 8.3 %collective-permute-start.14 = (bf16[128,128]{1,0:T(8,128)(2,1)S(1)}, bf16[128,128]{1,0:T(8,128)(2,1)S(1)}, u32[]{:S(2)}, u32[]{:S(2)}) collective-permute-start(bf16[128,128]{1,0:T(8,128)(2,1)S(1)} %get-tuple-element.24), channel_id=1, source_target_pairs={{512,896},{640,512},{768,640},{896,768},{513,897},{641,513},{769,6... | collective-permute-start | bytes 98312 | tf_op jit(solution)/shard_map/ppermute | solution.py:55
  141.4 12.6 %collective-permute-start.15 = (bf16[128,128]{1,0:T(8,128)(2,1)S(1)}, bf16[128,128]{1,0:T(8,128)(2,1)S(1)}, u32[]{:S(2)}, u32[]{:S(2)}) collective-permute-start(bf16[128,128]{1,0:T(8,128)(2,1)S(1)} %get-tuple-element.24), channel_id=1, source_target_pairs={{512,768},{640,896},{768,512},{896,640},{513,769},{641,897},{769,5... | collective-permute-start | bytes 98312 | tf_op jit(solution)/shard_map/ppermute | solution.py:55
  153.9 9.7 %collective-permute-start.16 = (bf16[128,128]{1,0:T(8,128)(2,1)S(1)}, bf16[128,128]{1,0:T(8,128)(2,1)S(1)}, u32[]{:S(2)}, u32[]{:S(2)}) collective-permute-start(bf16[128,128]{1,0:T(8,128)(2,1)S(1)} %get-tuple-element.24), channel_id=1, source_target_pairs={{512,640},{640,768},{768,896},{896,512},{513,641},{641,769},{769,8... | collective-permute-start | bytes 98312 | tf_op jit(solution)/shard_map/ppermute | solution.py:55
  163.6 4.7 %all-to-all-start.2 = ((bf16[4,1024,128]{2,1,0:T(8,128)(2,1)}), bf16[4,1024,128]{2,1,0:T(8,128)(2,1)}, u32[]{:S(2)}, u32[]{:S(2)}) async-start(bf16[4,1024,128]{2,1,0:T(8,128)(2,1)} %add_convert_fusion), calls=%async_computation.2 | async-start | bytes 2097152 | tf_op jit(solution)/shard_map/all_to_all | solution.py:35
  172.1 9.9 %all-to-all-done.2 = bf16[4,1024,128]{2,1,0:T(8,128)(2,1)} async-done(((bf16[4,1024,128]{2,1,0:T(8,128)(2,1)}), bf16[4,1024,128]{2,1,0:T(8,128)(2,1)}, u32[]{:S(2)}, u32[]{:S(2)}) %all-to-all-start.2) | async-done | bytes 1048608 | tf_op jit(solution)/shard_map/all_to_all | solution.py:35
  181.9 1.5 reduce_sum.39
  183.4 1.9 collective-permute-start.13
  186.2 3.4 %collective-permute-start.17 = (bf16[8,2,64,128]{3,2,1,0:T(8,128)(2,1)}, bf16[8,2,64,128]{3,2,1,0:T(8,128)(2,1)}, u32[]{:S(2)}, u32[]{:S(2)}) collective-permute-start(bf16[8,2,64,128]{3,2,1,0:T(8,128)(2,1)} %fusion.36), channel_id=1, source_target_pairs={{0,8},{8,0},{1,9},{9,1},{2,10},{10,2},{3,11},{11,3},{4,12},{12,4},... | collective-permute-start | bytes 786440 | tf_op jit(solution)/shard_map/ppermute | solution.py:45
  190.5 6.0 %collective-permute-done.17 = bf16[8,2,64,128]{3,2,1,0:T(8,128)(2,1)} collective-permute-done((bf16[8,2,64,128]{3,2,1,0:T(8,128)(2,1)}, bf16[8,2,64,128]{3,2,1,0:T(8,128)(2,1)}, u32[]{:S(2)}, u32[]{:S(2)}) %collective-permute-start.17) | collective-permute-done | bytes 262176 | tf_op jit(solution)/shard_map/ppermute | solution.py:45
  196.5 1.8 fusion.35
  198.2 8.8 %all-to-all-start.3 = ((bf16[8,2,64,128]{3,2,1,0:T(8,128)(2,1)}), bf16[8,2,64,128]{3,2,1,0:T(8,128)(2,1)}, u32[]{:S(2)}, u32[]{:S(2)}) async-start(bf16[8,2,64,128]{3,2,1,0:T(8,128)(2,1)} %fusion.35), calls=%async_computation.3 | async-start | bytes 524288 | tf_op jit(solution)/shard_map/all_to_all | solution.py:35
  209.4 2.0 fusion.80
  213.4 5.7 %all-to-all-done.3 = bf16[8,2,64,128]{3,2,1,0:T(8,128)(2,1)} async-done(((bf16[8,2,64,128]{3,2,1,0:T(8,128)(2,1)}), bf16[8,2,64,128]{3,2,1,0:T(8,128)(2,1)}, u32[]{:S(2)}, u32[]{:S(2)}) %all-to-all-start.3) | async-done | bytes 262176 | tf_op jit(solution)/shard_map/all_to_all | solution.py:35
  220.0 7.6 %collective-permute-start.18 = (bf16[8,64,128]{2,1,0:T(8,128)(2,1)S(1)}, bf16[8,64,128]{2,1,0:T(8,128)(2,1)S(1)}, u32[]{:S(2)}, u32[]{:S(2)}) collective-permute-start(bf16[8,64,128]{2,1,0:T(8,128)(2,1)S(1)} %dynamic-slice_bitcast_fusion.1), channel_id=1, source_target_pairs={{0,1},{1,0},{2,3},{3,2},{4,5},{5,4},{6,7},{7,6},{8,9},{9,8},{10,11... | collective-permute-start | bytes 393224 | tf_op jit(solution)/shard_map/ppermute | solution.py:45
  228.6 1.5 fusion.8
  (128 shorter events, 35.3 us)
Async XLA Ops:
  0.0 15.9 %copy-start.11 = (bf16[128,128]{1,0:T(8,128)(2,1)S(1)}, bf16[128,128]{1,0:T(8,128)(2,1)}, u32[]{:S(2)}) copy-start(bf16[128,128]{1,0:T(8,128)(2,1)} %param.11) | copy-start | bytes 98308
  2.4 31.2 %all-to-all-start = ((bf16[16,64,128]{2,1,0:T(8,128)(2,1)}), bf16[16,64,128]{2,1,0:T(8,128)(2,1)S(1)}, u32[]{:S(2)}, u32[]{:S(2)}) async-start(bf16[16,64,128]{2,1,0:T(8,128)(2,1)} %copy.60), calls=%async_computation | async-start | bytes 524288 | tf_op jit(solution)/shard_map/all_to_all | solution.py:35
  15.9 17.7 %collective-permute-start = (bf16[128,128]{1,0:T(8,128)(2,1)S(1)}, bf16[128,128]{1,0:T(8,128)(2,1)S(1)}, u32[]{:S(2)}, u32[]{:S(2)}) collective-permute-start(bf16[128,128]{1,0:T(8,128)(2,1)S(1)} %copy-done.11), channel_id=1, source_target_pairs={{0,64},{16,80},{32,96},{48,112},{64,0},{80,16},{96,32},{112,48},{1... | collective-permute-start | bytes 98312 | tf_op jit(solution)/shard_map/ppermute | solution.py:45
  33.7 5.9 %collective-permute-start.1 = (bf16[2,128,128]{2,1,0:T(8,128)(2,1)S(1)}, bf16[2,128,128]{2,1,0:T(8,128)(2,1)S(1)}, u32[]{:S(2)}, u32[]{:S(2)}) collective-permute-start(bf16[2,128,128]{2,1,0:T(8,128)(2,1)S(1)} %pad_maximum_fusion.5), channel_id=1, source_target_pairs={{0,32},{16,48},{32,0},{48,16},{64,96},{80,112},{96,64},{112,80},{1... | collective-permute-start | bytes 196616 | tf_op jit(solution)/shard_map/ppermute | solution.py:45
  39.6 8.7 %collective-permute-start.2 = (bf16[2,2,128,128]{3,2,1,0:T(8,128)(2,1)S(1)}, bf16[2,2,128,128]{3,2,1,0:T(8,128)(2,1)}, u32[]{:S(2)}, u32[]{:S(2)}) collective-permute-start(bf16[2,2,128,128]{3,2,1,0:T(8,128)(2,1)S(1)} %pad_maximum_fusion.3), channel_id=1, source_target_pairs={{0,16},{16,0},{32,48},{48,32},{64,80},{80,64},{96,112},{112,96},{1... | collective-permute-start | bytes 393224 | tf_op jit(solution)/shard_map/ppermute | solution.py:45
  44.3 15.7 %all-to-all-start.1 = ((bf16[4,1024,128]{2,1,0:T(8,128)(2,1)}), bf16[4,1024,128]{2,1,0:T(8,128)(2,1)S(1)}, u32[]{:S(2)}, u32[]{:S(2)}) async-start(bf16[4,1024,128]{2,1,0:T(8,128)(2,1)} %broadcast_in_dim.29), calls=%async_computation.1 | async-start | bytes 2097152 | tf_op jit(solution)/shard_map/all_to_all | solution.py:35
  49.9 7.6 %collective-permute-start.3 = (bf16[2,2,2,128,128]{4,3,2,1,0:T(8,128)(2,1)}, bf16[2,2,2,128,128]{4,3,2,1,0:T(8,128)(2,1)}, u32[]{:S(2)}, u32[]{:S(2)}) collective-permute-start(bf16[2,2,2,128,128]{4,3,2,1,0:T(8,128)(2,1)} %pad_maximum_fusion.2), channel_id=1, source_target_pairs={{0,8},{8,0},{1,9},{9,1},{2,10},{10,2},{3,11},{11,3},{4,12},{12,4},... | collective-permute-start | bytes 786440 | tf_op jit(solution)/shard_map/ppermute | solution.py:45
  59.9 8.6 %collective-permute-start.4 = (bf16[4,1024,128]{2,1,0:T(8,128)(2,1)S(1)}, bf16[4,1024,128]{2,1,0:T(8,128)(2,1)S(1)}, u32[]{:S(2)}, u32[]{:S(2)}) collective-permute-start(bf16[4,1024,128]{2,1,0:T(8,128)(2,1)S(1)} %all-to-all-done.1), channel_id=1, source_target_pairs={{0,1},{1,0},{2,3},{3,2},{4,5},{5,4},{6,7},{7,6},{8,9},{9,8},{10,11... | collective-permute-start | bytes 3145736 | tf_op jit(solution)/shard_map/ppermute | solution.py:45
  68.5 3.8 %copy-start.2 = (bf16[4,1024,128]{2,1,0:T(8,128)(2,1)}, bf16[4,1024,128]{2,1,0:T(8,128)(2,1)S(1)}, u32[]{:S(2)}) copy-start(bf16[4,1024,128]{2,1,0:T(8,128)(2,1)S(1)} %collective-permute-done.4) | copy-start | bytes 3145732
  69.6 2.0 collective-permute-start.9
  70.3 1.4 collective-permute-start.10
  71.0 0.7 collective-permute-start.11
  73.9 11.6 %collective-permute-start.12 = (bf16[4,1024,128]{2,1,0:T(8,128)(2,1)}, bf16[4,1024,128]{2,1,0:T(8,128)(2,1)}, u32[]{:S(2)}, u32[]{:S(2)}) collective-permute-start(bf16[4,1024,128]{2,1,0:T(8,128)(2,1)} %pad_maximum_fusion), channel_id=1, source_target_pairs={{0,1},{1,0},{2,3},{3,2},{4,5},{5,4},{6,7},{7,6},{8,9},{9,8},{10,11... | collective-permute-start | bytes 3145736 | tf_op jit(solution)/shard_map/ppermute | solution.py:45
  76.2 53.8 %collective-permute-start.5 = (bf16[128,128]{1,0:T(8,128)(2,1)S(1)}, bf16[128,128]{1,0:T(8,128)(2,1)S(1)}, u32[]{:S(2)}, u32[]{:S(2)}) collective-permute-start(bf16[128,128]{1,0:T(8,128)(2,1)S(1)} %get-tuple-element.38), channel_id=1, source_target_pairs={{0,768},{128,896},{256,512},{384,640},{1,769},{129,897},{257,513},... | collective-permute-start | bytes 98312 | tf_op jit(solution)/shard_map/ppermute | solution.py:55
  77.5 52.5 %collective-permute-start.6 = (bf16[128,128]{1,0:T(8,128)(2,1)S(1)}, bf16[128,128]{1,0:T(8,128)(2,1)S(1)}, u32[]{:S(2)}, u32[]{:S(2)}) collective-permute-start(bf16[128,128]{1,0:T(8,128)(2,1)S(1)} %get-tuple-element.37), channel_id=1, source_target_pairs={{0,640},{128,768},{256,896},{384,512},{1,641},{129,769},{257,897},... | collective-permute-start | bytes 98312 | tf_op jit(solution)/shard_map/ppermute | solution.py:55
  78.8 54.1 %collective-permute-start.7 = (bf16[128,128]{1,0:T(8,128)(2,1)S(1)}, bf16[128,128]{1,0:T(8,128)(2,1)S(1)}, u32[]{:S(2)}, u32[]{:S(2)}) collective-permute-start(bf16[128,128]{1,0:T(8,128)(2,1)S(1)} %get-tuple-element.36), channel_id=1, source_target_pairs={{0,896},{128,512},{256,640},{384,768},{1,897},{129,513},{257,641},... | collective-permute-start | bytes 98312 | tf_op jit(solution)/shard_map/ppermute | solution.py:55
  80.1 52.8 %collective-permute-start.8 = (bf16[128,128]{1,0:T(8,128)(2,1)S(1)}, bf16[128,128]{1,0:T(8,128)(2,1)S(1)}, u32[]{:S(2)}, u32[]{:S(2)}) collective-permute-start(bf16[128,128]{1,0:T(8,128)(2,1)S(1)} %get-tuple-element.35), channel_id=1, source_target_pairs={{0,512},{128,640},{256,768},{384,896},{1,513},{129,641},{257,769},... | collective-permute-start | bytes 98312 | tf_op jit(solution)/shard_map/ppermute | solution.py:55
  83.4 49.5 %copy-start.7 = (f32[128,128]{1,0:T(8,128)S(1)}, f32[128,128]{1,0:T(8,128)}, u32[]{:S(2)}) copy-start(f32[128,128]{1,0:T(8,128)} %param.12) | copy-start | bytes 196612
  83.4 49.5 %copy-start.8 = (f32[128,128]{1,0:T(8,128)S(1)}, f32[128,128]{1,0:T(8,128)}, u32[]{:S(2)}) copy-start(f32[128,128]{1,0:T(8,128)} %param.14) | copy-start | bytes 196612
  83.4 49.5 %copy-start.9 = (f32[128,128]{1,0:T(8,128)S(1)}, f32[128,128]{1,0:T(8,128)}, u32[]{:S(2)}) copy-start(f32[128,128]{1,0:T(8,128)} %param.13) | copy-start | bytes 196612
  133.0 35.3 %collective-permute-start.14 = (bf16[128,128]{1,0:T(8,128)(2,1)S(1)}, bf16[128,128]{1,0:T(8,128)(2,1)S(1)}, u32[]{:S(2)}, u32[]{:S(2)}) collective-permute-start(bf16[128,128]{1,0:T(8,128)(2,1)S(1)} %get-tuple-element.24), channel_id=1, source_target_pairs={{512,896},{640,512},{768,640},{896,768},{513,897},{641,513},{769,6... | collective-permute-start | bytes 98312 | tf_op jit(solution)/shard_map/ppermute | solution.py:55
  141.4 27.0 %collective-permute-start.15 = (bf16[128,128]{1,0:T(8,128)(2,1)S(1)}, bf16[128,128]{1,0:T(8,128)(2,1)S(1)}, u32[]{:S(2)}, u32[]{:S(2)}) collective-permute-start(bf16[128,128]{1,0:T(8,128)(2,1)S(1)} %get-tuple-element.24), channel_id=1, source_target_pairs={{512,768},{640,896},{768,512},{896,640},{513,769},{641,897},{769,5... | collective-permute-start | bytes 98312 | tf_op jit(solution)/shard_map/ppermute | solution.py:55
  153.9 14.4 %collective-permute-start.16 = (bf16[128,128]{1,0:T(8,128)(2,1)S(1)}, bf16[128,128]{1,0:T(8,128)(2,1)S(1)}, u32[]{:S(2)}, u32[]{:S(2)}) collective-permute-start(bf16[128,128]{1,0:T(8,128)(2,1)S(1)} %get-tuple-element.24), channel_id=1, source_target_pairs={{512,640},{640,768},{768,896},{896,512},{513,641},{641,769},{769,8... | collective-permute-start | bytes 98312 | tf_op jit(solution)/shard_map/ppermute | solution.py:55
  163.6 18.3 %all-to-all-start.2 = ((bf16[4,1024,128]{2,1,0:T(8,128)(2,1)}), bf16[4,1024,128]{2,1,0:T(8,128)(2,1)}, u32[]{:S(2)}, u32[]{:S(2)}) async-start(bf16[4,1024,128]{2,1,0:T(8,128)(2,1)} %add_convert_fusion), calls=%async_computation.2 | async-start | bytes 2097152 | tf_op jit(solution)/shard_map/all_to_all | solution.py:35
  171.8 13.5 %copy-start.1 = (f32[1024,128]{1,0:T(8,128)S(1)}, f32[1024,128]{1,0:T(8,128)}, u32[]{:S(2)}) copy-start(f32[1024,128]{1,0:T(8,128)} %convolution_add_fusion.2) | copy-start | bytes 1572868
  183.4 6.1 %collective-permute-start.13 = (bf16[8,64,128]{2,1,0:T(8,128)(2,1)S(1)}, bf16[8,64,128]{2,1,0:T(8,128)(2,1)}, u32[]{:S(2)}, u32[]{:S(2)}) collective-permute-start(bf16[8,64,128]{2,1,0:T(8,128)(2,1)S(1)} %dynamic-slice_bitcast_fusion.2), channel_id=1, source_target_pairs={{0,8},{8,0},{1,9},{9,1},{2,10},{10,2},{3,11},{11,3},{4,12},{12,4},... | collective-permute-start | bytes 393224 | tf_op jit(solution)/shard_map/ppermute | solution.py:45
  185.4 22.7 %copy-start.12 = (s32[16]{0:T(128)S(1)}, s32[16]{0:T(128)}, u32[]{:S(2)}) copy-start(s32[16]{0:T(128)} %param.19) | copy-start | bytes 196
  186.2 10.3 %collective-permute-start.17 = (bf16[8,2,64,128]{3,2,1,0:T(8,128)(2,1)}, bf16[8,2,64,128]{3,2,1,0:T(8,128)(2,1)}, u32[]{:S(2)}, u32[]{:S(2)}) collective-permute-start(bf16[8,2,64,128]{3,2,1,0:T(8,128)(2,1)} %fusion.36), channel_id=1, source_target_pairs={{0,8},{8,0},{1,9},{9,1},{2,10},{10,2},{3,11},{11,3},{4,12},{12,4},... | collective-permute-start | bytes 786440 | tf_op jit(solution)/shard_map/ppermute | solution.py:45
  189.5 18.6 %copy-start.10 = (bf16[8,16,128]{2,1,0:T(8,128)(2,1)S(1)}, bf16[8,16,128]{2,1,0:T(8,128)(2,1)}, u32[]{:S(2)}) copy-start(bf16[8,16,128]{2,1,0:T(8,128)(2,1)} %param.16) | copy-start | bytes 98308
  198.2 20.9 %all-to-all-start.3 = ((bf16[8,2,64,128]{3,2,1,0:T(8,128)(2,1)}), bf16[8,2,64,128]{3,2,1,0:T(8,128)(2,1)}, u32[]{:S(2)}, u32[]{:S(2)}) async-start(bf16[8,2,64,128]{3,2,1,0:T(8,128)(2,1)} %fusion.35), calls=%async_computation.3 | async-start | bytes 524288 | tf_op jit(solution)/shard_map/all_to_all | solution.py:35
  209.4 2.7 %copy-start.13 = (bf16[16,256,128]{2,1,0:T(8,128)(2,1)S(1)}, bf16[16,256,128]{2,1,0:T(8,128)(2,1)}, u32[]{:S(2)}) copy-start(bf16[16,256,128]{2,1,0:T(8,128)(2,1)} %param.18) | copy-start | bytes 3145732
  220.0 10.5 %collective-permute-start.18 = (bf16[8,64,128]{2,1,0:T(8,128)(2,1)S(1)}, bf16[8,64,128]{2,1,0:T(8,128)(2,1)S(1)}, u32[]{:S(2)}, u32[]{:S(2)}) collective-permute-start(bf16[8,64,128]{2,1,0:T(8,128)(2,1)S(1)} %dynamic-slice_bitcast_fusion.1), channel_id=1, source_target_pairs={{0,1},{1,0},{2,3},{3,2},{4,5},{5,4},{6,7},{7,6},{8,9},{9,8},{10,11... | collective-permute-start | bytes 393224 | tf_op jit(solution)/shard_map/ppermute | solution.py:45
  (5 other events, 8.7 us)

commit v4 on v3

--- a/solution.py
+++ b/solution.py
@@ -17,6 +17,7 @@
 bias_one = 1.0 - 0.9**10
 bias_two = 1.0 - 0.95**10
 neg_fill = -1e30
+
 
 DP = ("zh", "zl", "yl")
 TP = ("x", "core")
@@ -107,8 +108,12 @@
         for at in (core_at, 1 - core_at)
     )
 
+    mine, old_weight = lax.optimization_barrier((mine, master.astype(jnp.bfloat16)))
     mine = gather(mine.reshape(near * half, block), "x")
     other = swap(mine, "core")
+
+    old_parts = {k: far_shift(old_weight, k, 1, 0) for k in far_order(far)[:-1]}
+    old_parts[0] = old_weight
 
     partial = jnp.stack(
         [
@@ -116,28 +121,33 @@
             for f in range(far)
         ]
     ).astype(jnp.bfloat16)
-    partial, old_weight = lax.optimization_barrier((partial, master.astype(jnp.bfloat16)))
-    gradient = [far_shift(at_index(partial, (zh_at + k) % far), k, 0, 1) for k in far_order(far)]
-
-    old_parts = {k: far_shift(old_weight, k, 0, 0) for k in far_order(far)[:-1]}
-    old_parts[0] = old_weight
-    old_weight = by_source([old_parts[k] for k in range(far)])
+    gradient = [at_index(partial, zh_at)] + [
+        far_shift(at_index(partial, (zh_at + k) % far), k, 0, 0)
+        for k in far_order(far)[:-1]
+    ]
+
+    _, *old_parts = lax.optimization_barrier((partial, *(old_parts[k] for k in range(far))))
+    old_weight = by_source(old_parts)
     kept, sent = (
         jnp.stack([dot32(rows, old_weight[f], ((1,), (1,))).astype(jnp.bfloat16) for f in range(far)])
         for rows in (at_mine, at_other)
     )
     back = (kept.astype(jnp.float32) + swap(sent, "core").astype(jnp.float32)).astype(jnp.bfloat16)
     gradient, back = lax.optimization_barrier((gradient, back))
-    back = jnp.sum(exchange(back, "x").astype(jnp.float32), axis=0).astype(jnp.bfloat16)
+
+    fresh = adam_fresh(master, moment1, moment2, sum(g.astype(jnp.float32) for g in gradient))
+    parts = {k: far_shift(fresh, k, 0, 1) for k in far_order(far)}
+    parts = [parts[k] for k in range(far)]
+
+    back = exchange(back, "x")
+    back = jnp.sum(back.astype(jnp.float32), axis=0).astype(jnp.bfloat16)
     back = back.reshape(line, 2, half, block)
     stays = lax.dynamic_index_in_dim(back, yl_at, 1, keepdims=False)
     leaves = lax.dynamic_index_in_dim(back, 1 - yl_at, 1, keepdims=False)
     back = jnp.stack(ordered(stays, swap(leaves, "yl"), yl_at == 0), axis=1)
 
-    fresh = adam_fresh(master, moment1, moment2, sum(g.astype(jnp.float32) for g in gradient))
-    parts = {k: far_shift(fresh, k, 1, 1) for k in far_order(far)[:-1]}
-    parts[0] = fresh
-    weight = by_source([parts[k] for k in range(far)])
+    parts, back = lax.optimization_barrier((parts, back))
+    weight = by_source(parts)
     terms = [sum(dot32(rows[f], weight[f], ((1,), (0,))) for f in range(far)) for rows in (mine, other)]
     terms = jnp.stack([rows.reshape(line, 2, half, width_here) for rows in terms], axis=2)
     stays = lax.dynamic_index_in_dim(terms, yl_at, 1, keepdims=False)

time: 234 us -> 232 us (level)
  the two profiles are of different devices: /device:TPU:25 before, /device:TPU:17 now
where the time goes in v4:
time: 232 us; the launch traced here: 229 us
  starting transfers between devices  110 us (47%)
  waiting for transfers between devices  76.4 us (33%)
  other arithmetic  14.9 us (6%)
  matrix products  14.7 us (6%)
  local copies, waits for them, and re-layouts  12.8 us (6%)
    ppermute x9, starting transfers between devices, swap(): return lax.ppermute(value, axis, [(i, i ^ by) for i in range(peers)])  39.6 us
    all_to_all x4, starting transfers between devices, exchange(): return lax.all_to_all(value, axis, 0, 0, tiled=True)  37.4 us
    ppermute x10, waiting for transfers between devices, far_shift(): return lax.ppermute(value, ('role', 'zh'), pairs)  36.5 us
    ppermute x10, starting transfers between devices, far_shift(): return lax.ppermute(value, ('role', 'zh'), pairs)  32.8 us
    all_to_all x4, waiting for transfers between devices, exchange(): return lax.all_to_all(value, axis, 0, 0, tiled=True)  21.5 us
    ppermute x9, waiting for transfers between devices, swap(): return lax.ppermute(value, axis, [(i, i ^ by) for i in range(peers)])  18.4 us
    dot_general x24, matrix products, dot32(): lax.dot_general(a, b, (dims, ((), ())), preferred_element_type=jnp.float32)  8.68 us
    unnamed x47, local copies, waits for them, and re-layouts  6.19 us
  transfers between devices with their start and end apart: 23, of which 9 were waited for; matrix products, arithmetic and copies ran while one was open for 11% of the time, Pallas kernels for 0%

profile of v4, /device:TPU:17, one launch (start us, length us, event | category | flops | bytes accessed | tf_op | source)
XLA Modules:
  0.0 229.5 jit_solution(8914124378215743776)
XLA Ops:
  0.0 1.6 copy-done
  2.4 13.1 %all-to-all-start = ((bf16[16,64,128]{2,1,0:T(8,128)(2,1)}), bf16[16,64,128]{2,1,0:T(8,128)(2,1)S(1)}, u32[]{:S(2)}, u32[]{:S(2)}) async-start(bf16[16,64,128]{2,1,0:T(8,128)(2,1)} %copy.60), calls=%async_computation | async-start | bytes 524288 | tf_op jit(solution)/shard_map/all_to_all | solution.py:36
  15.5 7.2 %collective-permute-start = (bf16[128,128]{1,0:T(8,128)(2,1)S(1)}, bf16[128,128]{1,0:T(8,128)(2,1)S(1)}, u32[]{:S(2)}, u32[]{:S(2)}) collective-permute-start(bf16[128,128]{1,0:T(8,128)(2,1)S(1)} %copy-done.12), channel_id=1, source_target_pairs={{0,64},{16,80},{32,96},{48,112},{64,0},{80,16},{96,32},{112,48},{1... | collective-permute-start | bytes 98312 | tf_op jit(solution)/shard_map/ppermute | solution.py:46
  22.7 10.6 %collective-permute-done = bf16[128,128]{1,0:T(8,128)(2,1)S(1)} collective-permute-done((bf16[128,128]{1,0:T(8,128)(2,1)S(1)}, bf16[128,128]{1,0:T(8,128)(2,1)S(1)}, u32[]{:S(2)}, u32[]{:S(2)}) %collective-permute-start) | collective-permute-done | bytes 32800 | tf_op jit(solution)/shard_map/ppermute | solution.py:46
  33.3 1.9 collective-permute-start.1
  35.3 4.0 %collective-permute-done.1 = bf16[2,128,128]{2,1,0:T(8,128)(2,1)S(1)} collective-permute-done((bf16[2,128,128]{2,1,0:T(8,128)(2,1)S(1)}, bf16[2,128,128]{2,1,0:T(8,128)(2,1)S(1)}, u32[]{:S(2)}, u32[]{:S(2)}) %collective-permute-start.1) | collective-permute-done | bytes 65568 | tf_op jit(solution)/shard_map/ppermute | solution.py:46
  39.3 3.4 %collective-permute-start.2 = (bf16[2,2,128,128]{3,2,1,0:T(8,128)(2,1)S(1)}, bf16[2,2,128,128]{3,2,1,0:T(8,128)(2,1)}, u32[]{:S(2)}, u32[]{:S(2)}) collective-permute-start(bf16[2,2,128,128]{3,2,1,0:T(8,128)(2,1)S(1)} %pad_maximum_fusion.4), channel_id=1, source_target_pairs={{0,16},{16,0},{32,48},{48,32},{64,80},{80,64},{96,112},{112,96},{1... | collective-permute-start | bytes 393224 | tf_op jit(solution)/shard_map/ppermute | solution.py:46
  44.4 4.0 %all-to-all-start.1 = ((bf16[4,1024,128]{2,1,0:T(8,128)(2,1)}), bf16[4,1024,128]{2,1,0:T(8,128)(2,1)S(1)}, u32[]{:S(2)}, u32[]{:S(2)}) async-start(bf16[4,1024,128]{2,1,0:T(8,128)(2,1)} %broadcast_in_dim.29), calls=%async_computation.1 | async-start | bytes 2097152 | tf_op jit(solution)/shard_map/all_to_all | solution.py:36
  50.1 3.4 %collective-permute-start.3 = (bf16[2,2,2,128,128]{4,3,2,1,0:T(8,128)(2,1)}, bf16[2,2,2,128,128]{4,3,2,1,0:T(8,128)(2,1)}, u32[]{:S(2)}, u32[]{:S(2)}) collective-permute-start(bf16[2,2,2,128,128]{4,3,2,1,0:T(8,128)(2,1)} %pad_maximum_fusion.2), channel_id=1, source_target_pairs={{0,8},{8,0},{1,9},{9,1},{2,10},{10,2},{3,11},{11,3},{4,12},{12,4},... | collective-permute-start | bytes 786440 | tf_op jit(solution)/shard_map/ppermute | solution.py:46
  53.5 15.9 %collective-permute-start.10 = (bf16[128,128]{1,0:T(8,128)(2,1)}, bf16[128,128]{1,0:T(8,128)(2,1)}, u32[]{:S(2)}, u32[]{:S(2)}) collective-permute-start(bf16[128,128]{1,0:T(8,128)(2,1)} %convert_element_type.90), channel_id=1, source_target_pairs={{512,384},{640,0},{768,128},{896,256},{513,385},{641,1},{769,129},... | collective-permute-start | bytes 98312 | tf_op jit(solution)/shard_map/ppermute | solution.py:56
  69.4 1.9 collective-permute-start.8
  71.3 6.7 %collective-permute-start.9 = (bf16[128,128]{1,0:T(8,128)(2,1)}, bf16[128,128]{1,0:T(8,128)(2,1)}, u32[]{:S(2)}, u32[]{:S(2)}) collective-permute-start(bf16[128,128]{1,0:T(8,128)(2,1)} %convert_element_type.90), channel_id=1, source_target_pairs={{512,256},{640,384},{768,0},{896,128},{513,257},{641,385},{769,1},... | collective-permute-start | bytes 98312 | tf_op jit(solution)/shard_map/ppermute | solution.py:56
  79.8 5.7 %collective-permute-start.4 = (bf16[4,1024,128]{2,1,0:T(8,128)(2,1)S(1)}, bf16[4,1024,128]{2,1,0:T(8,128)(2,1)S(1)}, u32[]{:S(2)}, u32[]{:S(2)}) collective-permute-start(bf16[4,1024,128]{2,1,0:T(8,128)(2,1)S(1)} %all-to-all-done.1), channel_id=1, source_target_pairs={{0,1},{1,0},{2,3},{3,2},{4,5},{5,4},{6,7},{7,6},{8,9},{9,8},{10,11... | collective-permute-start | bytes 3145736 | tf_op jit(solution)/shard_map/ppermute | solution.py:46
  95.7 2.3 %collective-permute-start.11 = (bf16[4,1024,128]{2,1,0:T(8,128)(2,1)}, bf16[4,1024,128]{2,1,0:T(8,128)(2,1)}, u32[]{:S(2)}, u32[]{:S(2)}) collective-permute-start(bf16[4,1024,128]{2,1,0:T(8,128)(2,1)} %pad_maximum_fusion), channel_id=1, source_target_pairs={{0,1},{1,0},{2,3},{3,2},{4,5},{5,4},{6,7},{7,6},{8,9},{9,8},{10,11... | collective-permute-start | bytes 3145736 | tf_op jit(solution)/shard_map/ppermute | solution.py:46
  105.8 2.5 %add_convert_fusion = bf16[4,1024,128]{2,1,0:T(8,128)(2,1)} fusion(bf16[4,1024,128]{2,1,0:T(8,128)(2,1)} %collective-permute-done.11, bf16[1,1024,128]{2,1,0:T(8,128)(2,1)S(1)} %fusion.12, bf16[1,1024,128]{2,1,0:T(8,128)(2,1)S(1)} %fusion.11, bf16[1,1024,128]{2,1,0:T(8,128)(2,1)S(1)} %fusion.10, bf16[1,1024,128]{2,1,0:T(8,128)(2,1)S(1)} %fusion.9), kind=kLoop, calls=%fused_computation | loop fusion | flops 3670016 | bytes 3145728 | tf_op jit(solution)/shard_map/convert_element_type | solution.py:135
  108.3 4.6 %all-to-all-start.2 = ((bf16[4,1024,128]{2,1,0:T(8,128)(2,1)}), bf16[4,1024,128]{2,1,0:T(8,128)(2,1)}, u32[]{:S(2)}, u32[]{:S(2)}) async-start(bf16[4,1024,128]{2,1,0:T(8,128)(2,1)} %add_convert_fusion), calls=%async_computation.2 | async-start | bytes 2097152 | tf_op jit(solution)/shard_map/all_to_all | solution.py:36
  112.9 14.9 %all-to-all-done.2 = bf16[4,1024,128]{2,1,0:T(8,128)(2,1)} async-done(((bf16[4,1024,128]{2,1,0:T(8,128)(2,1)}), bf16[4,1024,128]{2,1,0:T(8,128)(2,1)}, u32[]{:S(2)}, u32[]{:S(2)}) %all-to-all-start.2) | async-done | bytes 1048608 | tf_op jit(solution)/shard_map/all_to_all | solution.py:36
  127.8 1.5 reduce_sum.39
  129.3 2.9 %collective-permute-start.16 = (bf16[8,64,128]{2,1,0:T(8,128)(2,1)S(1)}, bf16[8,64,128]{2,1,0:T(8,128)(2,1)S(1)}, u32[]{:S(2)}, u32[]{:S(2)}) collective-permute-start(bf16[8,64,128]{2,1,0:T(8,128)(2,1)S(1)} %dynamic-slice_bitcast_fusion.2), channel_id=1, source_target_pairs={{0,8},{8,0},{1,9},{9,1},{2,10},{10,2},{3,11},{11,3},{4,12},{12,4},... | collective-permute-start | bytes 393224 | tf_op jit(solution)/shard_map/ppermute | solution.py:46
  133.3 1.3 collective-permute-start.12
  134.6 1.3 collective-permute-start.13
  135.9 1.3 collective-permute-start.14
  138.6 26.9 %collective-permute-done.12 = bf16[128,128]{1,0:T(8,128)(2,1)S(1)} collective-permute-done((bf16[128,128]{1,0:T(8,128)(2,1)S(1)}, bf16[128,128]{1,0:T(8,128)(2,1)S(1)}, u32[]{:S(2)}, u32[]{:S(2)}) %collective-permute-start.12) | collective-permute-done | bytes 32800 | tf_op jit(solution)/shard_map/ppermute | solution.py:56
  165.5 8.7 %collective-permute-done.13 = bf16[128,128]{1,0:T(8,128)(2,1)S(1)} collective-permute-done((bf16[128,128]{1,0:T(8,128)(2,1)S(1)}, bf16[128,128]{1,0:T(8,128)(2,1)S(1)}, u32[]{:S(2)}, u32[]{:S(2)}) %collective-permute-start.13) | collective-permute-done | bytes 32800 | tf_op jit(solution)/shard_map/ppermute | solution.py:56
  177.5 3.9 %collective-permute-start.17 = (bf16[8,2,64,128]{3,2,1,0:T(8,128)(2,1)S(1)}, bf16[8,2,64,128]{3,2,1,0:T(8,128)(2,1)S(1)}, u32[]{:S(2)}, u32[]{:S(2)}) collective-permute-start(bf16[8,2,64,128]{3,2,1,0:T(8,128)(2,1)S(1)} %fusion.36), channel_id=1, source_target_pairs={{0,8},{8,0},{1,9},{9,1},{2,10},{10,2},{3,11},{11,3},{4,12},{12,4},... | collective-permute-start | bytes 786440 | tf_op jit(solution)/shard_map/ppermute | solution.py:46
  181.5 3.7 %collective-permute-done.17 = bf16[8,2,64,128]{3,2,1,0:T(8,128)(2,1)S(1)} collective-permute-done((bf16[8,2,64,128]{3,2,1,0:T(8,128)(2,1)S(1)}, bf16[8,2,64,128]{3,2,1,0:T(8,128)(2,1)S(1)}, u32[]{:S(2)}, u32[]{:S(2)}) %collective-permute-start.17) | collective-permute-done | bytes 262176 | tf_op jit(solution)/shard_map/ppermute | solution.py:46
  185.2 1.8 fusion.35
  187.0 15.7 %all-to-all-start.3 = ((bf16[8,2,64,128]{3,2,1,0:T(8,128)(2,1)}), bf16[8,2,64,128]{3,2,1,0:T(8,128)(2,1)}, u32[]{:S(2)}, u32[]{:S(2)}) async-start(bf16[8,2,64,128]{3,2,1,0:T(8,128)(2,1)} %fusion.35), calls=%async_computation.3 | async-start | bytes 524288 | tf_op jit(solution)/shard_map/all_to_all | solution.py:36
  204.2 2.0 fusion.79
  208.1 6.6 %all-to-all-done.3 = bf16[8,2,64,128]{3,2,1,0:T(8,128)(2,1)} async-done(((bf16[8,2,64,128]{3,2,1,0:T(8,128)(2,1)}), bf16[8,2,64,128]{3,2,1,0:T(8,128)(2,1)}, u32[]{:S(2)}, u32[]{:S(2)}) %all-to-all-start.3) | async-done | bytes 262176 | tf_op jit(solution)/shard_map/all_to_all | solution.py:36
  215.6 8.9 %collective-permute-start.18 = (bf16[8,64,128]{2,1,0:T(8,128)(2,1)S(1)}, bf16[8,64,128]{2,1,0:T(8,128)(2,1)S(1)}, u32[]{:S(2)}, u32[]{:S(2)}) collective-permute-start(bf16[8,64,128]{2,1,0:T(8,128)(2,1)S(1)} %dynamic-slice_bitcast_fusion.1), channel_id=1, source_target_pairs={{0,1},{1,0},{2,3},{3,2},{4,5},{5,4},{6,7},{7,6},{8,9},{9,8},{10,11... | collective-permute-start | bytes 393224 | tf_op jit(solution)/shard_map/ppermute | solution.py:46
  225.5 1.5 fusion.8
  (132 shorter events, 37.0 us)
Async XLA Ops:
  0.0 15.5 %copy-start.12 = (bf16[128,128]{1,0:T(8,128)(2,1)S(1)}, bf16[128,128]{1,0:T(8,128)(2,1)}, u32[]{:S(2)}) copy-start(bf16[128,128]{1,0:T(8,128)(2,1)} %param.11) | copy-start | bytes 98308
  0.0 42.7 %copy-start.8 = (f32[128,128]{1,0:T(8,128)S(1)}, f32[128,128]{1,0:T(8,128)}, u32[]{:S(2)}) copy-start(f32[128,128]{1,0:T(8,128)} %param.12) | copy-start | bytes 196612
  2.4 30.9 %all-to-all-start = ((bf16[16,64,128]{2,1,0:T(8,128)(2,1)}), bf16[16,64,128]{2,1,0:T(8,128)(2,1)S(1)}, u32[]{:S(2)}, u32[]{:S(2)}) async-start(bf16[16,64,128]{2,1,0:T(8,128)(2,1)} %copy.60), calls=%async_computation | async-start | bytes 524288 | tf_op jit(solution)/shard_map/all_to_all | solution.py:36
  15.5 17.8 %collective-permute-start = (bf16[128,128]{1,0:T(8,128)(2,1)S(1)}, bf16[128,128]{1,0:T(8,128)(2,1)S(1)}, u32[]{:S(2)}, u32[]{:S(2)}) collective-permute-start(bf16[128,128]{1,0:T(8,128)(2,1)S(1)} %copy-done.12), channel_id=1, source_target_pairs={{0,64},{16,80},{32,96},{48,112},{64,0},{80,16},{96,32},{112,48},{1... | collective-permute-start | bytes 98312 | tf_op jit(solution)/shard_map/ppermute | solution.py:46
  33.3 5.9 %collective-permute-start.1 = (bf16[2,128,128]{2,1,0:T(8,128)(2,1)S(1)}, bf16[2,128,128]{2,1,0:T(8,128)(2,1)S(1)}, u32[]{:S(2)}, u32[]{:S(2)}) collective-permute-start(bf16[2,128,128]{2,1,0:T(8,128)(2,1)S(1)} %pad_maximum_fusion.6), channel_id=1, source_target_pairs={{0,32},{16,48},{32,0},{48,16},{64,96},{80,112},{96,64},{112,80},{1... | collective-permute-start | bytes 196616 | tf_op jit(solution)/shard_map/ppermute | solution.py:46
  39.3 9.1 %collective-permute-start.2 = (bf16[2,2,128,128]{3,2,1,0:T(8,128)(2,1)S(1)}, bf16[2,2,128,128]{3,2,1,0:T(8,128)(2,1)}, u32[]{:S(2)}, u32[]{:S(2)}) collective-permute-start(bf16[2,2,128,128]{3,2,1,0:T(8,128)(2,1)S(1)} %pad_maximum_fusion.4), channel_id=1, source_target_pairs={{0,16},{16,0},{32,48},{48,32},{64,80},{80,64},{96,112},{112,96},{1... | collective-permute-start | bytes 393224 | tf_op jit(solution)/shard_map/ppermute | solution.py:46
  44.4 35.4 %all-to-all-start.1 = ((bf16[4,1024,128]{2,1,0:T(8,128)(2,1)}), bf16[4,1024,128]{2,1,0:T(8,128)(2,1)S(1)}, u32[]{:S(2)}, u32[]{:S(2)}) async-start(bf16[4,1024,128]{2,1,0:T(8,128)(2,1)} %broadcast_in_dim.29), calls=%async_computation.1 | async-start | bytes 2097152 | tf_op jit(solution)/shard_map/all_to_all | solution.py:36
  50.1 27.9 %collective-permute-start.3 = (bf16[2,2,2,128,128]{4,3,2,1,0:T(8,128)(2,1)}, bf16[2,2,2,128,128]{4,3,2,1,0:T(8,128)(2,1)}, u32[]{:S(2)}, u32[]{:S(2)}) collective-permute-start(bf16[2,2,2,128,128]{4,3,2,1,0:T(8,128)(2,1)} %pad_maximum_fusion.2), channel_id=1, source_target_pairs={{0,8},{8,0},{1,9},{9,1},{2,10},{10,2},{3,11},{11,3},{4,12},{12,4},... | collective-permute-start | bytes 786440 | tf_op jit(solution)/shard_map/ppermute | solution.py:46
  53.5 35.4 %collective-permute-start.10 = (bf16[128,128]{1,0:T(8,128)(2,1)}, bf16[128,128]{1,0:T(8,128)(2,1)}, u32[]{:S(2)}, u32[]{:S(2)}) collective-permute-start(bf16[128,128]{1,0:T(8,128)(2,1)} %convert_element_type.90), channel_id=1, source_target_pairs={{512,384},{640,0},{768,128},{896,256},{513,385},{641,1},{769,129},... | collective-permute-start | bytes 98312 | tf_op jit(solution)/shard_map/ppermute | solution.py:56
  69.4 19.5 %collective-permute-start.8 = (bf16[128,128]{1,0:T(8,128)(2,1)}, bf16[128,128]{1,0:T(8,128)(2,1)}, u32[]{:S(2)}, u32[]{:S(2)}) collective-permute-start(bf16[128,128]{1,0:T(8,128)(2,1)} %convert_element_type.90), channel_id=1, source_target_pairs={{512,128},{640,256},{768,384},{896,0},{513,129},{641,257},{769,385... | collective-permute-start | bytes 98312 | tf_op jit(solution)/shard_map/ppermute | solution.py:56
  71.3 17.7 %collective-permute-start.9 = (bf16[128,128]{1,0:T(8,128)(2,1)}, bf16[128,128]{1,0:T(8,128)(2,1)}, u32[]{:S(2)}, u32[]{:S(2)}) collective-permute-start(bf16[128,128]{1,0:T(8,128)(2,1)} %convert_element_type.90), channel_id=1, source_target_pairs={{512,256},{640,384},{768,0},{896,128},{513,257},{641,385},{769,1},... | collective-permute-start | bytes 98312 | tf_op jit(solution)/shard_map/ppermute | solution.py:56
  79.8 8.0 %collective-permute-start.4 = (bf16[4,1024,128]{2,1,0:T(8,128)(2,1)S(1)}, bf16[4,1024,128]{2,1,0:T(8,128)(2,1)S(1)}, u32[]{:S(2)}, u32[]{:S(2)}) collective-permute-start(bf16[4,1024,128]{2,1,0:T(8,128)(2,1)S(1)} %all-to-all-done.1), channel_id=1, source_target_pairs={{0,1},{1,0},{2,3},{3,2},{4,5},{5,4},{6,7},{7,6},{8,9},{9,8},{10,11... | collective-permute-start | bytes 3145736 | tf_op jit(solution)/shard_map/ppermute | solution.py:46
  87.8 6.3 %copy-start.2 = (bf16[4,1024,128]{2,1,0:T(8,128)(2,1)}, bf16[4,1024,128]{2,1,0:T(8,128)(2,1)S(1)}, u32[]{:S(2)}) copy-start(bf16[4,1024,128]{2,1,0:T(8,128)(2,1)S(1)} %collective-permute-done.4) | copy-start | bytes 3145732
  95.7 10.1 %collective-permute-start.11 = (bf16[4,1024,128]{2,1,0:T(8,128)(2,1)}, bf16[4,1024,128]{2,1,0:T(8,128)(2,1)}, u32[]{:S(2)}, u32[]{:S(2)}) collective-permute-start(bf16[4,1024,128]{2,1,0:T(8,128)(2,1)} %pad_maximum_fusion), channel_id=1, source_target_pairs={{0,1},{1,0},{2,3},{3,2},{4,5},{5,4},{6,7},{7,6},{8,9},{9,8},{10,11... | collective-permute-start | bytes 3145736 | tf_op jit(solution)/shard_map/ppermute | solution.py:46
  98.6 9.7 %collective-permute-start.5 = (bf16[128,128]{1,0:T(8,128)(2,1)S(1)}, bf16[128,128]{1,0:T(8,128)(2,1)S(1)}, u32[]{:S(2)}, u32[]{:S(2)}) collective-permute-start(bf16[128,128]{1,0:T(8,128)(2,1)S(1)} %get-tuple-element.53), channel_id=1, source_target_pairs={{0,256},{128,384},{256,0},{384,128},{1,257},{129,385},{257,1},{385... | collective-permute-start | bytes 98312 | tf_op jit(solution)/shard_map/ppermute | solution.py:56
  99.3 9.0 %collective-permute-start.6 = (bf16[128,128]{1,0:T(8,128)(2,1)S(1)}, bf16[128,128]{1,0:T(8,128)(2,1)}, u32[]{:S(2)}, u32[]{:S(2)}) collective-permute-start(bf16[128,128]{1,0:T(8,128)(2,1)S(1)} %get-tuple-element.52), channel_id=1, source_target_pairs={{0,128},{128,256},{256,384},{384,0},{1,129},{129,257},{257,385},{3... | collective-permute-start | bytes 98312 | tf_op jit(solution)/shard_map/ppermute | solution.py:56
  100.5 7.7 %collective-permute-start.7 = (bf16[128,128]{1,0:T(8,128)(2,1)S(1)}, bf16[128,128]{1,0:T(8,128)(2,1)}, u32[]{:S(2)}, u32[]{:S(2)}) collective-permute-start(bf16[128,128]{1,0:T(8,128)(2,1)S(1)} %get-tuple-element.51), channel_id=1, source_target_pairs={{0,384},{128,0},{256,128},{384,256},{1,385},{129,1},{257,129},{385... | collective-permute-start | bytes 98312 | tf_op jit(solution)/shard_map/ppermute | solution.py:56
  108.3 24.0 %copy-start.9 = (f32[128,128]{1,0:T(8,128)S(1)}, f32[128,128]{1,0:T(8,128)}, u32[]{:S(2)}) copy-start(f32[128,128]{1,0:T(8,128)} %param.12) | copy-start | bytes 196612
  108.3 24.0 %copy-start.10 = (bf16[128,128]{1,0:T(8,128)(2,1)S(1)}, bf16[128,128]{1,0:T(8,128)(2,1)}, u32[]{:S(2)}) copy-start(bf16[128,128]{1,0:T(8,128)(2,1)} %get-tuple-element.31) | copy-start | bytes 98308
  108.3 19.5 %all-to-all-start.2 = ((bf16[4,1024,128]{2,1,0:T(8,128)(2,1)}), bf16[4,1024,128]{2,1,0:T(8,128)(2,1)}, u32[]{:S(2)}, u32[]{:S(2)}) async-start(bf16[4,1024,128]{2,1,0:T(8,128)(2,1)} %add_convert_fusion), calls=%async_computation.2 | async-start | bytes 2097152 | tf_op jit(solution)/shard_map/all_to_all | solution.py:36
  129.3 45.8 %copy-start.3 = (bf16[4,1024,128]{2,1,0:T(8,128)(2,1)S(1)}, bf16[4,1024,128]{2,1,0:T(8,128)(2,1)}, u32[]{:S(2)}) copy-start(bf16[4,1024,128]{2,1,0:T(8,128)(2,1)} %copy-done.2) | copy-start | bytes 3145732
  129.3 9.2 %collective-permute-start.16 = (bf16[8,64,128]{2,1,0:T(8,128)(2,1)S(1)}, bf16[8,64,128]{2,1,0:T(8,128)(2,1)S(1)}, u32[]{:S(2)}, u32[]{:S(2)}) collective-permute-start(bf16[8,64,128]{2,1,0:T(8,128)(2,1)S(1)} %dynamic-slice_bitcast_fusion.2), channel_id=1, source_target_pairs={{0,8},{8,0},{1,9},{9,1},{2,10},{10,2},{3,11},{11,3},{4,12},{12,4},... | collective-permute-start | bytes 393224 | tf_op jit(solution)/shard_map/ppermute | solution.py:46
  133.3 32.2 %collective-permute-start.12 = (bf16[128,128]{1,0:T(8,128)(2,1)S(1)}, bf16[128,128]{1,0:T(8,128)(2,1)S(1)}, u32[]{:S(2)}, u32[]{:S(2)}) collective-permute-start(bf16[128,128]{1,0:T(8,128)(2,1)S(1)} %fusion.58), channel_id=1, source_target_pairs={{0,512},{128,640},{256,768},{384,896},{1,513},{129,641},{257,769},... | collective-permute-start | bytes 98312 | tf_op jit(solution)/shard_map/ppermute | solution.py:56
  134.6 39.6 %collective-permute-start.13 = (bf16[128,128]{1,0:T(8,128)(2,1)S(1)}, bf16[128,128]{1,0:T(8,128)(2,1)S(1)}, u32[]{:S(2)}, u32[]{:S(2)}) collective-permute-start(bf16[128,128]{1,0:T(8,128)(2,1)S(1)} %fusion.58), channel_id=1, source_target_pairs={{0,640},{128,768},{256,896},{384,512},{1,641},{129,769},{257,897},... | collective-permute-start | bytes 98312 | tf_op jit(solution)/shard_map/ppermute | solution.py:56
  135.9 39.1 %collective-permute-start.14 = (bf16[128,128]{1,0:T(8,128)(2,1)S(1)}, bf16[128,128]{1,0:T(8,128)(2,1)S(1)}, u32[]{:S(2)}, u32[]{:S(2)}) collective-permute-start(bf16[128,128]{1,0:T(8,128)(2,1)S(1)} %fusion.58), channel_id=1, source_target_pairs={{0,768},{128,896},{256,512},{384,640},{1,769},{129,897},{257,513},... | collective-permute-start | bytes 98312 | tf_op jit(solution)/shard_map/ppermute | solution.py:56
  137.2 37.8 %collective-permute-start.15 = (bf16[128,128]{1,0:T(8,128)(2,1)S(1)}, bf16[128,128]{1,0:T(8,128)(2,1)S(1)}, u32[]{:S(2)}, u32[]{:S(2)}) collective-permute-start(bf16[128,128]{1,0:T(8,128)(2,1)S(1)} %fusion.58), channel_id=1, source_target_pairs={{0,896},{128,512},{256,640},{384,768},{1,897},{129,513},{257,641},... | collective-permute-start | bytes 98312 | tf_op jit(solution)/shard_map/ppermute | solution.py:56
  177.4 25.3 %copy-start.13 = (s32[16]{0:T(128)S(1)}, s32[16]{0:T(128)}, u32[]{:S(2)}) copy-start(s32[16]{0:T(128)} %param.19) | copy-start | bytes 196
  177.5 25.4 %copy-start.11 = (bf16[8,16,128]{2,1,0:T(8,128)(2,1)S(1)}, bf16[8,16,128]{2,1,0:T(8,128)(2,1)}, u32[]{:S(2)}) copy-start(bf16[8,16,128]{2,1,0:T(8,128)(2,1)} %param.16) | copy-start | bytes 98308
  177.5 7.7 %collective-permute-start.17 = (bf16[8,2,64,128]{3,2,1,0:T(8,128)(2,1)S(1)}, bf16[8,2,64,128]{3,2,1,0:T(8,128)(2,1)S(1)}, u32[]{:S(2)}, u32[]{:S(2)}) collective-permute-start(bf16[8,2,64,128]{3,2,1,0:T(8,128)(2,1)S(1)} %fusion.36), channel_id=1, source_target_pairs={{0,8},{8,0},{1,9},{9,1},{2,10},{10,2},{3,11},{11,3},{4,12},{12,4},... | collective-permute-start | bytes 786440 | tf_op jit(solution)/shard_map/ppermute | solution.py:46
  185.2 17.5 %copy-start.7 = (bf16[8,16,1024]{2,1,0:T(8,128)(2,1)S(1)}, bf16[8,16,1024]{2,1,0:T(8,128)(2,1)}, u32[]{:S(2)}) copy-start(bf16[8,16,1024]{2,1,0:T(8,128)(2,1)} %param.15) | copy-start | bytes 786436
  187.0 27.7 %all-to-all-start.3 = ((bf16[8,2,64,128]{3,2,1,0:T(8,128)(2,1)}), bf16[8,2,64,128]{3,2,1,0:T(8,128)(2,1)}, u32[]{:S(2)}, u32[]{:S(2)}) async-start(bf16[8,2,64,128]{3,2,1,0:T(8,128)(2,1)} %fusion.35), calls=%async_computation.3 | async-start | bytes 524288 | tf_op jit(solution)/shard_map/all_to_all | solution.py:36
  215.6 11.8 %collective-permute-start.18 = (bf16[8,64,128]{2,1,0:T(8,128)(2,1)S(1)}, bf16[8,64,128]{2,1,0:T(8,128)(2,1)S(1)}, u32[]{:S(2)}, u32[]{:S(2)}) collective-permute-start(bf16[8,64,128]{2,1,0:T(8,128)(2,1)S(1)} %dynamic-slice_bitcast_fusion.1), channel_id=1, source_target_pairs={{0,1},{1,0},{2,3},{3,2},{4,5},{5,4},{6,7},{7,6},{8,9},{9,8},{10,11... | collective-permute-start | bytes 393224 | tf_op jit(solution)/shard_map/ppermute | solution.py:46
  (6 other events, 10.3 us)

commit v5 on v4

--- a/solution.py
+++ b/solution.py
@@ -1,6 +1,8 @@
 import jax
 import jax.numpy as jnp
 from jax import lax
+from jax.experimental import pallas as pl
+from jax.experimental.pallas import tpu as pltpu
 from jax.sharding import Mesh, PartitionSpec as P
 
 
@@ -19,6 +21,8 @@
 neg_fill = -1e30
 
 
+INTERPRET = False
+
 DP = ("zh", "zl", "yl")
 TP = ("x", "core")
 NEAR = ("zl", "yl")
@@ -72,6 +76,26 @@
 
 def dot32(a, b, dims):
     return lax.dot_general(a, b, (dims, ((), ())), preferred_element_type=jnp.float32)
+
+
+def value_terms(at_ref, mine_ref, other_ref, *refs):
+    parts, (stays_ref, leaves_ref) = refs[:-2], refs[-2:]
+    far = len(parts)
+    zh_at, first = at_ref[0], at_ref[1] == 0
+    line, _, half, width = stays_ref.shape
+    step = max(line // 2, 1)
+    for slot, rows_ref in enumerate((mine_ref, other_ref)):
+        for begin in range(0, line, step):
+            rows = pl.ds(begin * 2 * half, step * 2 * half)
+            total = None
+            for k, part in enumerate(parts):
+                f = lax.rem(zh_at - k + far, far)
+                term = jnp.dot(rows_ref[f, rows, :], part[...], preferred_element_type=jnp.float32)
+                total = term if total is None else total + term
+            total = total.reshape(step, 2, half, width)
+            low, high = total[:, 0], total[:, 1]
+            stays_ref[pl.ds(begin, step), slot] = jnp.where(first, low, high)
+            leaves_ref[pl.ds(begin, step), slot] = jnp.where(first, high, low).astype(jnp.bfloat16)
 
 
 def local(
@@ -93,13 +117,15 @@
     mine = lax.dynamic_slice(hidden[0], (core_at * half, x_at * near * block), (half, near * block))
     mine = mine.reshape(half, near, block).transpose(1, 0, 2)
     mine = exchange(mine, NEAR)
+    mine, old_weight = lax.optimization_barrier((mine, master.astype(jnp.bfloat16)))
+    mine = gather(mine.reshape(near * half, block), "x")
+    other = swap(mine, "core")
 
     by, grads, at = line // 2, out_grad, 0
     while by:
         first = lax.axis_index("zl") & by == 0
-        grads = jnp.stack(ordered(grads, swap(grads, "zl", by), first), axis=at)
-        if at == 0:
-            grads, mine = lax.optimization_barrier((grads, mine))
+        met = swap(grads, "zl", by)
+        grads = jnp.stack(ordered(grads, met, first), axis=at)
         by, at = by // 2, at + 1
     grads = jnp.stack(ordered(grads, swap(grads, "yl"), yl_at == 0), axis=at)
     grads = grads.reshape(near, tokens, width_here)
@@ -108,10 +134,6 @@
         for at in (core_at, 1 - core_at)
     )
 
-    mine, old_weight = lax.optimization_barrier((mine, master.astype(jnp.bfloat16)))
-    mine = gather(mine.reshape(near * half, block), "x")
-    other = swap(mine, "core")
-
     old_parts = {k: far_shift(old_weight, k, 1, 0) for k in far_order(far)[:-1]}
     old_parts[0] = old_weight
 
@@ -121,10 +143,7 @@
             for f in range(far)
         ]
     ).astype(jnp.bfloat16)
-    gradient = [at_index(partial, zh_at)] + [
-        far_shift(at_index(partial, (zh_at + k) % far), k, 0, 0)
-        for k in far_order(far)[:-1]
-    ]
+    gradient = exchange(partial, "zh")
 
     _, *old_parts = lax.optimization_barrier((partial, *(old_parts[k] for k in range(far))))
     old_weight = by_source(old_parts)
@@ -135,26 +154,43 @@
     back = (kept.astype(jnp.float32) + swap(sent, "core").astype(jnp.float32)).astype(jnp.bfloat16)
     gradient, back = lax.optimization_barrier((gradient, back))
 
-    fresh = adam_fresh(master, moment1, moment2, sum(g.astype(jnp.float32) for g in gradient))
+    fresh = adam_fresh(master, moment1, moment2, jnp.sum(gradient.astype(jnp.float32), axis=0))
     parts = {k: far_shift(fresh, k, 0, 1) for k in far_order(far)}
     parts = [parts[k] for k in range(far)]
 
     back = exchange(back, "x")
     back = jnp.sum(back.astype(jnp.float32), axis=0).astype(jnp.bfloat16)
     back = back.reshape(line, 2, half, block)
-    stays = lax.dynamic_index_in_dim(back, yl_at, 1, keepdims=False)
-    leaves = lax.dynamic_index_in_dim(back, 1 - yl_at, 1, keepdims=False)
-    back = jnp.stack(ordered(stays, swap(leaves, "yl"), yl_at == 0), axis=1)
 
     parts, back = lax.optimization_barrier((parts, back))
-    weight = by_source(parts)
-    terms = [sum(dot32(rows[f], weight[f], ((1,), (0,))) for f in range(far)) for rows in (mine, other)]
-    terms = jnp.stack([rows.reshape(line, 2, half, width_here) for rows in terms], axis=2)
-    stays = lax.dynamic_index_in_dim(terms, yl_at, 1, keepdims=False)
-    leaves = lax.dynamic_index_in_dim(terms, 1 - yl_at, 1, keepdims=False)
-    terms = stays + swap(leaves.astype(jnp.bfloat16), "yl").astype(jnp.float32)
-
-    moved = exchange(jnp.where(is_learner, back, terms.astype(jnp.bfloat16)), "zl")
+    shape = (line, 2, half, width_here)
+    stays, leaves = pl.pallas_call(
+        value_terms,
+        out_shape=(
+            jax.ShapeDtypeStruct(shape, jnp.float32),
+            jax.ShapeDtypeStruct(shape, jnp.bfloat16),
+        ),
+        in_specs=[pl.BlockSpec(memory_space=pltpu.SMEM)]
+        + [pl.BlockSpec(memory_space=pltpu.VMEM)] * (2 + far),
+        out_specs=[pl.BlockSpec(memory_space=pltpu.VMEM)] * 2,
+        cost_estimate=pl.CostEstimate(
+            flops=4 * far * near * half * block * width_here,
+            bytes_accessed=4 * far * near * half * block,
+            transcendentals=0,
+        ),
+        interpret=INTERPRET,
+    )(jnp.stack([zh_at, yl_at]), mine, other, *parts)
+    met = swap(jnp.where(is_learner, back, leaves), "yl")
+    back = jnp.stack(
+        ordered(
+            lax.dynamic_index_in_dim(back, yl_at, 1, keepdims=False),
+            lax.dynamic_index_in_dim(met, yl_at, 1, keepdims=False),
+            yl_at == 0,
+        ),
+        axis=1,
+    )
+    terms = (stays + met.astype(jnp.float32)).astype(jnp.bfloat16)
+    moved = exchange(jnp.where(is_learner, back, terms), "zl")
     values = jnp.sum(moved.astype(jnp.float32), axis=0)
     values = jnp.concatenate(ordered(values[0], values[1], core_at == 0))
     back = moved.reshape(2, near // 2, half, block)

time: 232 us -> 217 us (0.935)
  the two profiles are of different devices: /device:TPU:17 before, /device:TPU:19 now
where the time goes in v5:
time: 217 us; the launch traced here: 215 us
  starting transfers between devices  104 us (48%)
  waiting for transfers between devices  75.2 us (35%)
  matrix products  12.8 us (6%)
  other arithmetic  12.6 us (6%)
  local copies, waits for them, and re-layouts  6.75 us (3%)
  Pallas kernels  3.13 us (1%)
    ppermute x8, starting transfers between devices, swap(): return lax.ppermute(value, axis, [(i, i ^ by) for i in range(peers)])  38.4 us
    all_to_all x5, starting transfers between devices, exchange(): return lax.all_to_all(value, axis, 0, 0, tiled=True)  36.8 us
    ppermute x7, starting transfers between devices, far_shift(): return lax.ppermute(value, ('role', 'zh'), pairs)  29 us
    all_to_all x5, waiting for transfers between devices, exchange(): return lax.all_to_all(value, axis, 0, 0, tiled=True)  28.7 us
    ppermute x7, waiting for transfers between devices, far_shift(): return lax.ppermute(value, ('role', 'zh'), pairs)  23.9 us
    ppermute x8, waiting for transfers between devices, swap(): return lax.ppermute(value, axis, [(i, i ^ by) for i in range(peers)])  22.5 us
    dot_general x16, matrix products, dot32(): lax.dot_general(a, b, (dims, ((), ())), preferred_element_type=jnp.float32)  7.02 us
  transfers between devices with their start and end apart: 20, of which 12 were waited for; matrix products, arithmetic and copies ran while one was open for 11% of the time, Pallas kernels for 0%

profile of v5, /device:TPU:19, one launch (start us, length us, event | category | flops | bytes accessed | tf_op | source)
XLA Modules:
  0.0 215.4 jit_solution(5224827278790539925)
XLA Ops:
  0.0 1.6 copy-done
  2.4 13.1 %all-to-all-start = ((bf16[16,64,128]{2,1,0:T(8,128)(2,1)}), bf16[16,64,128]{2,1,0:T(8,128)(2,1)S(1)}, u32[]{:S(2)}, u32[]{:S(2)}) async-start(bf16[16,64,128]{2,1,0:T(8,128)(2,1)} %copy.37), calls=%async_computation | async-start | bytes 524288 | tf_op jit(solution)/shard_map/all_to_all | solution.py:40
  15.5 7.2 %collective-permute-start = (bf16[128,128]{1,0:T(8,128)(2,1)S(1)}, bf16[128,128]{1,0:T(8,128)(2,1)S(1)}, u32[]{:S(2)}, u32[]{:S(2)}) collective-permute-start(bf16[128,128]{1,0:T(8,128)(2,1)S(1)} %copy-done.15), channel_id=1, source_target_pairs={{0,64},{16,80},{32,96},{48,112},{64,0},{80,16},{96,32},{112,48},{1... | collective-permute-start | bytes 98312 | tf_op jit(solution)/shard_map/ppermute | solution.py:50
  22.7 10.6 %collective-permute-done = bf16[128,128]{1,0:T(8,128)(2,1)S(1)} collective-permute-done((bf16[128,128]{1,0:T(8,128)(2,1)S(1)}, bf16[128,128]{1,0:T(8,128)(2,1)S(1)}, u32[]{:S(2)}, u32[]{:S(2)}) %collective-permute-start) | collective-permute-done | bytes 32800 | tf_op jit(solution)/shard_map/ppermute | solution.py:50
  33.3 1.9 collective-permute-start.1
  35.3 4.0 %collective-permute-done.1 = bf16[2,128,128]{2,1,0:T(8,128)(2,1)S(1)} collective-permute-done((bf16[2,128,128]{2,1,0:T(8,128)(2,1)S(1)}, bf16[2,128,128]{2,1,0:T(8,128)(2,1)S(1)}, u32[]{:S(2)}, u32[]{:S(2)}) %collective-permute-start.1) | collective-permute-done | bytes 65568 | tf_op jit(solution)/shard_map/ppermute | solution.py:50
  39.3 3.4 %collective-permute-start.2 = (bf16[2,2,128,128]{3,2,1,0:T(8,128)(2,1)S(1)}, bf16[2,2,128,128]{3,2,1,0:T(8,128)(2,1)}, u32[]{:S(2)}, u32[]{:S(2)}) collective-permute-start(bf16[2,2,128,128]{3,2,1,0:T(8,128)(2,1)S(1)} %pad_maximum_fusion.3), channel_id=1, source_target_pairs={{0,16},{16,0},{32,48},{48,32},{64,80},{80,64},{96,112},{112,96},{1... | collective-permute-start | bytes 393224 | tf_op jit(solution)/shard_map/ppermute | solution.py:50
  44.4 4.3 %all-to-all-start.1 = ((bf16[4,1024,128]{2,1,0:T(8,128)(2,1)}), bf16[4,1024,128]{2,1,0:T(8,128)(2,1)S(1)}, u32[]{:S(2)}, u32[]{:S(2)}) async-start(bf16[4,1024,128]{2,1,0:T(8,128)(2,1)} %broadcast_in_dim.29), calls=%async_computation.1 | async-start | bytes 2097152 | tf_op jit(solution)/shard_map/all_to_all | solution.py:40
  50.3 3.4 %collective-permute-start.3 = (bf16[2,2,2,128,128]{4,3,2,1,0:T(8,128)(2,1)}, bf16[2,2,2,128,128]{4,3,2,1,0:T(8,128)(2,1)}, u32[]{:S(2)}, u32[]{:S(2)}) collective-permute-start(bf16[2,2,2,128,128]{4,3,2,1,0:T(8,128)(2,1)} %pad_maximum_fusion.2), channel_id=1, source_target_pairs={{0,8},{8,0},{1,9},{9,1},{2,10},{10,2},{3,11},{11,3},{4,12},{12,4},... | collective-permute-start | bytes 786440 | tf_op jit(solution)/shard_map/ppermute | solution.py:50
  53.7 4.2 %collective-permute-done.3 = bf16[2,2,2,128,128]{4,3,2,1,0:T(8,128)(2,1)} collective-permute-done((bf16[2,2,2,128,128]{4,3,2,1,0:T(8,128)(2,1)}, bf16[2,2,2,128,128]{4,3,2,1,0:T(8,128)(2,1)}, u32[]{:S(2)}, u32[]{:S(2)}) %collective-permute-start.3) | collective-permute-done | bytes 262176 | tf_op jit(solution)/shard_map/ppermute | solution.py:50
  59.8 6.7 %collective-permute-start.4 = (bf16[4,1024,128]{2,1,0:T(8,128)(2,1)S(1)}, bf16[4,1024,128]{2,1,0:T(8,128)(2,1)S(1)}, u32[]{:S(2)}, u32[]{:S(2)}) collective-permute-start(bf16[4,1024,128]{2,1,0:T(8,128)(2,1)S(1)} %all-to-all-done.1.mine_ref), channel_id=1, source_target_pairs={{0,1},{1,0},{2,3},{3,2},{4,5},{5,4},{6,7},{7,6},{8,9},{9,8},{10,11... | collective-permute-start | bytes 3145736 | tf_op jit(solution)/shard_map/ppermute | solution.py:50
  67.6 15.5 %collective-permute-start.5 = (bf16[128,128]{1,0:T(8,128)(2,1)}, bf16[128,128]{1,0:T(8,128)(2,1)S(1)}, u32[]{:S(2)}, u32[]{:S(2)}) collective-permute-start(bf16[128,128]{1,0:T(8,128)(2,1)} %convert_element_type.75), channel_id=1, source_target_pairs={{512,128},{640,256},{768,384},{896,0},{513,129},{641,257},{769,385... | collective-permute-start | bytes 98312 | tf_op jit(solution)/shard_map/ppermute | solution.py:60
  83.1 7.0 %collective-permute-start.6 = (bf16[128,128]{1,0:T(8,128)(2,1)}, bf16[128,128]{1,0:T(8,128)(2,1)S(1)}, u32[]{:S(2)}, u32[]{:S(2)}) collective-permute-start(bf16[128,128]{1,0:T(8,128)(2,1)} %convert_element_type.75), channel_id=1, source_target_pairs={{512,256},{640,384},{768,0},{896,128},{513,257},{641,385},{769,1},... | collective-permute-start | bytes 98312 | tf_op jit(solution)/shard_map/ppermute | solution.py:60
  94.6 6.9 %collective-permute-done.7 = bf16[128,128]{1,0:T(8,128)(2,1)S(1)} collective-permute-done((bf16[128,128]{1,0:T(8,128)(2,1)}, bf16[128,128]{1,0:T(8,128)(2,1)S(1)}, u32[]{:S(2)}, u32[]{:S(2)}) %collective-permute-start.7) | collective-permute-done | bytes 32800 | tf_op jit(solution)/shard_map/ppermute | solution.py:60
  103.7 2.9 %collective-permute-start.8 = (bf16[4,1024,128]{2,1,0:T(8,128)(2,1)}, bf16[4,1024,128]{2,1,0:T(8,128)(2,1)S(1)}, u32[]{:S(2)}, u32[]{:S(2)}) collective-permute-start(bf16[4,1024,128]{2,1,0:T(8,128)(2,1)} %pad_maximum_fusion), channel_id=1, source_target_pairs={{0,1},{1,0},{2,3},{3,2},{4,5},{5,4},{6,7},{7,6},{8,9},{9,8},{10,11... | collective-permute-start | bytes 3145736 | tf_op jit(solution)/shard_map/ppermute | solution.py:50
  106.6 5.5 %all-to-all-start.2 = ((bf16[4,128,128]{2,1,0:T(8,128)(2,1)}), bf16[4,128,128]{2,1,0:T(8,128)(2,1)S(1)}, u32[]{:S(2)}, u32[]{:S(2)}) async-start(bf16[4,128,128]{2,1,0:T(8,128)(2,1)} %pad_maximum_fusion.4), calls=%async_computation.2 | async-start | bytes 262144 | tf_op jit(solution)/shard_map/all_to_all | solution.py:40
  117.4 16.5 %all-to-all-done.2 = bf16[4,128,128]{2,1,0:T(8,128)(2,1)S(1)} async-done(((bf16[4,128,128]{2,1,0:T(8,128)(2,1)}), bf16[4,128,128]{2,1,0:T(8,128)(2,1)S(1)}, u32[]{:S(2)}, u32[]{:S(2)}) %all-to-all-start.2) | async-done | bytes 131104 | tf_op jit(solution)/shard_map/all_to_all | solution.py:40
  133.9 4.4 %all-to-all-start.3 = ((bf16[4,1024,128]{2,1,0:T(8,128)(2,1)}), bf16[4,1024,128]{2,1,0:T(8,128)(2,1)S(1)}, u32[]{:S(2)}, u32[]{:S(2)}) async-start(bf16[4,1024,128]{2,1,0:T(8,128)(2,1)} %add_convert_fusion), calls=%async_computation.3 | async-start | bytes 2097152 | tf_op jit(solution)/shard_map/all_to_all | solution.py:40
  140.3 1.3 collective-permute-start.11
  141.6 1.3 collective-permute-start.12
  144.9 5.6 %all-to-all-done.3 = bf16[4,1024,128]{2,1,0:T(8,128)(2,1)S(1)} async-done(((bf16[4,1024,128]{2,1,0:T(8,128)(2,1)}), bf16[4,1024,128]{2,1,0:T(8,128)(2,1)S(1)}, u32[]{:S(2)}, u32[]{:S(2)}) %all-to-all-start.3) | async-done | bytes 1048608 | tf_op jit(solution)/shard_map/all_to_all | solution.py:40
  150.8 5.0 %collective-permute-done.10.refs_1_ = bf16[128,128]{1,0:T(8,128)(2,1)S(1)} collective-permute-done((bf16[128,128]{1,0:T(8,128)(2,1)}, bf16[128,128]{1,0:T(8,128)(2,1)S(1)}, u32[]{:S(2)}, u32[]{:S(2)}) %collective-permute-start.10) | collective-permute-done | bytes 32800 | tf_op jit(solution)/shard_map/ppermute | solution.py:60
  155.7 11.5 %collective-permute-done.11.refs_2_ = bf16[128,128]{1,0:T(8,128)(2,1)S(1)} collective-permute-done((bf16[128,128]{1,0:T(8,128)(2,1)}, bf16[128,128]{1,0:T(8,128)(2,1)S(1)}, u32[]{:S(2)}, u32[]{:S(2)}) %collective-permute-start.11) | collective-permute-done | bytes 32800 | tf_op jit(solution)/shard_map/ppermute | solution.py:60
  168.2 3.1 %shard_map.100 = (f32[8,2,64,128]{3,2,1,0:T(8,128)}, bf16[8,2,64,128]{3,2,1,0:T(8,128)(2,1)}) custom-call(s32[2]{0:T(128)} %pad_add_fusion.at_ref, bf16[4,1024,128]{2,1,0:T(8,128)(2,1)} %copy-done.1, bf16[4,1024,128]{2,1,0:T(8,128)(2,1)} %copy-done.2, bf16[128,128]{1,0:T(8,128)(2,1)} %copy-done.13, bf16[128,128]{1,0:T(8,128)(2,1)} %copy-done.10, ...), custom_call_target="tpu_custom_call" | custom-call | flops 268435456 | bytes 2097152 | tf_op jit(solution)/shard_map/pallas_call | solution.py:167
  172.3 3.9 %collective-permute-start.13 = (bf16[8,2,64,128]{3,2,1,0:T(8,128)(2,1)S(1)}, bf16[8,2,64,128]{3,2,1,0:T(8,128)(2,1)S(1)}, u32[]{:S(2)}, u32[]{:S(2)}) collective-permute-start(bf16[8,2,64,128]{3,2,1,0:T(8,128)(2,1)S(1)} %broadcast_select_fusion), channel_id=1, source_target_pairs={{0,8},{8,0},{1,9},{9,1},{2,10},{10,2},{3,11},{11,3},{4,12},{12,4},... | collective-permute-start | bytes 786440 | tf_op jit(solution)/shard_map/ppermute | solution.py:50
  176.3 3.7 %collective-permute-done.13 = bf16[8,2,64,128]{3,2,1,0:T(8,128)(2,1)S(1)} collective-permute-done((bf16[8,2,64,128]{3,2,1,0:T(8,128)(2,1)S(1)}, bf16[8,2,64,128]{3,2,1,0:T(8,128)(2,1)S(1)}, u32[]{:S(2)}, u32[]{:S(2)}) %collective-permute-start.13) | collective-permute-done | bytes 262176 | tf_op jit(solution)/shard_map/ppermute | solution.py:50
  180.1 1.9 fusion.29
  181.9 9.6 %all-to-all-start.4 = ((bf16[8,2,64,128]{3,2,1,0:T(8,128)(2,1)}), bf16[8,2,64,128]{3,2,1,0:T(8,128)(2,1)S(1)}, u32[]{:S(2)}, u32[]{:S(2)}) async-start(bf16[8,2,64,128]{3,2,1,0:T(8,128)(2,1)} %fusion.29), calls=%async_computation.4 | async-start | bytes 524288 | tf_op jit(solution)/shard_map/all_to_all | solution.py:40
  192.9 1.9 fusion.58
  196.8 6.6 %all-to-all-done.4 = bf16[8,2,64,128]{3,2,1,0:T(8,128)(2,1)S(1)} async-done(((bf16[8,2,64,128]{3,2,1,0:T(8,128)(2,1)}), bf16[8,2,64,128]{3,2,1,0:T(8,128)(2,1)S(1)}, u32[]{:S(2)}, u32[]{:S(2)}) %all-to-all-start.4) | async-done | bytes 262176 | tf_op jit(solution)/shard_map/all_to_all | solution.py:40
  203.4 9.0 %collective-permute-start.14 = (bf16[8,64,128]{2,1,0:T(8,128)(2,1)S(1)}, bf16[8,64,128]{2,1,0:T(8,128)(2,1)S(1)}, u32[]{:S(2)}, u32[]{:S(2)}) collective-permute-start(bf16[8,64,128]{2,1,0:T(8,128)(2,1)S(1)} %dynamic-slice_bitcast_fusion.1), channel_id=1, source_target_pairs={{0,1},{1,0},{2,3},{3,2},{4,5},{5,4},{6,7},{7,6},{8,9},{9,8},{10,11... | collective-permute-start | bytes 393224 | tf_op jit(solution)/shard_map/ppermute | solution.py:50
  212.5 1.4 fusion.6
  (116 shorter events, 30.0 us)
Async XLA Ops:
  0.0 15.5 %copy-start.15 = (bf16[128,128]{1,0:T(8,128)(2,1)S(1)}, bf16[128,128]{1,0:T(8,128)(2,1)}, u32[]{:S(2)}) copy-start(bf16[128,128]{1,0:T(8,128)(2,1)} %param.11) | copy-start | bytes 98308
  0.0 42.7 %copy-start.6 = (f32[128,128]{1,0:T(8,128)S(1)}, f32[128,128]{1,0:T(8,128)}, u32[]{:S(2)}) copy-start(f32[128,128]{1,0:T(8,128)} %param.12) | copy-start | bytes 196612
  2.4 40.9 %all-to-all-start = ((bf16[16,64,128]{2,1,0:T(8,128)(2,1)}), bf16[16,64,128]{2,1,0:T(8,128)(2,1)S(1)}, u32[]{:S(2)}, u32[]{:S(2)}) async-start(bf16[16,64,128]{2,1,0:T(8,128)(2,1)} %copy.37), calls=%async_computation | async-start | bytes 524288 | tf_op jit(solution)/shard_map/all_to_all | solution.py:40
  15.5 17.8 %collective-permute-start = (bf16[128,128]{1,0:T(8,128)(2,1)S(1)}, bf16[128,128]{1,0:T(8,128)(2,1)S(1)}, u32[]{:S(2)}, u32[]{:S(2)}) collective-permute-start(bf16[128,128]{1,0:T(8,128)(2,1)S(1)} %copy-done.15), channel_id=1, source_target_pairs={{0,64},{16,80},{32,96},{48,112},{64,0},{80,16},{96,32},{112,48},{1... | collective-permute-start | bytes 98312 | tf_op jit(solution)/shard_map/ppermute | solution.py:50
  33.3 5.9 %collective-permute-start.1 = (bf16[2,128,128]{2,1,0:T(8,128)(2,1)S(1)}, bf16[2,128,128]{2,1,0:T(8,128)(2,1)S(1)}, u32[]{:S(2)}, u32[]{:S(2)}) collective-permute-start(bf16[2,128,128]{2,1,0:T(8,128)(2,1)S(1)} %pad_maximum_fusion.5), channel_id=1, source_target_pairs={{0,32},{16,48},{32,0},{48,16},{64,96},{80,112},{96,64},{112,80},{1... | collective-permute-start | bytes 196616 | tf_op jit(solution)/shard_map/ppermute | solution.py:50
  39.3 9.4 %collective-permute-start.2 = (bf16[2,2,128,128]{3,2,1,0:T(8,128)(2,1)S(1)}, bf16[2,2,128,128]{3,2,1,0:T(8,128)(2,1)}, u32[]{:S(2)}, u32[]{:S(2)}) collective-permute-start(bf16[2,2,128,128]{3,2,1,0:T(8,128)(2,1)S(1)} %pad_maximum_fusion.3), channel_id=1, source_target_pairs={{0,16},{16,0},{32,48},{48,32},{64,80},{80,64},{96,112},{112,96},{1... | collective-permute-start | bytes 393224 | tf_op jit(solution)/shard_map/ppermute | solution.py:50
  44.4 15.4 %all-to-all-start.1 = ((bf16[4,1024,128]{2,1,0:T(8,128)(2,1)}), bf16[4,1024,128]{2,1,0:T(8,128)(2,1)S(1)}, u32[]{:S(2)}, u32[]{:S(2)}) async-start(bf16[4,1024,128]{2,1,0:T(8,128)(2,1)} %broadcast_in_dim.29), calls=%async_computation.1 | async-start | bytes 2097152 | tf_op jit(solution)/shard_map/all_to_all | solution.py:40
  50.3 7.6 %collective-permute-start.3 = (bf16[2,2,2,128,128]{4,3,2,1,0:T(8,128)(2,1)}, bf16[2,2,2,128,128]{4,3,2,1,0:T(8,128)(2,1)}, u32[]{:S(2)}, u32[]{:S(2)}) collective-permute-start(bf16[2,2,2,128,128]{4,3,2,1,0:T(8,128)(2,1)} %pad_maximum_fusion.2), channel_id=1, source_target_pairs={{0,8},{8,0},{1,9},{9,1},{2,10},{10,2},{3,11},{11,3},{4,12},{12,4},... | collective-permute-start | bytes 786440 | tf_op jit(solution)/shard_map/ppermute | solution.py:50
  59.8 33.3 %copy-start.1 = (bf16[4,1024,128]{2,1,0:T(8,128)(2,1)}, bf16[4,1024,128]{2,1,0:T(8,128)(2,1)S(1)}, u32[]{:S(2)}) copy-start(bf16[4,1024,128]{2,1,0:T(8,128)(2,1)S(1)} %all-to-all-done.1.mine_ref) | copy-start | bytes 3145732
  59.8 32.7 %collective-permute-start.4 = (bf16[4,1024,128]{2,1,0:T(8,128)(2,1)S(1)}, bf16[4,1024,128]{2,1,0:T(8,128)(2,1)S(1)}, u32[]{:S(2)}, u32[]{:S(2)}) collective-permute-start(bf16[4,1024,128]{2,1,0:T(8,128)(2,1)S(1)} %all-to-all-done.1.mine_ref), channel_id=1, source_target_pairs={{0,1},{1,0},{2,3},{3,2},{4,5},{5,4},{6,7},{7,6},{8,9},{9,8},{10,11... | collective-permute-start | bytes 3145736 | tf_op jit(solution)/shard_map/ppermute | solution.py:50
  67.6 26.8 %collective-permute-start.5 = (bf16[128,128]{1,0:T(8,128)(2,1)}, bf16[128,128]{1,0:T(8,128)(2,1)S(1)}, u32[]{:S(2)}, u32[]{:S(2)}) collective-permute-start(bf16[128,128]{1,0:T(8,128)(2,1)} %convert_element_type.75), channel_id=1, source_target_pairs={{512,128},{640,256},{768,384},{896,0},{513,129},{641,257},{769,385... | collective-permute-start | bytes 98312 | tf_op jit(solution)/shard_map/ppermute | solution.py:60
  83.1 11.6 %collective-permute-start.6 = (bf16[128,128]{1,0:T(8,128)(2,1)}, bf16[128,128]{1,0:T(8,128)(2,1)S(1)}, u32[]{:S(2)}, u32[]{:S(2)}) collective-permute-start(bf16[128,128]{1,0:T(8,128)(2,1)} %convert_element_type.75), channel_id=1, source_target_pairs={{512,256},{640,384},{768,0},{896,128},{513,257},{641,385},{769,1},... | collective-permute-start | bytes 98312 | tf_op jit(solution)/shard_map/ppermute | solution.py:60
  90.1 11.4 %collective-permute-start.7 = (bf16[128,128]{1,0:T(8,128)(2,1)}, bf16[128,128]{1,0:T(8,128)(2,1)S(1)}, u32[]{:S(2)}, u32[]{:S(2)}) collective-permute-start(bf16[128,128]{1,0:T(8,128)(2,1)} %convert_element_type.75), channel_id=1, source_target_pairs={{512,384},{640,0},{768,128},{896,256},{513,385},{641,1},{769,129},... | collective-permute-start | bytes 98312 | tf_op jit(solution)/shard_map/ppermute | solution.py:60
  92.0 9.5 %copy-start.4 = (bf16[128,128]{1,0:T(8,128)(2,1)S(1)}, bf16[128,128]{1,0:T(8,128)(2,1)}, u32[]{:S(2)}) copy-start(bf16[128,128]{1,0:T(8,128)(2,1)} %convert_element_type.75) | copy-start | bytes 98308
  92.5 9.6 %copy-start.2 = (bf16[4,1024,128]{2,1,0:T(8,128)(2,1)}, bf16[4,1024,128]{2,1,0:T(8,128)(2,1)S(1)}, u32[]{:S(2)}) copy-start(bf16[4,1024,128]{2,1,0:T(8,128)(2,1)S(1)} %collective-permute-done.4.other_ref) | copy-start | bytes 3145732
  103.7 12.4 %collective-permute-start.8 = (bf16[4,1024,128]{2,1,0:T(8,128)(2,1)}, bf16[4,1024,128]{2,1,0:T(8,128)(2,1)S(1)}, u32[]{:S(2)}, u32[]{:S(2)}) collective-permute-start(bf16[4,1024,128]{2,1,0:T(8,128)(2,1)} %pad_maximum_fusion), channel_id=1, source_target_pairs={{0,1},{1,0},{2,3},{3,2},{4,5},{5,4},{6,7},{7,6},{8,9},{9,8},{10,11... | collective-permute-start | bytes 3145736 | tf_op jit(solution)/shard_map/ppermute | solution.py:50
  106.6 27.2 %all-to-all-start.2 = ((bf16[4,128,128]{2,1,0:T(8,128)(2,1)}), bf16[4,128,128]{2,1,0:T(8,128)(2,1)S(1)}, u32[]{:S(2)}, u32[]{:S(2)}) async-start(bf16[4,128,128]{2,1,0:T(8,128)(2,1)} %pad_maximum_fusion.4), calls=%async_computation.2 | async-start | bytes 262144 | tf_op jit(solution)/shard_map/all_to_all | solution.py:40
  116.1 22.2 %copy-start.7 = (f32[128,128]{1,0:T(8,128)S(1)}, f32[128,128]{1,0:T(8,128)}, u32[]{:S(2)}) copy-start(f32[128,128]{1,0:T(8,128)} %param.12) | copy-start | bytes 196612
  116.1 22.2 %copy-start.8 = (f32[128,128]{1,0:T(8,128)S(1)}, f32[128,128]{1,0:T(8,128)}, u32[]{:S(2)}) copy-start(f32[128,128]{1,0:T(8,128)} %param.14) | copy-start | bytes 196612
  116.1 22.2 %copy-start.9 = (f32[128,128]{1,0:T(8,128)S(1)}, f32[128,128]{1,0:T(8,128)}, u32[]{:S(2)}) copy-start(f32[128,128]{1,0:T(8,128)} %param.13) | copy-start | bytes 196612
  133.9 16.6 %all-to-all-start.3 = ((bf16[4,1024,128]{2,1,0:T(8,128)(2,1)}), bf16[4,1024,128]{2,1,0:T(8,128)(2,1)S(1)}, u32[]{:S(2)}, u32[]{:S(2)}) async-start(bf16[4,1024,128]{2,1,0:T(8,128)(2,1)} %add_convert_fusion), calls=%async_computation.3 | async-start | bytes 2097152 | tf_op jit(solution)/shard_map/all_to_all | solution.py:40
  139.0 16.7 %collective-permute-start.10 = (bf16[128,128]{1,0:T(8,128)(2,1)}, bf16[128,128]{1,0:T(8,128)(2,1)S(1)}, u32[]{:S(2)}, u32[]{:S(2)}) collective-permute-start(bf16[128,128]{1,0:T(8,128)(2,1)} %fusion.45), channel_id=1, source_target_pairs={{0,640},{128,768},{256,896},{384,512},{1,641},{129,769},{257,897},... | collective-permute-start | bytes 98312 | tf_op jit(solution)/shard_map/ppermute | solution.py:60
  140.3 26.9 %collective-permute-start.11 = (bf16[128,128]{1,0:T(8,128)(2,1)}, bf16[128,128]{1,0:T(8,128)(2,1)S(1)}, u32[]{:S(2)}, u32[]{:S(2)}) collective-permute-start(bf16[128,128]{1,0:T(8,128)(2,1)} %fusion.45), channel_id=1, source_target_pairs={{0,768},{128,896},{256,512},{384,640},{1,769},{129,897},{257,513},... | collective-permute-start | bytes 98312 | tf_op jit(solution)/shard_map/ppermute | solution.py:60
  141.6 25.9 %collective-permute-start.12 = (bf16[128,128]{1,0:T(8,128)(2,1)}, bf16[128,128]{1,0:T(8,128)(2,1)S(1)}, u32[]{:S(2)}, u32[]{:S(2)}) collective-permute-start(bf16[128,128]{1,0:T(8,128)(2,1)} %fusion.45), channel_id=1, source_target_pairs={{0,896},{128,512},{256,640},{384,768},{1,897},{129,513},{257,641},... | collective-permute-start | bytes 98312 | tf_op jit(solution)/shard_map/ppermute | solution.py:60
  142.9 24.6 %collective-permute-start.9 = (bf16[128,128]{1,0:T(8,128)(2,1)}, bf16[128,128]{1,0:T(8,128)(2,1)S(1)}, u32[]{:S(2)}, u32[]{:S(2)}) collective-permute-start(bf16[128,128]{1,0:T(8,128)(2,1)} %fusion.45), channel_id=1, source_target_pairs={{0,512},{128,640},{256,768},{384,896},{1,513},{129,641},{257,769},... | collective-permute-start | bytes 98312 | tf_op jit(solution)/shard_map/ppermute | solution.py:60
  155.7 11.8 %copy-start.10 = (bf16[128,128]{1,0:T(8,128)(2,1)}, bf16[128,128]{1,0:T(8,128)(2,1)S(1)}, u32[]{:S(2)}) copy-start(bf16[128,128]{1,0:T(8,128)(2,1)S(1)} %collective-permute-done.10.refs_1_) | copy-start | bytes 98308
  171.3 20.2 %copy-start.5 = (bf16[8,16,1024]{2,1,0:T(8,128)(2,1)S(1)}, bf16[8,16,1024]{2,1,0:T(8,128)(2,1)}, u32[]{:S(2)}) copy-start(bf16[8,16,1024]{2,1,0:T(8,128)(2,1)} %param.15) | copy-start | bytes 786436
  171.3 20.2 %copy-start.16 = (s32[16]{0:T(128)S(1)}, s32[16]{0:T(128)}, u32[]{:S(2)}) copy-start(s32[16]{0:T(128)} %param.19) | copy-start | bytes 196
  171.3 20.3 %copy-start.14 = (bf16[8,16,128]{2,1,0:T(8,128)(2,1)S(1)}, bf16[8,16,128]{2,1,0:T(8,128)(2,1)}, u32[]{:S(2)}) copy-start(bf16[8,16,128]{2,1,0:T(8,128)(2,1)} %param.16) | copy-start | bytes 98308
  172.3 7.7 %collective-permute-start.13 = (bf16[8,2,64,128]{3,2,1,0:T(8,128)(2,1)S(1)}, bf16[8,2,64,128]{3,2,1,0:T(8,128)(2,1)S(1)}, u32[]{:S(2)}, u32[]{:S(2)}) collective-permute-start(bf16[8,2,64,128]{3,2,1,0:T(8,128)(2,1)S(1)} %broadcast_select_fusion), channel_id=1, source_target_pairs={{0,8},{8,0},{1,9},{9,1},{2,10},{10,2},{3,11},{11,3},{4,12},{12,4},... | collective-permute-start | bytes 786440 | tf_op jit(solution)/shard_map/ppermute | solution.py:50
  181.9 21.5 %all-to-all-start.4 = ((bf16[8,2,64,128]{3,2,1,0:T(8,128)(2,1)}), bf16[8,2,64,128]{3,2,1,0:T(8,128)(2,1)S(1)}, u32[]{:S(2)}, u32[]{:S(2)}) async-start(bf16[8,2,64,128]{3,2,1,0:T(8,128)(2,1)} %fusion.29), calls=%async_computation.4 | async-start | bytes 524288 | tf_op jit(solution)/shard_map/all_to_all | solution.py:40
  203.4 10.8 %collective-permute-start.14 = (bf16[8,64,128]{2,1,0:T(8,128)(2,1)S(1)}, bf16[8,64,128]{2,1,0:T(8,128)(2,1)S(1)}, u32[]{:S(2)}, u32[]{:S(2)}) collective-permute-start(bf16[8,64,128]{2,1,0:T(8,128)(2,1)S(1)} %dynamic-slice_bitcast_fusion.1), channel_id=1, source_target_pairs={{0,1},{1,0},{2,3},{3,2},{4,5},{5,4},{6,7},{7,6},{8,9},{9,8},{10,11... | collective-permute-start | bytes 393224 | tf_op jit(solution)/shard_map/ppermute | solution.py:50
  (6 other events, 6.7 us)

commit v6 on v3

--- a/solution.py
+++ b/solution.py
@@ -1,6 +1,8 @@
 import jax
 import jax.numpy as jnp
 from jax import lax
+from jax.experimental import pallas as pl
+from jax.experimental.pallas import tpu as pltpu
 from jax.sharding import Mesh, PartitionSpec as P
 
 
@@ -18,6 +20,9 @@
 bias_two = 1.0 - 0.95**10
 neg_fill = -1e30
 
+
+INTERPRET = False
+
 DP = ("zh", "zl", "yl")
 TP = ("x", "core")
 NEAR = ("zl", "yl")
@@ -59,18 +64,84 @@
     return sorted(range(far), key=lambda k: -min(k, far - k))
 
 
-def by_source(received):
-    far = len(received)
-    back = [received[-m % far] for m in range(far)]
-    return lax.dynamic_slice_in_dim(jnp.stack(back + back), -lax.axis_index("zh") % far, far, 0)
-
-
 def at_index(value, index):
     return lax.dynamic_index_in_dim(value, index, 0, keepdims=False)
 
 
 def dot32(a, b, dims):
     return lax.dot_general(a, b, (dims, ((), ())), preferred_element_type=jnp.float32)
+
+
+def back_terms(at_ref, mine_ref, other_ref, *refs):
+    parts, outs = refs[:-2], refs[-2:]
+    far = len(parts)
+
+    @pl.when(at_ref[0] == 0)
+    def _():
+        for k, part in enumerate(parts):
+            f = lax.rem(at_ref[1] - k + far, far)
+            for rows, out in zip((mine_ref, other_ref), outs):
+                out[f] = dot32(rows[...], part[...], ((1,), (1,))).astype(jnp.bfloat16)
+
+
+def before_swap(at_ref, mine_ref, other_ref, back_ref, *refs):
+    parts, (stays_ref, sent_ref) = refs[:-2], refs[-2:]
+    far = len(parts)
+    zh_at, first = at_ref[1], at_ref[2] == 0
+    line, _, half, width = stays_ref.shape
+    step = max(line // 2, 1)
+
+    @pl.when(at_ref[0] == 0)
+    def _():
+        for begin in range(0, line, step):
+            rows = pl.ds(begin * 2 * half, step * 2 * half)
+            total = sum(back_ref[i, rows, :].astype(jnp.float32) for i in range(far))
+            sent_ref[pl.ds(begin, step)] = total.astype(jnp.bfloat16).reshape(step, 2, half, width)
+
+    @pl.when(at_ref[0] == 1)
+    def _():
+        for slot, rows_ref in enumerate((mine_ref, other_ref)):
+            for begin in range(0, line, step):
+                rows = pl.ds(begin * 2 * half, step * 2 * half)
+                total = None
+                for k, part in enumerate(parts):
+                    f = lax.rem(zh_at - k + far, far)
+                    term = dot32(rows_ref[f, rows, :], part[...], ((1,), (0,)))
+                    total = term if total is None else total + term
+                total = total.reshape(step, 2, half, width)
+                low, high = total[:, 0], total[:, 1]
+                stays_ref[pl.ds(begin, step), slot] = jnp.where(first, low, high)
+                sent_ref[pl.ds(begin, step), slot] = jnp.where(first, high, low).astype(jnp.bfloat16)
+
+
+def after_swap(at_ref, own_ref, met_ref, stays_ref, out_ref):
+    @pl.when(at_ref[0] == 1)
+    def _():
+        out_ref[...] = (stays_ref[...] + met_ref[...].astype(jnp.float32)).astype(jnp.bfloat16)
+
+    @pl.when((at_ref[0] == 0) & (at_ref[2] == 0))
+    def _():
+        out_ref[:, 0] = own_ref[:, 0]
+        out_ref[:, 1] = met_ref[:, 0]
+
+    @pl.when((at_ref[0] == 0) & (at_ref[2] == 1))
+    def _():
+        out_ref[:, 0] = met_ref[:, 1]
+        out_ref[:, 1] = own_ref[:, 1]
+
+
+def in_vmem(kernel, outs, flops, at, *args):
+    vmem = pl.BlockSpec(memory_space=pltpu.VMEM)
+    many = isinstance(outs, tuple)
+    moved = sum(v.size * v.dtype.itemsize for v in (*args, *(outs if many else (outs,))))
+    return pl.pallas_call(
+        kernel,
+        out_shape=outs,
+        in_specs=[pl.BlockSpec(memory_space=pltpu.SMEM)] + [vmem] * len(args),
+        out_specs=(vmem,) * len(outs) if many else vmem,
+        cost_estimate=pl.CostEstimate(flops=flops, bytes_accessed=moved, transcendentals=0),
+        interpret=INTERPRET,
+    )(at, *args)
 
 
 def local(
@@ -92,13 +163,15 @@
     mine = lax.dynamic_slice(hidden[0], (core_at * half, x_at * near * block), (half, near * block))
     mine = mine.reshape(half, near, block).transpose(1, 0, 2)
     mine = exchange(mine, NEAR)
+    mine, old_weight = lax.optimization_barrier((mine, master.astype(jnp.bfloat16)))
+    mine = gather(mine.reshape(near * half, block), "x")
+    other = swap(mine, "core")
 
     by, grads, at = line // 2, out_grad, 0
     while by:
         first = lax.axis_index("zl") & by == 0
-        grads = jnp.stack(ordered(grads, swap(grads, "zl", by), first), axis=at)
-        if at == 0:
-            grads, mine = lax.optimization_barrier((grads, mine))
+        met = swap(grads, "zl", by)
+        grads = jnp.stack(ordered(grads, met, first), axis=at)
         by, at = by // 2, at + 1
     grads = jnp.stack(ordered(grads, swap(grads, "yl"), yl_at == 0), axis=at)
     grads = grads.reshape(near, tokens, width_here)
@@ -107,8 +180,8 @@
         for at in (core_at, 1 - core_at)
     )
 
-    mine = gather(mine.reshape(near * half, block), "x")
-    other = swap(mine, "core")
+    old_parts = {k: far_shift(old_weight, k, 1, 0) for k in far_order(far)[:-1]}
+    old_parts[0] = old_weight
 
     partial = jnp.stack(
         [
@@ -116,35 +189,31 @@
             for f in range(far)
         ]
     ).astype(jnp.bfloat16)
-    partial, old_weight = lax.optimization_barrier((partial, master.astype(jnp.bfloat16)))
-    gradient = [far_shift(at_index(partial, (zh_at + k) % far), k, 0, 1) for k in far_order(far)]
-
-    old_parts = {k: far_shift(old_weight, k, 0, 0) for k in far_order(far)[:-1]}
-    old_parts[0] = old_weight
-    old_weight = by_source([old_parts[k] for k in range(far)])
-    kept, sent = (
-        jnp.stack([dot32(rows, old_weight[f], ((1,), (1,))).astype(jnp.bfloat16) for f in range(far)])
-        for rows in (at_mine, at_other)
+    gradient = at_index(partial, zh_at).astype(jnp.float32)
+    for k in far_order(far)[:-1]:
+        gradient += far_shift(at_index(partial, (zh_at + k) % far), k, 0, 0).astype(jnp.float32)
+
+    fresh = adam_fresh(master, moment1, moment2, gradient)
+    parts = {k: far_shift(fresh, k, 0, 1) for k in far_order(far)}
+
+    at = jnp.stack([lax.axis_index("role"), zh_at, yl_at])
+    flops = 4 * far * near * half * block * width_here
+    wide = jax.ShapeDtypeStruct((far, near * half, block), jnp.bfloat16)
+    kept, sent = in_vmem(
+        back_terms, (wide, wide), flops, at, at_mine, at_other, *(old_parts[k] for k in range(far))
     )
     back = (kept.astype(jnp.float32) + swap(sent, "core").astype(jnp.float32)).astype(jnp.bfloat16)
-    gradient, back = lax.optimization_barrier((gradient, back))
-    back = jnp.sum(exchange(back, "x").astype(jnp.float32), axis=0).astype(jnp.bfloat16)
-    back = back.reshape(line, 2, half, block)
-    stays = lax.dynamic_index_in_dim(back, yl_at, 1, keepdims=False)
-    leaves = lax.dynamic_index_in_dim(back, 1 - yl_at, 1, keepdims=False)
-    back = jnp.stack(ordered(stays, swap(leaves, "yl"), yl_at == 0), axis=1)
-
-    fresh = adam_fresh(master, moment1, moment2, sum(g.astype(jnp.float32) for g in gradient))
-    parts = {k: far_shift(fresh, k, 1, 1) for k in far_order(far)[:-1]}
-    parts[0] = fresh
-    weight = by_source([parts[k] for k in range(far)])
-    terms = [sum(dot32(rows[f], weight[f], ((1,), (0,))) for f in range(far)) for rows in (mine, other)]
-    terms = jnp.stack([rows.reshape(line, 2, half, width_here) for rows in terms], axis=2)
-    stays = lax.dynamic_index_in_dim(terms, yl_at, 1, keepdims=False)
-    leaves = lax.dynamic_index_in_dim(terms, 1 - yl_at, 1, keepdims=False)
-    terms = stays + swap(leaves.astype(jnp.bfloat16), "yl").astype(jnp.float32)
-
-    moved = exchange(jnp.where(is_learner, back, terms.astype(jnp.bfloat16)), "zl")
+    back = exchange(back, "x")
+
+    shape = (line, 2, half, width_here)
+    narrow = jax.ShapeDtypeStruct(shape, jnp.bfloat16)
+    stays, own = in_vmem(
+        before_swap,
+        (jax.ShapeDtypeStruct(shape, jnp.float32), narrow),
+        flops, at, mine, other, back, *(parts[k] for k in range(far)),
+    )
+    last = in_vmem(after_swap, narrow, 0, at, own, swap(own, "yl"), stays)
+    moved = exchange(last, "zl")
     values = jnp.sum(moved.astype(jnp.float32), axis=0)
     values = jnp.concatenate(ordered(values[0], values[1], core_at == 0))
     back = moved.reshape(2, near // 2, half, block)

time: 234 us -> 231 us (0.987)
  the two profiles are of different devices: /device:TPU:25 before, /device:TPU:29 now
where the time goes in v6:
time: 231 us; the launch traced here: 229 us
  starting transfers between devices  96.4 us (42%)
  waiting for transfers between devices  95.1 us (41%)
  matrix products  14.9 us (6%)
  local copies, waits for them, and re-layouts  8.44 us (4%)
  Pallas kernels  7.88 us (3%)
  other arithmetic  5.92 us (3%)
    ppermute x10, waiting for transfers between devices, far_shift(): return lax.ppermute(value, ('role', 'zh'), pairs)  64.1 us
    ppermute x8, starting transfers between devices, swap(): return lax.ppermute(value, axis, [(i, i ^ by) for i in range(peers)])  38.2 us
    ppermute x10, starting transfers between devices, far_shift(): return lax.ppermute(value, ('role', 'zh'), pairs)  31.7 us
    all_to_all x4, starting transfers between devices, exchange(): return lax.all_to_all(value, axis, 0, 0, tiled=True)  26.5 us
    ppermute x8, waiting for transfers between devices, swap(): return lax.ppermute(value, axis, [(i, i ^ by) for i in range(peers)])  24.4 us
    dot_general x8, matrix products, dot32(): lax.dot_general(a, b, (dims, ((), ())), preferred_element_type=jnp.float32)  9.13 us
    pallas_call x3, Pallas kernels, in_vmem(): pl.pallas_call(kernel, out_shape=outs, in_specs=[pl.BlockSpec(memory_spac...  7.88 us
    all_to_all x4, waiting for transfers between devices, exchange(): return lax.all_to_all(value, axis, 0, 0, tiled=True)  6.56 us
  transfers between devices with their start and end apart: 22, of which 9 were waited for; matrix products, arithmetic and copies ran while one was open for 10% of the time, Pallas kernels for 1%

profile of v6, /device:TPU:29, one launch (start us, length us, event | category | flops | bytes accessed | tf_op | source)
XLA Modules:
  0.0 229.4 jit_solution(15036090313801395187)
XLA Ops:
  0.0 1.6 copy-done
  2.4 13.4 %all-to-all-start = ((bf16[16,64,128]{2,1,0:T(8,128)(2,1)}), bf16[16,64,128]{2,1,0:T(8,128)(2,1)S(1)}, u32[]{:S(2)}, u32[]{:S(2)}) async-start(bf16[16,64,128]{2,1,0:T(8,128)(2,1)} %copy.37), calls=%async_computation | async-start | bytes 524288 | tf_op jit(solution)/shard_map/all_to_all | solution.py:40
  15.9 7.0 %collective-permute-start.1 = (bf16[128,128]{1,0:T(8,128)(2,1)S(1)}, bf16[128,128]{1,0:T(8,128)(2,1)S(1)}, u32[]{:S(2)}, u32[]{:S(2)}) collective-permute-start(bf16[128,128]{1,0:T(8,128)(2,1)S(1)} %copy-done.17), channel_id=1, source_target_pairs={{0,64},{16,80},{32,96},{48,112},{64,0},{80,16},{96,32},{112,48},{1... | collective-permute-start | bytes 98312 | tf_op jit(solution)/shard_map/ppermute | solution.py:50
  22.9 10.7 %collective-permute-done.1 = bf16[128,128]{1,0:T(8,128)(2,1)S(1)} collective-permute-done((bf16[128,128]{1,0:T(8,128)(2,1)S(1)}, bf16[128,128]{1,0:T(8,128)(2,1)S(1)}, u32[]{:S(2)}, u32[]{:S(2)}) %collective-permute-start.1) | collective-permute-done | bytes 32800 | tf_op jit(solution)/shard_map/ppermute | solution.py:50
  33.6 1.9 collective-permute-start.2
  35.6 4.0 %collective-permute-done.2 = bf16[2,128,128]{2,1,0:T(8,128)(2,1)S(1)} collective-permute-done((bf16[2,128,128]{2,1,0:T(8,128)(2,1)S(1)}, bf16[2,128,128]{2,1,0:T(8,128)(2,1)S(1)}, u32[]{:S(2)}, u32[]{:S(2)}) %collective-permute-start.2) | collective-permute-done | bytes 65568 | tf_op jit(solution)/shard_map/ppermute | solution.py:50
  39.6 3.5 %collective-permute-start.3 = (bf16[2,2,128,128]{3,2,1,0:T(8,128)(2,1)S(1)}, bf16[2,2,128,128]{3,2,1,0:T(8,128)(2,1)S(1)}, u32[]{:S(2)}, u32[]{:S(2)}) collective-permute-start(bf16[2,2,128,128]{3,2,1,0:T(8,128)(2,1)S(1)} %pad_maximum_fusion.2), channel_id=1, source_target_pairs={{0,16},{16,0},{32,48},{48,32},{64,80},{80,64},{96,112},{112,96},{1... | collective-permute-start | bytes 393224 | tf_op jit(solution)/shard_map/ppermute | solution.py:50
  43.1 2.3 %collective-permute-done.3 = bf16[2,2,128,128]{3,2,1,0:T(8,128)(2,1)S(1)} collective-permute-done((bf16[2,2,128,128]{3,2,1,0:T(8,128)(2,1)S(1)}, bf16[2,2,128,128]{3,2,1,0:T(8,128)(2,1)S(1)}, u32[]{:S(2)}, u32[]{:S(2)}) %collective-permute-start.3) | collective-permute-done | bytes 131104 | tf_op jit(solution)/shard_map/ppermute | solution.py:50
  46.2 1.9 collective-permute-start.4
  49.4 4.2 %all-to-all-start.1 = ((bf16[4,1024,128]{2,1,0:T(8,128)(2,1)}), bf16[4,1024,128]{2,1,0:T(8,128)(2,1)S(1)}, u32[]{:S(2)}, u32[]{:S(2)}) async-start(bf16[4,1024,128]{2,1,0:T(8,128)(2,1)} %broadcast_in_dim.29), calls=%async_computation.1 | async-start | bytes 2097152 | tf_op jit(solution)/shard_map/all_to_all | solution.py:40
  55.2 16.1 %collective-permute-start.5 = (bf16[128,128]{1,0:T(8,128)(2,1)S(1)}, bf16[128,128]{1,0:T(8,128)(2,1)S(1)}, u32[]{:S(2)}, u32[]{:S(2)}) collective-permute-start(bf16[128,128]{1,0:T(8,128)(2,1)S(1)} %convert_element_type.55.refs_0_), channel_id=1, source_target_pairs={{512,128},{640,256},{768,384},{896,0},{513,129},{641,257},{769,385... | collective-permute-start | bytes 98312 | tf_op jit(solution)/shard_map/ppermute | solution.py:60
  71.3 7.0 %collective-permute-start.6 = (bf16[128,128]{1,0:T(8,128)(2,1)S(1)}, bf16[128,128]{1,0:T(8,128)(2,1)S(1)}, u32[]{:S(2)}, u32[]{:S(2)}) collective-permute-start(bf16[128,128]{1,0:T(8,128)(2,1)S(1)} %convert_element_type.55.refs_0_), channel_id=1, source_target_pairs={{512,256},{640,384},{768,0},{896,128},{513,257},{641,385},{769,1},... | collective-permute-start | bytes 98312 | tf_op jit(solution)/shard_map/ppermute | solution.py:60
  82.1 2.4 %shard_map.100 = (bf16[4,1024,128]{2,1,0:T(8,128)(2,1)}, bf16[4,1024,128]{2,1,0:T(8,128)(2,1)}) custom-call(s32[3]{0:T(128)} %pad_add_fusion.at_ref, bf16[1024,128]{1,0:T(8,128)(2,1)} %bitcast.165, bf16[1024,128]{1,0:T(8,128)(2,1)} %bitcast.160, bf16[128,128]{1,0:T(8,128)(2,1)} %copy-done.16, bf16[128,128]{1,0:T(8,128)(2,1)} %copy-done.20, ...), custom_call_target="tpu_custom_call" | custom-call | flops 268435456 | bytes 2752512 | tf_op jit(solution)/shard_map/pallas_call | solution.py:137
  84.5 10.8 %collective-permute-start.8 = (bf16[4,1024,128]{2,1,0:T(8,128)(2,1)}, bf16[4,1024,128]{2,1,0:T(8,128)(2,1)}, u32[]{:S(2)}, u32[]{:S(2)}) collective-permute-start(bf16[4,1024,128]{2,1,0:T(8,128)(2,1)} %get-tuple-element.14), channel_id=1, source_target_pairs={{0,1},{1,0},{2,3},{3,2},{4,5},{5,4},{6,7},{7,6},{8,9},{9,8},{10,11... | collective-permute-start | bytes 3145736 | tf_op jit(solution)/shard_map/ppermute | solution.py:50
  95.4 2.1 collective-permute-start
  97.4 1.8 fusion.24
  99.3 1.8 fusion.23
  101.7 2.5 %add_convert_fusion = bf16[4,1024,128]{2,1,0:T(8,128)(2,1)} fusion(bf16[4,1024,128]{2,1,0:T(8,128)(2,1)} %collective-permute-done.8, bf16[4,1024,128]{2,1,0:T(8,128)(2,1)S(1)} %copy-done.4), kind=kLoop, calls=%fused_computation | loop fusion | flops 2097152 | bytes 3145728 | tf_op jit(solution)/shard_map/convert_element_type | solution.py:205
  104.2 5.4 %all-to-all-start.2 = ((bf16[4,1024,128]{2,1,0:T(8,128)(2,1)}), bf16[4,1024,128]{2,1,0:T(8,128)(2,1)}, u32[]{:S(2)}, u32[]{:S(2)}) async-start(bf16[4,1024,128]{2,1,0:T(8,128)(2,1)} %add_convert_fusion), calls=%async_computation.2 | async-start | bytes 2097152 | tf_op jit(solution)/shard_map/all_to_all | solution.py:40
  116.9 1.4 collective-permute-start.12
  122.2 38.9 %collective-permute-done.12.refs_0_ = bf16[128,128]{1,0:T(8,128)(2,1)S(1)} collective-permute-done((bf16[128,128]{1,0:T(8,128)(2,1)S(1)}, bf16[128,128]{1,0:T(8,128)(2,1)S(1)}, u32[]{:S(2)}, u32[]{:S(2)}) %collective-permute-start.12) | collective-permute-done | bytes 32800 | tf_op jit(solution)/shard_map/ppermute | solution.py:60
  161.1 8.7 %collective-permute-done.13.refs_1_ = bf16[128,128]{1,0:T(8,128)(2,1)S(1)} collective-permute-done((bf16[128,128]{1,0:T(8,128)(2,1)S(1)}, bf16[128,128]{1,0:T(8,128)(2,1)S(1)}, u32[]{:S(2)}, u32[]{:S(2)}) %collective-permute-start.13) | collective-permute-done | bytes 32800 | tf_op jit(solution)/shard_map/ppermute | solution.py:60
  169.8 15.6 %collective-permute-done.14.refs_2_ = bf16[128,128]{1,0:T(8,128)(2,1)S(1)} collective-permute-done((bf16[128,128]{1,0:T(8,128)(2,1)S(1)}, bf16[128,128]{1,0:T(8,128)(2,1)S(1)}, u32[]{:S(2)}, u32[]{:S(2)}) %collective-permute-start.14) | collective-permute-done | bytes 32800 | tf_op jit(solution)/shard_map/ppermute | solution.py:60
  186.6 3.5 %shard_map.101 = (f32[8,2,64,128]{3,2,1,0:T(8,128)}, bf16[8,2,64,128]{3,2,1,0:T(8,128)(2,1)}) custom-call(s32[3]{0:T(128)} %pad_add_fusion.at_ref, bf16[4,1024,128]{2,1,0:T(8,128)(2,1)} %copy-done.1, bf16[4,1024,128]{2,1,0:T(8,128)(2,1)} %collective-permute-done.other_ref, bf16[4,1024,128]{2,1,0:T(8,128)(2,1)} %all-to-all-done.2.back_ref, ...), custom_call_target="tpu_custom_call" | custom-call | flops 268435456 | bytes 4063232 | tf_op jit(solution)/shard_map/pallas_call | solution.py:137
  190.1 1.9 collective-permute-start.16
  192.0 7.3 %collective-permute-done.16.met_ref = bf16[8,2,64,128]{3,2,1,0:T(8,128)(2,1)S(1)} collective-permute-done((bf16[8,2,64,128]{3,2,1,0:T(8,128)(2,1)}, bf16[8,2,64,128]{3,2,1,0:T(8,128)(2,1)S(1)}, u32[]{:S(2)}, u32[]{:S(2)}) %collective-permute-start.16) | collective-permute-done | bytes 262176 | tf_op jit(solution)/shard_map/ppermute | solution.py:50
  200.1 2.0 shard_map.102
  202.1 3.4 %all-to-all-start.3 = ((bf16[8,2,64,128]{3,2,1,0:T(8,128)(2,1)}), bf16[8,2,64,128]{3,2,1,0:T(8,128)(2,1)S(1)}, u32[]{:S(2)}, u32[]{:S(2)}) async-start(bf16[8,2,64,128]{3,2,1,0:T(8,128)(2,1)} %shard_map.102), calls=%async_computation.3 | async-start | bytes 524288 | tf_op jit(solution)/shard_map/all_to_all | solution.py:40
  207.0 1.9 fusion.43
  210.8 6.6 %all-to-all-done.3 = bf16[8,2,64,128]{3,2,1,0:T(8,128)(2,1)S(1)} async-done(((bf16[8,2,64,128]{3,2,1,0:T(8,128)(2,1)}), bf16[8,2,64,128]{3,2,1,0:T(8,128)(2,1)S(1)}, u32[]{:S(2)}, u32[]{:S(2)}) %all-to-all-start.3) | async-done | bytes 262176 | tf_op jit(solution)/shard_map/all_to_all | solution.py:40
  217.4 9.0 %collective-permute-start.17 = (bf16[8,64,128]{2,1,0:T(8,128)(2,1)S(1)}, bf16[8,64,128]{2,1,0:T(8,128)(2,1)S(1)}, u32[]{:S(2)}, u32[]{:S(2)}) collective-permute-start(bf16[8,64,128]{2,1,0:T(8,128)(2,1)S(1)} %dynamic-slice_bitcast_fusion.1), channel_id=1, source_target_pairs={{0,1},{1,0},{2,3},{3,2},{4,5},{5,4},{6,7},{7,6},{8,9},{9,8},{10,11... | collective-permute-start | bytes 393224 | tf_op jit(solution)/shard_map/ppermute | solution.py:50
  226.5 1.4 fusion.6
  (111 shorter events, 26.3 us)
Async XLA Ops:
  0.0 15.9 %copy-start.17 = (bf16[128,128]{1,0:T(8,128)(2,1)S(1)}, bf16[128,128]{1,0:T(8,128)(2,1)}, u32[]{:S(2)}) copy-start(bf16[128,128]{1,0:T(8,128)(2,1)} %param.11) | copy-start | bytes 98308
  0.0 48.2 %copy-start.7 = (f32[128,128]{1,0:T(8,128)S(1)}, f32[128,128]{1,0:T(8,128)}, u32[]{:S(2)}) copy-start(f32[128,128]{1,0:T(8,128)} %param.12) | copy-start | bytes 196612
  2.4 45.8 %all-to-all-start = ((bf16[16,64,128]{2,1,0:T(8,128)(2,1)}), bf16[16,64,128]{2,1,0:T(8,128)(2,1)S(1)}, u32[]{:S(2)}, u32[]{:S(2)}) async-start(bf16[16,64,128]{2,1,0:T(8,128)(2,1)} %copy.37), calls=%async_computation | async-start | bytes 524288 | tf_op jit(solution)/shard_map/all_to_all | solution.py:40
  15.9 17.7 %collective-permute-start.1 = (bf16[128,128]{1,0:T(8,128)(2,1)S(1)}, bf16[128,128]{1,0:T(8,128)(2,1)S(1)}, u32[]{:S(2)}, u32[]{:S(2)}) collective-permute-start(bf16[128,128]{1,0:T(8,128)(2,1)S(1)} %copy-done.17), channel_id=1, source_target_pairs={{0,64},{16,80},{32,96},{48,112},{64,0},{80,16},{96,32},{112,48},{1... | collective-permute-start | bytes 98312 | tf_op jit(solution)/shard_map/ppermute | solution.py:50
  33.6 5.9 %collective-permute-start.2 = (bf16[2,128,128]{2,1,0:T(8,128)(2,1)S(1)}, bf16[2,128,128]{2,1,0:T(8,128)(2,1)S(1)}, u32[]{:S(2)}, u32[]{:S(2)}) collective-permute-start(bf16[2,128,128]{2,1,0:T(8,128)(2,1)S(1)} %pad_maximum_fusion.4), channel_id=1, source_target_pairs={{0,32},{16,48},{32,0},{48,16},{64,96},{80,112},{96,64},{112,80},{1... | collective-permute-start | bytes 196616 | tf_op jit(solution)/shard_map/ppermute | solution.py:50
  39.6 5.9 %collective-permute-start.3 = (bf16[2,2,128,128]{3,2,1,0:T(8,128)(2,1)S(1)}, bf16[2,2,128,128]{3,2,1,0:T(8,128)(2,1)S(1)}, u32[]{:S(2)}, u32[]{:S(2)}) collective-permute-start(bf16[2,2,128,128]{3,2,1,0:T(8,128)(2,1)S(1)} %pad_maximum_fusion.2), channel_id=1, source_target_pairs={{0,16},{16,0},{32,48},{48,32},{64,80},{80,64},{96,112},{112,96},{1... | collective-permute-start | bytes 393224 | tf_op jit(solution)/shard_map/ppermute | solution.py:50
  46.2 7.9 %collective-permute-start.4 = (bf16[2,2,2,128,128]{4,3,2,1,0:T(8,128)(2,1)}, bf16[2,2,2,128,128]{4,3,2,1,0:T(8,128)(2,1)}, u32[]{:S(2)}, u32[]{:S(2)}) collective-permute-start(bf16[2,2,2,128,128]{4,3,2,1,0:T(8,128)(2,1)} %pad_maximum_fusion.1), channel_id=1, source_target_pairs={{0,8},{8,0},{1,9},{9,1},{2,10},{10,2},{3,11},{11,3},{4,12},{12,4},... | collective-permute-start | bytes 786440 | tf_op jit(solution)/shard_map/ppermute | solution.py:50
  48.2 30.2 %copy-start.16 = (bf16[128,128]{1,0:T(8,128)(2,1)}, bf16[128,128]{1,0:T(8,128)(2,1)S(1)}, u32[]{:S(2)}) copy-start(bf16[128,128]{1,0:T(8,128)(2,1)S(1)} %convert_element_type.55.refs_0_) | copy-start | bytes 98308
  49.4 46.0 %all-to-all-start.1 = ((bf16[4,1024,128]{2,1,0:T(8,128)(2,1)}), bf16[4,1024,128]{2,1,0:T(8,128)(2,1)S(1)}, u32[]{:S(2)}, u32[]{:S(2)}) async-start(bf16[4,1024,128]{2,1,0:T(8,128)(2,1)} %broadcast_in_dim.29), calls=%async_computation.1 | async-start | bytes 2097152 | tf_op jit(solution)/shard_map/all_to_all | solution.py:40
  55.2 25.3 %collective-permute-start.5 = (bf16[128,128]{1,0:T(8,128)(2,1)S(1)}, bf16[128,128]{1,0:T(8,128)(2,1)S(1)}, u32[]{:S(2)}, u32[]{:S(2)}) collective-permute-start(bf16[128,128]{1,0:T(8,128)(2,1)S(1)} %convert_element_type.55.refs_0_), channel_id=1, source_target_pairs={{512,128},{640,256},{768,384},{896,0},{513,129},{641,257},{769,385... | collective-permute-start | bytes 98312 | tf_op jit(solution)/shard_map/ppermute | solution.py:60
  71.3 9.2 %collective-permute-start.6 = (bf16[128,128]{1,0:T(8,128)(2,1)S(1)}, bf16[128,128]{1,0:T(8,128)(2,1)S(1)}, u32[]{:S(2)}, u32[]{:S(2)}) collective-permute-start(bf16[128,128]{1,0:T(8,128)(2,1)S(1)} %convert_element_type.55.refs_0_), channel_id=1, source_target_pairs={{512,256},{640,384},{768,0},{896,128},{513,257},{641,385},{769,1},... | collective-permute-start | bytes 98312 | tf_op jit(solution)/shard_map/ppermute | solution.py:60
  78.4 3.1 %collective-permute-start.7 = (bf16[128,128]{1,0:T(8,128)(2,1)S(1)}, bf16[128,128]{1,0:T(8,128)(2,1)S(1)}, u32[]{:S(2)}, u32[]{:S(2)}) collective-permute-start(bf16[128,128]{1,0:T(8,128)(2,1)S(1)} %convert_element_type.55.refs_0_), channel_id=1, source_target_pairs={{512,384},{640,0},{768,128},{896,256},{513,385},{641,1},{769,129},... | collective-permute-start | bytes 98312 | tf_op jit(solution)/shard_map/ppermute | solution.py:60
  80.5 20.6 %copy-start.3 = (bf16[16,64,128]{2,1,0:T(8,128)(2,1)S(1)}, bf16[16,64,128]{2,1,0:T(8,128)(2,1)}, u32[]{:S(2)}) copy-start(bf16[16,64,128]{2,1,0:T(8,128)(2,1)} %get-tuple-element.18) | copy-start | bytes 786436
  84.5 17.2 %collective-permute-start.8 = (bf16[4,1024,128]{2,1,0:T(8,128)(2,1)}, bf16[4,1024,128]{2,1,0:T(8,128)(2,1)}, u32[]{:S(2)}, u32[]{:S(2)}) collective-permute-start(bf16[4,1024,128]{2,1,0:T(8,128)(2,1)} %get-tuple-element.14), channel_id=1, source_target_pairs={{0,1},{1,0},{2,3},{3,2},{4,5},{5,4},{6,7},{7,6},{8,9},{9,8},{10,11... | collective-permute-start | bytes 3145736 | tf_op jit(solution)/shard_map/ppermute | solution.py:50
  95.3 8.9 %copy-start.1 = (bf16[4,1024,128]{2,1,0:T(8,128)(2,1)}, bf16[4,1024,128]{2,1,0:T(8,128)(2,1)S(1)}, u32[]{:S(2)}) copy-start(bf16[4,1024,128]{2,1,0:T(8,128)(2,1)S(1)} %all-to-all-done.1.mine_ref) | copy-start | bytes 3145732
  95.4 14.3 %collective-permute-start = (bf16[4,1024,128]{2,1,0:T(8,128)(2,1)S(1)}, bf16[4,1024,128]{2,1,0:T(8,128)(2,1)}, u32[]{:S(2)}, u32[]{:S(2)}) collective-permute-start(bf16[4,1024,128]{2,1,0:T(8,128)(2,1)S(1)} %all-to-all-done.1.mine_ref), channel_id=1, source_target_pairs={{0,1},{1,0},{2,3},{3,2},{4,5},{5,4},{6,7},{7,6},{8,9},{9,8},{10,11... | collective-permute-start | bytes 3145736 | tf_op jit(solution)/shard_map/ppermute | solution.py:50
  104.2 18.0 %all-to-all-start.2 = ((bf16[4,1024,128]{2,1,0:T(8,128)(2,1)}), bf16[4,1024,128]{2,1,0:T(8,128)(2,1)}, u32[]{:S(2)}, u32[]{:S(2)}) async-start(bf16[4,1024,128]{2,1,0:T(8,128)(2,1)} %add_convert_fusion), calls=%async_computation.2 | async-start | bytes 2097152 | tf_op jit(solution)/shard_map/all_to_all | solution.py:40
  114.7 2.0 collective-permute-start.10
  115.3 1.4 collective-permute-start.11
  116.0 0.7 collective-permute-start.9
  116.8 88.7 %copy-start.6 = (bf16[8,16,1024]{2,1,0:T(8,128)(2,1)S(1)}, bf16[8,16,1024]{2,1,0:T(8,128)(2,1)}, u32[]{:S(2)}) copy-start(bf16[8,16,1024]{2,1,0:T(8,128)(2,1)} %param.15) | copy-start | bytes 786436
  116.8 88.8 %copy-start.18 = (s32[16]{0:T(128)S(1)}, s32[16]{0:T(128)}, u32[]{:S(2)}) copy-start(s32[16]{0:T(128)} %param.19) | copy-start | bytes 196
  116.8 88.8 %copy-start.15 = (bf16[8,16,128]{2,1,0:T(8,128)(2,1)S(1)}, bf16[8,16,128]{2,1,0:T(8,128)(2,1)}, u32[]{:S(2)}) copy-start(bf16[8,16,128]{2,1,0:T(8,128)(2,1)} %param.16) | copy-start | bytes 98308
  116.9 44.2 %collective-permute-start.12 = (bf16[128,128]{1,0:T(8,128)(2,1)S(1)}, bf16[128,128]{1,0:T(8,128)(2,1)S(1)}, u32[]{:S(2)}, u32[]{:S(2)}) collective-permute-start(bf16[128,128]{1,0:T(8,128)(2,1)S(1)} %fusion.38), channel_id=1, source_target_pairs={{0,512},{128,640},{256,768},{384,896},{1,513},{129,641},{257,769},... | collective-permute-start | bytes 98312 | tf_op jit(solution)/shard_map/ppermute | solution.py:60
  118.3 51.5 %collective-permute-start.13 = (bf16[128,128]{1,0:T(8,128)(2,1)S(1)}, bf16[128,128]{1,0:T(8,128)(2,1)S(1)}, u32[]{:S(2)}, u32[]{:S(2)}) collective-permute-start(bf16[128,128]{1,0:T(8,128)(2,1)S(1)} %fusion.38), channel_id=1, source_target_pairs={{0,640},{128,768},{256,896},{384,512},{1,641},{129,769},{257,897},... | collective-permute-start | bytes 98312 | tf_op jit(solution)/shard_map/ppermute | solution.py:60
  119.6 65.8 %collective-permute-start.14 = (bf16[128,128]{1,0:T(8,128)(2,1)S(1)}, bf16[128,128]{1,0:T(8,128)(2,1)S(1)}, u32[]{:S(2)}, u32[]{:S(2)}) collective-permute-start(bf16[128,128]{1,0:T(8,128)(2,1)S(1)} %fusion.38), channel_id=1, source_target_pairs={{0,768},{128,896},{256,512},{384,640},{1,769},{129,897},{257,513},... | collective-permute-start | bytes 98312 | tf_op jit(solution)/shard_map/ppermute | solution.py:60
  120.9 64.5 %collective-permute-start.15 = (bf16[128,128]{1,0:T(8,128)(2,1)S(1)}, bf16[128,128]{1,0:T(8,128)(2,1)S(1)}, u32[]{:S(2)}, u32[]{:S(2)}) collective-permute-start(bf16[128,128]{1,0:T(8,128)(2,1)S(1)} %fusion.38), channel_id=1, source_target_pairs={{0,896},{128,512},{256,640},{384,768},{1,897},{129,513},{257,641},... | collective-permute-start | bytes 98312 | tf_op jit(solution)/shard_map/ppermute | solution.py:60
  161.1 24.4 %copy-start.11 = (bf16[128,128]{1,0:T(8,128)(2,1)}, bf16[128,128]{1,0:T(8,128)(2,1)S(1)}, u32[]{:S(2)}) copy-start(bf16[128,128]{1,0:T(8,128)(2,1)S(1)} %collective-permute-done.12.refs_0_) | copy-start | bytes 98308
  169.8 15.6 %copy-start.12 = (bf16[128,128]{1,0:T(8,128)(2,1)}, bf16[128,128]{1,0:T(8,128)(2,1)S(1)}, u32[]{:S(2)}) copy-start(bf16[128,128]{1,0:T(8,128)(2,1)S(1)} %collective-permute-done.13.refs_1_) | copy-start | bytes 98308
  190.1 9.3 %collective-permute-start.16 = (bf16[8,2,64,128]{3,2,1,0:T(8,128)(2,1)}, bf16[8,2,64,128]{3,2,1,0:T(8,128)(2,1)S(1)}, u32[]{:S(2)}, u32[]{:S(2)}) collective-permute-start(bf16[8,2,64,128]{3,2,1,0:T(8,128)(2,1)} %get-tuple-element.15.own_ref), channel_id=1, source_target_pairs={{0,8},{8,0},{1,9},{9,1},{2,10},{10,2},{3,11},{11,3},{4,12},{12,4},... | collective-permute-start | bytes 786440 | tf_op jit(solution)/shard_map/ppermute | solution.py:50
  202.1 15.3 %all-to-all-start.3 = ((bf16[8,2,64,128]{3,2,1,0:T(8,128)(2,1)}), bf16[8,2,64,128]{3,2,1,0:T(8,128)(2,1)S(1)}, u32[]{:S(2)}, u32[]{:S(2)}) async-start(bf16[8,2,64,128]{3,2,1,0:T(8,128)(2,1)} %shard_map.102), calls=%async_computation.3 | async-start | bytes 524288 | tf_op jit(solution)/shard_map/all_to_all | solution.py:40
  217.4 10.8 %collective-permute-start.17 = (bf16[8,64,128]{2,1,0:T(8,128)(2,1)S(1)}, bf16[8,64,128]{2,1,0:T(8,128)(2,1)S(1)}, u32[]{:S(2)}, u32[]{:S(2)}) collective-permute-start(bf16[8,64,128]{2,1,0:T(8,128)(2,1)S(1)} %dynamic-slice_bitcast_fusion.1), channel_id=1, source_target_pairs={{0,1},{1,0},{2,3},{3,2},{4,5},{5,4},{6,7},{7,6},{8,9},{9,8},{10,11... | collective-permute-start | bytes 393224 | tf_op jit(solution)/shard_map/ppermute | solution.py:50
  (13 other events, 44.0 us)

commit v7 on v6

--- a/solution.py
+++ b/solution.py
@@ -173,7 +173,8 @@
         met = swap(grads, "zl", by)
         grads = jnp.stack(ordered(grads, met, first), axis=at)
         by, at = by // 2, at + 1
-    grads = jnp.stack(ordered(grads, swap(grads, "yl"), yl_at == 0), axis=at)
+    met = swap(grads, "yl")
+    grads = jnp.stack(ordered(grads, met, yl_at == 0), axis=at)
     grads = grads.reshape(near, tokens, width_here)
     at_mine, at_other = (
         lax.dynamic_slice(grads, (0, at * half, 0), (near, half, width_here)).reshape(near * half, width_here)
@@ -189,12 +190,10 @@
             for f in range(far)
         ]
     ).astype(jnp.bfloat16)
-    gradient = at_index(partial, zh_at).astype(jnp.float32)
-    for k in far_order(far)[:-1]:
-        gradient += far_shift(at_index(partial, (zh_at + k) % far), k, 0, 0).astype(jnp.float32)
-
-    fresh = adam_fresh(master, moment1, moment2, gradient)
-    parts = {k: far_shift(fresh, k, 0, 1) for k in far_order(far)}
+    gradient = [at_index(partial, zh_at)] + [
+        far_shift(at_index(partial, (zh_at + k) % far), k, 0, 0)
+        for k in far_order(far)[:-1]
+    ]
 
     at = jnp.stack([lax.axis_index("role"), zh_at, yl_at])
     flops = 4 * far * near * half * block * width_here
@@ -203,7 +202,12 @@
         back_terms, (wide, wide), flops, at, at_mine, at_other, *(old_parts[k] for k in range(far))
     )
     back = (kept.astype(jnp.float32) + swap(sent, "core").astype(jnp.float32)).astype(jnp.bfloat16)
+    gradient, _ = lax.optimization_barrier((gradient, back))
     back = exchange(back, "x")
+
+
+    fresh = adam_fresh(master, moment1, moment2, sum(g.astype(jnp.float32) for g in gradient))
+    parts = {k: far_shift(fresh, k, 0, 1) for k in far_order(far)}
 
     shape = (line, 2, half, width_here)
     narrow = jax.ShapeDtypeStruct(shape, jnp.bfloat16)

time: 231 us -> 231 us (level)
  no operation moved by 1% of the time
where the time goes in v7:
time: 231 us; the launch traced here: 229 us
  starting transfers between devices  96.4 us (42%)
  waiting for transfers between devices  95.1 us (41%)
  matrix products  14.9 us (6%)
  local copies, waits for them, and re-layouts  8.44 us (4%)
  Pallas kernels  7.88 us (3%)
  other arithmetic  5.92 us (3%)
    ppermute x10, waiting for transfers between devices, far_shift(): return lax.ppermute(value, ('role', 'zh'), pairs)  64.1 us
    ppermute x8, starting transfers between devices, swap(): return lax.ppermute(value, axis, [(i, i ^ by) for i in range(peers)])  38.2 us
    ppermute x10, starting transfers between devices, far_shift(): return lax.ppermute(value, ('role', 'zh'), pairs)  31.7 us
    all_to_all x4, starting transfers between devices, exchange(): return lax.all_to_all(value, axis, 0, 0, tiled=True)  26.5 us
    ppermute x8, waiting for transfers between devices, swap(): return lax.ppermute(value, axis, [(i, i ^ by) for i in range(peers)])  24.4 us
    dot_general x8, matrix products, dot32(): lax.dot_general(a, b, (dims, ((), ())), preferred_element_type=jnp.float32)  9.12 us
    pallas_call x3, Pallas kernels, in_vmem(): pl.pallas_call(kernel, out_shape=outs, in_specs=[pl.BlockSpec(memory_spac...  7.88 us
    all_to_all x4, waiting for transfers between devices, exchange(): return lax.all_to_all(value, axis, 0, 0, tiled=True)  6.56 us
  transfers between devices with their start and end apart: 22, of which 9 were waited for; matrix products, arithmetic and copies ran while one was open for 10% of the time, Pallas kernels for 1%

profile of v7, /device:TPU:29, one launch (start us, length us, event | category | flops | bytes accessed | tf_op | source)
XLA Modules:
  0.0 229.4 jit_solution(4935492443708932386)
XLA Ops:
  0.0 1.6 copy-done
  2.4 13.4 %all-to-all-start = ((bf16[16,64,128]{2,1,0:T(8,128)(2,1)}), bf16[16,64,128]{2,1,0:T(8,128)(2,1)S(1)}, u32[]{:S(2)}, u32[]{:S(2)}) async-start(bf16[16,64,128]{2,1,0:T(8,128)(2,1)} %copy.37), calls=%async_computation | async-start | bytes 524288 | tf_op jit(solution)/shard_map/all_to_all | solution.py:40
  15.9 7.0 %collective-permute-start.1 = (bf16[128,128]{1,0:T(8,128)(2,1)S(1)}, bf16[128,128]{1,0:T(8,128)(2,1)S(1)}, u32[]{:S(2)}, u32[]{:S(2)}) collective-permute-start(bf16[128,128]{1,0:T(8,128)(2,1)S(1)} %copy-done.17), channel_id=1, source_target_pairs={{0,64},{16,80},{32,96},{48,112},{64,0},{80,16},{96,32},{112,48},{1... | collective-permute-start | bytes 98312 | tf_op jit(solution)/shard_map/ppermute | solution.py:50
  22.9 10.7 %collective-permute-done.1 = bf16[128,128]{1,0:T(8,128)(2,1)S(1)} collective-permute-done((bf16[128,128]{1,0:T(8,128)(2,1)S(1)}, bf16[128,128]{1,0:T(8,128)(2,1)S(1)}, u32[]{:S(2)}, u32[]{:S(2)}) %collective-permute-start.1) | collective-permute-done | bytes 32800 | tf_op jit(solution)/shard_map/ppermute | solution.py:50
  33.6 1.9 collective-permute-start.2
  35.6 4.0 %collective-permute-done.2 = bf16[2,128,128]{2,1,0:T(8,128)(2,1)S(1)} collective-permute-done((bf16[2,128,128]{2,1,0:T(8,128)(2,1)S(1)}, bf16[2,128,128]{2,1,0:T(8,128)(2,1)S(1)}, u32[]{:S(2)}, u32[]{:S(2)}) %collective-permute-start.2) | collective-permute-done | bytes 65568 | tf_op jit(solution)/shard_map/ppermute | solution.py:50
  39.6 3.5 %collective-permute-start.3 = (bf16[2,2,128,128]{3,2,1,0:T(8,128)(2,1)S(1)}, bf16[2,2,128,128]{3,2,1,0:T(8,128)(2,1)S(1)}, u32[]{:S(2)}, u32[]{:S(2)}) collective-permute-start(bf16[2,2,128,128]{3,2,1,0:T(8,128)(2,1)S(1)} %pad_maximum_fusion.2), channel_id=1, source_target_pairs={{0,16},{16,0},{32,48},{48,32},{64,80},{80,64},{96,112},{112,96},{1... | collective-permute-start | bytes 393224 | tf_op jit(solution)/shard_map/ppermute | solution.py:50
  43.1 2.3 %collective-permute-done.3 = bf16[2,2,128,128]{3,2,1,0:T(8,128)(2,1)S(1)} collective-permute-done((bf16[2,2,128,128]{3,2,1,0:T(8,128)(2,1)S(1)}, bf16[2,2,128,128]{3,2,1,0:T(8,128)(2,1)S(1)}, u32[]{:S(2)}, u32[]{:S(2)}) %collective-permute-start.3) | collective-permute-done | bytes 131104 | tf_op jit(solution)/shard_map/ppermute | solution.py:50
  46.2 1.9 collective-permute-start.4
  49.4 4.2 %all-to-all-start.1 = ((bf16[4,1024,128]{2,1,0:T(8,128)(2,1)}), bf16[4,1024,128]{2,1,0:T(8,128)(2,1)S(1)}, u32[]{:S(2)}, u32[]{:S(2)}) async-start(bf16[4,1024,128]{2,1,0:T(8,128)(2,1)} %broadcast_in_dim.29), calls=%async_computation.1 | async-start | bytes 2097152 | tf_op jit(solution)/shard_map/all_to_all | solution.py:40
  55.2 16.1 %collective-permute-start.5 = (bf16[128,128]{1,0:T(8,128)(2,1)S(1)}, bf16[128,128]{1,0:T(8,128)(2,1)S(1)}, u32[]{:S(2)}, u32[]{:S(2)}) collective-permute-start(bf16[128,128]{1,0:T(8,128)(2,1)S(1)} %convert_element_type.52.refs_0_), channel_id=1, source_target_pairs={{512,128},{640,256},{768,384},{896,0},{513,129},{641,257},{769,385... | collective-permute-start | bytes 98312 | tf_op jit(solution)/shard_map/ppermute | solution.py:60
  71.3 7.0 %collective-permute-start.6 = (bf16[128,128]{1,0:T(8,128)(2,1)S(1)}, bf16[128,128]{1,0:T(8,128)(2,1)S(1)}, u32[]{:S(2)}, u32[]{:S(2)}) collective-permute-start(bf16[128,128]{1,0:T(8,128)(2,1)S(1)} %convert_element_type.52.refs_0_), channel_id=1, source_target_pairs={{512,256},{640,384},{768,0},{896,128},{513,257},{641,385},{769,1},... | collective-permute-start | bytes 98312 | tf_op jit(solution)/shard_map/ppermute | solution.py:60
  82.1 2.4 %shard_map.100 = (bf16[4,1024,128]{2,1,0:T(8,128)(2,1)}, bf16[4,1024,128]{2,1,0:T(8,128)(2,1)}) custom-call(s32[3]{0:T(128)} %pad_add_fusion.at_ref, bf16[1024,128]{1,0:T(8,128)(2,1)} %bitcast.164, bf16[1024,128]{1,0:T(8,128)(2,1)} %bitcast.159, bf16[128,128]{1,0:T(8,128)(2,1)} %copy-done.16, bf16[128,128]{1,0:T(8,128)(2,1)} %copy-done.20, ...), custom_call_target="tpu_custom_call" | custom-call | flops 268435456 | bytes 2752512 | tf_op jit(solution)/shard_map/pallas_call | solution.py:137
  84.5 10.8 %collective-permute-start.8 = (bf16[4,1024,128]{2,1,0:T(8,128)(2,1)}, bf16[4,1024,128]{2,1,0:T(8,128)(2,1)}, u32[]{:S(2)}, u32[]{:S(2)}) collective-permute-start(bf16[4,1024,128]{2,1,0:T(8,128)(2,1)} %get-tuple-element.18), channel_id=1, source_target_pairs={{0,1},{1,0},{2,3},{3,2},{4,5},{5,4},{6,7},{7,6},{8,9},{9,8},{10,11... | collective-permute-start | bytes 3145736 | tf_op jit(solution)/shard_map/ppermute | solution.py:50
  95.4 2.1 collective-permute-start
  97.4 1.8 fusion.24
  99.3 1.8 fusion.23
  101.7 2.5 %add_convert_fusion = bf16[4,1024,128]{2,1,0:T(8,128)(2,1)} fusion(bf16[4,1024,128]{2,1,0:T(8,128)(2,1)} %collective-permute-done.8, bf16[4,1024,128]{2,1,0:T(8,128)(2,1)S(1)} %copy-done.4), kind=kLoop, calls=%fused_computation | loop fusion | flops 2097152 | bytes 3145728 | tf_op jit(solution)/shard_map/convert_element_type | solution.py:204
  104.2 5.4 %all-to-all-start.2 = ((bf16[4,1024,128]{2,1,0:T(8,128)(2,1)}), bf16[4,1024,128]{2,1,0:T(8,128)(2,1)}, u32[]{:S(2)}, u32[]{:S(2)}) async-start(bf16[4,1024,128]{2,1,0:T(8,128)(2,1)} %add_convert_fusion), calls=%async_computation.2 | async-start | bytes 2097152 | tf_op jit(solution)/shard_map/all_to_all | solution.py:40
  116.8 1.4 collective-permute-start.12
  122.2 38.9 %collective-permute-done.12.refs_0_ = bf16[128,128]{1,0:T(8,128)(2,1)S(1)} collective-permute-done((bf16[128,128]{1,0:T(8,128)(2,1)S(1)}, bf16[128,128]{1,0:T(8,128)(2,1)S(1)}, u32[]{:S(2)}, u32[]{:S(2)}) %collective-permute-start.12) | collective-permute-done | bytes 32800 | tf_op jit(solution)/shard_map/ppermute | solution.py:60
  161.0 8.7 %collective-permute-done.13.refs_1_ = bf16[128,128]{1,0:T(8,128)(2,1)S(1)} collective-permute-done((bf16[128,128]{1,0:T(8,128)(2,1)S(1)}, bf16[128,128]{1,0:T(8,128)(2,1)S(1)}, u32[]{:S(2)}, u32[]{:S(2)}) %collective-permute-start.13) | collective-permute-done | bytes 32800 | tf_op jit(solution)/shard_map/ppermute | solution.py:60
  169.8 15.6 %collective-permute-done.14.refs_2_ = bf16[128,128]{1,0:T(8,128)(2,1)S(1)} collective-permute-done((bf16[128,128]{1,0:T(8,128)(2,1)S(1)}, bf16[128,128]{1,0:T(8,128)(2,1)S(1)}, u32[]{:S(2)}, u32[]{:S(2)}) %collective-permute-start.14) | collective-permute-done | bytes 32800 | tf_op jit(solution)/shard_map/ppermute | solution.py:60
  186.6 3.5 %shard_map.101 = (f32[8,2,64,128]{3,2,1,0:T(8,128)}, bf16[8,2,64,128]{3,2,1,0:T(8,128)(2,1)}) custom-call(s32[3]{0:T(128)} %pad_add_fusion.at_ref, bf16[4,1024,128]{2,1,0:T(8,128)(2,1)} %copy-done.1, bf16[4,1024,128]{2,1,0:T(8,128)(2,1)} %collective-permute-done.other_ref, bf16[4,1024,128]{2,1,0:T(8,128)(2,1)} %all-to-all-done.2.back_ref, ...), custom_call_target="tpu_custom_call" | custom-call | flops 268435456 | bytes 4063232 | tf_op jit(solution)/shard_map/pallas_call | solution.py:137
  190.1 1.9 collective-permute-start.16
  192.0 7.3 %collective-permute-done.16.met_ref = bf16[8,2,64,128]{3,2,1,0:T(8,128)(2,1)S(1)} collective-permute-done((bf16[8,2,64,128]{3,2,1,0:T(8,128)(2,1)}, bf16[8,2,64,128]{3,2,1,0:T(8,128)(2,1)S(1)}, u32[]{:S(2)}, u32[]{:S(2)}) %collective-permute-start.16) | collective-permute-done | bytes 262176 | tf_op jit(solution)/shard_map/ppermute | solution.py:50
  200.1 2.0 shard_map.102
  202.1 3.4 %all-to-all-start.3 = ((bf16[8,2,64,128]{3,2,1,0:T(8,128)(2,1)}), bf16[8,2,64,128]{3,2,1,0:T(8,128)(2,1)S(1)}, u32[]{:S(2)}, u32[]{:S(2)}) async-start(bf16[8,2,64,128]{3,2,1,0:T(8,128)(2,1)} %shard_map.102), calls=%async_computation.3 | async-start | bytes 524288 | tf_op jit(solution)/shard_map/all_to_all | solution.py:40
  207.0 1.9 fusion.41
  210.8 6.6 %all-to-all-done.3 = bf16[8,2,64,128]{3,2,1,0:T(8,128)(2,1)S(1)} async-done(((bf16[8,2,64,128]{3,2,1,0:T(8,128)(2,1)}), bf16[8,2,64,128]{3,2,1,0:T(8,128)(2,1)S(1)}, u32[]{:S(2)}, u32[]{:S(2)}) %all-to-all-start.3) | async-done | bytes 262176 | tf_op jit(solution)/shard_map/all_to_all | solution.py:40
  217.4 9.0 %collective-permute-start.17 = (bf16[8,64,128]{2,1,0:T(8,128)(2,1)S(1)}, bf16[8,64,128]{2,1,0:T(8,128)(2,1)S(1)}, u32[]{:S(2)}, u32[]{:S(2)}) collective-permute-start(bf16[8,64,128]{2,1,0:T(8,128)(2,1)S(1)} %dynamic-slice_bitcast_fusion.1), channel_id=1, source_target_pairs={{0,1},{1,0},{2,3},{3,2},{4,5},{5,4},{6,7},{7,6},{8,9},{9,8},{10,11... | collective-permute-start | bytes 393224 | tf_op jit(solution)/shard_map/ppermute | solution.py:50
  226.5 1.4 fusion.6
  (111 shorter events, 26.3 us)
Async XLA Ops:
  0.0 15.9 %copy-start.17 = (bf16[128,128]{1,0:T(8,128)(2,1)S(1)}, bf16[128,128]{1,0:T(8,128)(2,1)}, u32[]{:S(2)}) copy-start(bf16[128,128]{1,0:T(8,128)(2,1)} %param.11) | copy-start | bytes 98308
  0.0 48.2 %copy-start.7 = (f32[128,128]{1,0:T(8,128)S(1)}, f32[128,128]{1,0:T(8,128)}, u32[]{:S(2)}) copy-start(f32[128,128]{1,0:T(8,128)} %param.12) | copy-start | bytes 196612
  2.4 45.8 %all-to-all-start = ((bf16[16,64,128]{2,1,0:T(8,128)(2,1)}), bf16[16,64,128]{2,1,0:T(8,128)(2,1)S(1)}, u32[]{:S(2)}, u32[]{:S(2)}) async-start(bf16[16,64,128]{2,1,0:T(8,128)(2,1)} %copy.37), calls=%async_computation | async-start | bytes 524288 | tf_op jit(solution)/shard_map/all_to_all | solution.py:40
  15.9 17.7 %collective-permute-start.1 = (bf16[128,128]{1,0:T(8,128)(2,1)S(1)}, bf16[128,128]{1,0:T(8,128)(2,1)S(1)}, u32[]{:S(2)}, u32[]{:S(2)}) collective-permute-start(bf16[128,128]{1,0:T(8,128)(2,1)S(1)} %copy-done.17), channel_id=1, source_target_pairs={{0,64},{16,80},{32,96},{48,112},{64,0},{80,16},{96,32},{112,48},{1... | collective-permute-start | bytes 98312 | tf_op jit(solution)/shard_map/ppermute | solution.py:50
  33.6 5.9 %collective-permute-start.2 = (bf16[2,128,128]{2,1,0:T(8,128)(2,1)S(1)}, bf16[2,128,128]{2,1,0:T(8,128)(2,1)S(1)}, u32[]{:S(2)}, u32[]{:S(2)}) collective-permute-start(bf16[2,128,128]{2,1,0:T(8,128)(2,1)S(1)} %pad_maximum_fusion.4), channel_id=1, source_target_pairs={{0,32},{16,48},{32,0},{48,16},{64,96},{80,112},{96,64},{112,80},{1... | collective-permute-start | bytes 196616 | tf_op jit(solution)/shard_map/ppermute | solution.py:50
  39.6 5.9 %collective-permute-start.3 = (bf16[2,2,128,128]{3,2,1,0:T(8,128)(2,1)S(1)}, bf16[2,2,128,128]{3,2,1,0:T(8,128)(2,1)S(1)}, u32[]{:S(2)}, u32[]{:S(2)}) collective-permute-start(bf16[2,2,128,128]{3,2,1,0:T(8,128)(2,1)S(1)} %pad_maximum_fusion.2), channel_id=1, source_target_pairs={{0,16},{16,0},{32,48},{48,32},{64,80},{80,64},{96,112},{112,96},{1... | collective-permute-start | bytes 393224 | tf_op jit(solution)/shard_map/ppermute | solution.py:50
  46.2 7.9 %collective-permute-start.4 = (bf16[2,2,2,128,128]{4,3,2,1,0:T(8,128)(2,1)}, bf16[2,2,2,128,128]{4,3,2,1,0:T(8,128)(2,1)}, u32[]{:S(2)}, u32[]{:S(2)}) collective-permute-start(bf16[2,2,2,128,128]{4,3,2,1,0:T(8,128)(2,1)} %pad_maximum_fusion.1), channel_id=1, source_target_pairs={{0,8},{8,0},{1,9},{9,1},{2,10},{10,2},{3,11},{11,3},{4,12},{12,4},... | collective-permute-start | bytes 786440 | tf_op jit(solution)/shard_map/ppermute | solution.py:50
  48.2 30.2 %copy-start.16 = (bf16[128,128]{1,0:T(8,128)(2,1)}, bf16[128,128]{1,0:T(8,128)(2,1)S(1)}, u32[]{:S(2)}) copy-start(bf16[128,128]{1,0:T(8,128)(2,1)S(1)} %convert_element_type.52.refs_0_) | copy-start | bytes 98308
  49.4 46.0 %all-to-all-start.1 = ((bf16[4,1024,128]{2,1,0:T(8,128)(2,1)}), bf16[4,1024,128]{2,1,0:T(8,128)(2,1)S(1)}, u32[]{:S(2)}, u32[]{:S(2)}) async-start(bf16[4,1024,128]{2,1,0:T(8,128)(2,1)} %broadcast_in_dim.29), calls=%async_computation.1 | async-start | bytes 2097152 | tf_op jit(solution)/shard_map/all_to_all | solution.py:40
  55.2 25.3 %collective-permute-start.5 = (bf16[128,128]{1,0:T(8,128)(2,1)S(1)}, bf16[128,128]{1,0:T(8,128)(2,1)S(1)}, u32[]{:S(2)}, u32[]{:S(2)}) collective-permute-start(bf16[128,128]{1,0:T(8,128)(2,1)S(1)} %convert_element_type.52.refs_0_), channel_id=1, source_target_pairs={{512,128},{640,256},{768,384},{896,0},{513,129},{641,257},{769,385... | collective-permute-start | bytes 98312 | tf_op jit(solution)/shard_map/ppermute | solution.py:60
  71.3 9.2 %collective-permute-start.6 = (bf16[128,128]{1,0:T(8,128)(2,1)S(1)}, bf16[128,128]{1,0:T(8,128)(2,1)S(1)}, u32[]{:S(2)}, u32[]{:S(2)}) collective-permute-start(bf16[128,128]{1,0:T(8,128)(2,1)S(1)} %convert_element_type.52.refs_0_), channel_id=1, source_target_pairs={{512,256},{640,384},{768,0},{896,128},{513,257},{641,385},{769,1},... | collective-permute-start | bytes 98312 | tf_op jit(solution)/shard_map/ppermute | solution.py:60
  78.4 3.1 %collective-permute-start.7 = (bf16[128,128]{1,0:T(8,128)(2,1)S(1)}, bf16[128,128]{1,0:T(8,128)(2,1)S(1)}, u32[]{:S(2)}, u32[]{:S(2)}) collective-permute-start(bf16[128,128]{1,0:T(8,128)(2,1)S(1)} %convert_element_type.52.refs_0_), channel_id=1, source_target_pairs={{512,384},{640,0},{768,128},{896,256},{513,385},{641,1},{769,129},... | collective-permute-start | bytes 98312 | tf_op jit(solution)/shard_map/ppermute | solution.py:60
  80.5 20.6 %copy-start.3 = (bf16[16,64,128]{2,1,0:T(8,128)(2,1)S(1)}, bf16[16,64,128]{2,1,0:T(8,128)(2,1)}, u32[]{:S(2)}) copy-start(bf16[16,64,128]{2,1,0:T(8,128)(2,1)} %get-tuple-element.26) | copy-start | bytes 786436
  84.5 17.2 %collective-permute-start.8 = (bf16[4,1024,128]{2,1,0:T(8,128)(2,1)}, bf16[4,1024,128]{2,1,0:T(8,128)(2,1)}, u32[]{:S(2)}, u32[]{:S(2)}) collective-permute-start(bf16[4,1024,128]{2,1,0:T(8,128)(2,1)} %get-tuple-element.18), channel_id=1, source_target_pairs={{0,1},{1,0},{2,3},{3,2},{4,5},{5,4},{6,7},{7,6},{8,9},{9,8},{10,11... | collective-permute-start | bytes 3145736 | tf_op jit(solution)/shard_map/ppermute | solution.py:50
  95.3 8.9 %copy-start.1 = (bf16[4,1024,128]{2,1,0:T(8,128)(2,1)}, bf16[4,1024,128]{2,1,0:T(8,128)(2,1)S(1)}, u32[]{:S(2)}) copy-start(bf16[4,1024,128]{2,1,0:T(8,128)(2,1)S(1)} %all-to-all-done.1.mine_ref) | copy-start | bytes 3145732
  95.4 14.3 %collective-permute-start = (bf16[4,1024,128]{2,1,0:T(8,128)(2,1)S(1)}, bf16[4,1024,128]{2,1,0:T(8,128)(2,1)}, u32[]{:S(2)}, u32[]{:S(2)}) collective-permute-start(bf16[4,1024,128]{2,1,0:T(8,128)(2,1)S(1)} %all-to-all-done.1.mine_ref), channel_id=1, source_target_pairs={{0,1},{1,0},{2,3},{3,2},{4,5},{5,4},{6,7},{7,6},{8,9},{9,8},{10,11... | collective-permute-start | bytes 3145736 | tf_op jit(solution)/shard_map/ppermute | solution.py:50
  104.2 17.9 %all-to-all-start.2 = ((bf16[4,1024,128]{2,1,0:T(8,128)(2,1)}), bf16[4,1024,128]{2,1,0:T(8,128)(2,1)}, u32[]{:S(2)}, u32[]{:S(2)}) async-start(bf16[4,1024,128]{2,1,0:T(8,128)(2,1)} %add_convert_fusion), calls=%async_computation.2 | async-start | bytes 2097152 | tf_op jit(solution)/shard_map/all_to_all | solution.py:40
  114.6 2.0 collective-permute-start.10
  115.3 1.4 collective-permute-start.11
  116.0 0.7 collective-permute-start.9
  116.8 88.7 %copy-start.6 = (bf16[8,16,1024]{2,1,0:T(8,128)(2,1)S(1)}, bf16[8,16,1024]{2,1,0:T(8,128)(2,1)}, u32[]{:S(2)}) copy-start(bf16[8,16,1024]{2,1,0:T(8,128)(2,1)} %param.15) | copy-start | bytes 786436
  116.8 88.8 %copy-start.18 = (s32[16]{0:T(128)S(1)}, s32[16]{0:T(128)}, u32[]{:S(2)}) copy-start(s32[16]{0:T(128)} %param.19) | copy-start | bytes 196
  116.8 88.9 %copy-start.15 = (bf16[8,16,128]{2,1,0:T(8,128)(2,1)S(1)}, bf16[8,16,128]{2,1,0:T(8,128)(2,1)}, u32[]{:S(2)}) copy-start(bf16[8,16,128]{2,1,0:T(8,128)(2,1)} %param.16) | copy-start | bytes 98308
  116.8 44.2 %collective-permute-start.12 = (bf16[128,128]{1,0:T(8,128)(2,1)S(1)}, bf16[128,128]{1,0:T(8,128)(2,1)S(1)}, u32[]{:S(2)}, u32[]{:S(2)}) collective-permute-start(bf16[128,128]{1,0:T(8,128)(2,1)S(1)} %fusion.36), channel_id=1, source_target_pairs={{0,512},{128,640},{256,768},{384,896},{1,513},{129,641},{257,769},... | collective-permute-start | bytes 98312 | tf_op jit(solution)/shard_map/ppermute | solution.py:60
  118.3 51.5 %collective-permute-start.13 = (bf16[128,128]{1,0:T(8,128)(2,1)S(1)}, bf16[128,128]{1,0:T(8,128)(2,1)S(1)}, u32[]{:S(2)}, u32[]{:S(2)}) collective-permute-start(bf16[128,128]{1,0:T(8,128)(2,1)S(1)} %fusion.36), channel_id=1, source_target_pairs={{0,640},{128,768},{256,896},{384,512},{1,641},{129,769},{257,897},... | collective-permute-start | bytes 98312 | tf_op jit(solution)/shard_map/ppermute | solution.py:60
  119.6 65.8 %collective-permute-start.14 = (bf16[128,128]{1,0:T(8,128)(2,1)S(1)}, bf16[128,128]{1,0:T(8,128)(2,1)S(1)}, u32[]{:S(2)}, u32[]{:S(2)}) collective-permute-start(bf16[128,128]{1,0:T(8,128)(2,1)S(1)} %fusion.36), channel_id=1, source_target_pairs={{0,768},{128,896},{256,512},{384,640},{1,769},{129,897},{257,513},... | collective-permute-start | bytes 98312 | tf_op jit(solution)/shard_map/ppermute | solution.py:60
  120.9 64.5 %collective-permute-start.15 = (bf16[128,128]{1,0:T(8,128)(2,1)S(1)}, bf16[128,128]{1,0:T(8,128)(2,1)S(1)}, u32[]{:S(2)}, u32[]{:S(2)}) collective-permute-start(bf16[128,128]{1,0:T(8,128)(2,1)S(1)} %fusion.36), channel_id=1, source_target_pairs={{0,896},{128,512},{256,640},{384,768},{1,897},{129,513},{257,641},... | collective-permute-start | bytes 98312 | tf_op jit(solution)/shard_map/ppermute | solution.py:60
  161.0 24.4 %copy-start.11 = (bf16[128,128]{1,0:T(8,128)(2,1)}, bf16[128,128]{1,0:T(8,128)(2,1)S(1)}, u32[]{:S(2)}) copy-start(bf16[128,128]{1,0:T(8,128)(2,1)S(1)} %collective-permute-done.12.refs_0_) | copy-start | bytes 98308
  169.8 15.6 %copy-start.12 = (bf16[128,128]{1,0:T(8,128)(2,1)}, bf16[128,128]{1,0:T(8,128)(2,1)S(1)}, u32[]{:S(2)}) copy-start(bf16[128,128]{1,0:T(8,128)(2,1)S(1)} %collective-permute-done.13.refs_1_) | copy-start | bytes 98308
  190.1 9.3 %collective-permute-start.16 = (bf16[8,2,64,128]{3,2,1,0:T(8,128)(2,1)}, bf16[8,2,64,128]{3,2,1,0:T(8,128)(2,1)S(1)}, u32[]{:S(2)}, u32[]{:S(2)}) collective-permute-start(bf16[8,2,64,128]{3,2,1,0:T(8,128)(2,1)} %get-tuple-element.23.own_ref), channel_id=1, source_target_pairs={{0,8},{8,0},{1,9},{9,1},{2,10},{10,2},{3,11},{11,3},{4,12},{12,4},... | collective-permute-start | bytes 786440 | tf_op jit(solution)/shard_map/ppermute | solution.py:50
  202.1 15.3 %all-to-all-start.3 = ((bf16[8,2,64,128]{3,2,1,0:T(8,128)(2,1)}), bf16[8,2,64,128]{3,2,1,0:T(8,128)(2,1)S(1)}, u32[]{:S(2)}, u32[]{:S(2)}) async-start(bf16[8,2,64,128]{3,2,1,0:T(8,128)(2,1)} %shard_map.102), calls=%async_computation.3 | async-start | bytes 524288 | tf_op jit(solution)/shard_map/all_to_all | solution.py:40
  217.4 10.8 %collective-permute-start.17 = (bf16[8,64,128]{2,1,0:T(8,128)(2,1)S(1)}, bf16[8,64,128]{2,1,0:T(8,128)(2,1)S(1)}, u32[]{:S(2)}, u32[]{:S(2)}) collective-permute-start(bf16[8,64,128]{2,1,0:T(8,128)(2,1)S(1)} %dynamic-slice_bitcast_fusion.1), channel_id=1, source_target_pairs={{0,1},{1,0},{2,3},{3,2},{4,5},{5,4},{6,7},{7,6},{8,9},{9,8},{10,11... | collective-permute-start | bytes 393224 | tf_op jit(solution)/shard_map/ppermute | solution.py:50
  (13 other events, 44.0 us)
